TPU v7x, 128 devices: a whole 4x4x4 slice. The times are simulated.
128 devices in a mesh: seq: 32 (over y, x, core), head: 4 (over z).
Axes of the slice: x: 4, y: 4, z: 4, core: 2. Of those that a mesh axis runs over, the one named last changes fastest.
Arguments:
- queries: float32 [32768, 8192], P('seq', 'head'), may hold values from -200 to 200, as said below
- keys: float32 [32768, 1024], P('seq', 'head'), may hold values from -8 to 8, as said below
- values: float32 [32768, 1024], P('seq', 'head'), may hold values from -40 to 40, as said below
- gain: float32 [8192], P('head'), may hold values from 0.1 to 1.9
Outputs:
- attended: float32 [32768, 8192], P('seq', 'head')
Inputs may be any that keep to these rules, and one draw needn't show every extreme that they name: `queries`: queries are real-valued. `keys`: keys are real-valued of order one. `values`: values are real-valued; their scale differs between heads.
All inputs are finite; a program needn't handle non-finite values.
Results may differ from a plain program's by a relative error of at most 0.0003.
Values sent between devices are 32-bit elements; how exact they have to be, the bound alone decides.
No kernel may reach another device: no remote copies, remote signals or barrier semaphores. Data moves between devices by JAX's collectives and lax.ppermute only.
A program may use at most 128 MiB of HBM per device.

v0:
```python
import math

import jax
import jax.numpy as jnp
from jax import lax
from jax.sharding import PartitionSpec as P

QUERY_HEADS = 64
KEY_VALUE_HEADS = 8
HEAD_DIMENSION = 128
WINDOW = 128


HIGH_ACCURACY = lax.Precision.HIGHEST


def from_behind(shard, axis, by):
    peers = lax.axis_size(axis)
    pairs = [(i, i + by) for i in range(peers) if 0 <= i + by < peers]
    return lax.ppermute(shard, axis, pairs)


def shards(queries, keys, values, gain):
    count = queries.shape[0]
    kv_local = keys.shape[1] // HEAD_DIMENSION
    group_count = QUERY_HEADS // KEY_VALUE_HEADS
    window_border = WINDOW - 1
    block_index = math.gcd(count, 128)
    nblocks = count // block_index
    query_features = jnp.tanh(queries).reshape(count, kv_local, group_count, HEAD_DIMENSION)
    raw_q = queries.reshape(count, kv_local, group_count, HEAD_DIMENSION)
    key_rows = keys.reshape(count, kv_local, HEAD_DIMENSION)
    value_rows = values.reshape(count, kv_local, HEAD_DIMENSION)
    key_features = jnp.tanh(key_rows)
    own_state = jnp.einsum("sgd,sge->gde", key_features, value_rows, precision=HIGH_ACCURACY)
    shard = lax.axis_index("seq")
    piece = lax.all_gather(own_state[None], "seq", axis=0, tiled=True)
    place = jnp.arange(piece.shape[0], dtype=jnp.int32)
    keep = place < shard
    prior = jnp.sum(jnp.where(keep[:, None, None, None], piece, 0.0), axis=0)
    prev_k, prev_v = from_behind(
        (keys[count - window_border :], values[count - window_border :]), "seq", 1
    )
    every_key_row = jnp.concatenate(
        [prev_k.reshape(window_border, kv_local, HEAD_DIMENSION), key_rows], 0
    )
    every_value_row = jnp.concatenate(
        [prev_v.reshape(window_border, kv_local, HEAD_DIMENSION), value_rows], 0
    )
    base_offset = shard * count
    rows = jnp.arange(block_index, dtype=jnp.int32)
    cols = jnp.arange(window_border + block_index, dtype=jnp.int32)
    causal = rows[:, None] >= rows[None, :]
    score_scale = 1.0 / math.sqrt(HEAD_DIMENSION)

    def advance(state, number):
        first = number * block_index
        query_feature_block = lax.dynamic_slice_in_dim(query_features, first, block_index, 0)
        query_block = lax.dynamic_slice_in_dim(raw_q, first, block_index, 0)
        key_feature_block = lax.dynamic_slice_in_dim(key_features, first, block_index, 0)
        value_block = lax.dynamic_slice_in_dim(value_rows, first, block_index, 0)
        inner_product = jnp.einsum(
            "cmop,nmp->mocn", query_feature_block, key_feature_block, precision=HIGH_ACCURACY
        )
        inner_product = jnp.where(causal[None, None], inner_product, 0.0)
        linear_branch = jnp.einsum(
            "xjpa,axf->pxjf", inner_product, value_block, precision=HIGH_ACCURACY
        )
        linear_branch = linear_branch + jnp.einsum(
            "tgrd,gde->tgre", query_feature_block, state, precision=HIGH_ACCURACY
        )
        state = state + jnp.einsum(
            "sgd,sge->gde", key_feature_block, value_block, precision=HIGH_ACCURACY
        )
        key_block = lax.dynamic_slice_in_dim(every_key_row, first, block_index + window_border, 0)
        key_value_block = lax.dynamic_slice_in_dim(
            every_value_row, first, block_index + window_border, 0
        )
        q_pos = base_offset + first + rows
        k_pos = base_offset + first - window_border + cols
        valid = (
            (k_pos[None, :] <= q_pos[:, None])
            & (k_pos[None, :] > q_pos[:, None] - WINDOW)
            & (k_pos[None, :] >= 0)
        )
        score_matrix = (
            jnp.einsum("cmop,nmp->mocn", query_block, key_block, precision=HIGH_ACCURACY)
            * score_scale
        )
        score_matrix = jnp.where(valid[None, None], score_matrix, -jnp.inf)
        top = jnp.max(score_matrix, axis=3, keepdims=True)
        softmax_weights = jnp.where(valid[None, None], jnp.exp(score_matrix - top), 0.0)
        total = jnp.sum(softmax_weights, axis=3)
        window_length = jnp.einsum(
            "xjpa,axf->pxjf", softmax_weights, key_value_block, precision=HIGH_ACCURACY
        )
        window_length = window_length / jnp.transpose(total, (2, 0, 1))[..., None]
        return (state, (linear_branch, window_length))

    numbers = jnp.arange(nblocks, dtype=jnp.int32)
    _, (linear_branch, window_length) = lax.scan(advance, prior, numbers)
    linear_branch = linear_branch.reshape(count, queries.shape[1])
    window_length = window_length.reshape(count, queries.shape[1])
    squares = jnp.sum(linear_branch * linear_branch, axis=1)
    squares = lax.psum(squares, "head")
    normed = (
        linear_branch
        / jnp.sqrt(squares / (QUERY_HEADS * HEAD_DIMENSION) + 1e-06)[:, None]
        * gain[None, :]
    )
    return normed + window_length


def solution(mesh):
    in_specs = (P("seq", "head"), P("seq", "head"), P("seq", "head"), P("head"))
    out_specs = P("seq", "head")
    return jax.shard_map(shards, mesh=mesh, in_specs=in_specs, out_specs=out_specs, check_vma=False)
```

profile of v0, /device:TPU:0, one launch (start us, length us, event | category | flops | bytes accessed | tf_op | source)
XLA Modules:
  0.0 273.3 jit_solution(10381405209762765146)
XLA Ops:
  8.1 2.5 copy.36
  10.6 3.0 %fusion.45 = f32[2,128,128]{2,1,0:T(8,128)} fusion(f32[1024,2,128]{0,2,1:T(8,128)} %bitcast.1, f32[1024,2,128]{0,2,1:T(8,128)S(1)} %bitcast.122), kind=kOutput, calls=%fused_computation.62 | convolution fusion | flops 402653184 | bytes 2228224 | tf_op jit(solution)/shard_map/sgd,sge->gde/dot_general | solution.py:35
  16.8 4.2 %collective-permute-start.1 = (f32[127,256]{1,0:T(8,128)S(1)}, f32[127,256]{1,0:T(8,128)S(1)}, u32[]{:S(2)}, u32[]{:S(2)}) collective-permute-start(f32[127,256]{1,0:T(8,128)S(1)} %slice.7), channel_id=1, source_target_pairs={{0,4},{4,8},{8,12},{12,16},{16,20},{20,24},{24,28},{28,32},{32,36}... | collective-permute-start | bytes 390152 | tf_op jit(solution)/shard_map/ppermute | solution.py:20
  22.2 9.3 %copy.38 = f32[1024,2048]{0,1:T(8,128)} copy(f32[1024,2048]{1,0:T(8,128)} %param.6) | data formatting | bytes 16777216 | tf_op args[0]
  31.5 8.6 %tanh.7 = f32[1024,2048]{0,1:T(8,128)} tanh(f32[1024,2048]{0,1:T(8,128)} %copy.38) | non-fusion elementwise | bytes 16777216 | tf_op jit(solution)/shard_map/tanh | solution.py:30
  40.3 3.3 %pad_maximum_fusion = (f32[1151,2,128]{0,2,1:T(8,128)}, f32[1151,2,128]{0,2,1:T(8,128)}) fusion(f32[1024,2,128]{0,2,1:T(8,128)} %bitcast.1, f32[127,2,128]{0,2,1:T(8,128)S(1)} %bitcast.126, f32[1024,2,128]{0,2,1:T(8,128)S(1)} %bitcast.124, f32[127,2,128]{0,2,1:T(8,128)S(1)} %bitcast.127), kind=kLoop, calls=%fused_computation.58 | loop fusion | flops 589312 | bytes 4714496 | tf_op jit(solution)/shard_map/concatenate | solution.py:47
  43.6 18.6 %all-gather.3.cloned.1.call-done = f32[64,128,128]{2,1,0:T(8,128)} async-done(((f32[2,128,128]{2,1,0:T(8,128)}), f32[64,128,128]{2,1,0:T(8,128)}) %all-gather.3.cloned.1.call-update) | async-done | bytes 4194320 | tf_op jit(solution)/shard_map/all_gather | solution.py:37
  62.2 2.6 select_reduce_fusion
  64.9 149.5 %while.17 = (s32[]{:T(128)}, f32[2,128,128]{2,1,0:T(8,128)S(1)}, f32[8,128,2,8,128]{1,4,3,2,0:T(8,128)}, f32[8,128,2,8,128]{4,3,2,1,0:T(8,128)}, s32[8]{0:T(128)...) while((s32[]{:T(128)}, f32[2,128,128]{2,1,0:T(8,128)S(1)}, ...), condition=%wide.region_4.5_spmd.clone, body=%wide.region_1.4_spmd.clone.sunk | while | flops 2869842432 | bytes 21551412 | solution.py:101
  66.4 2.4 fusion.72
  70.7 3.4 %fusion.74 = (f32[2,8,128]{2,1,0:T(8,128)S(1)}, f32[2,255,128,8]{2,1,3,0:T(8,128)S(1)}) fusion(pred[128,255]{0,1:T(8,128)(4,1)S(1)} %and_and_fusion.2, f32[1024,2,8,128]{0,3,2,1:T(8,128)} %get-tuple-element.416, s32[]{:T(128)S(6)} %select_n.86, f32[1151,2,128]{0,2,1:T(8,128)} %get-tuple-element.415, s32[]{:T(128)S(6)} %select_n.87), kind=kOutput, calls=%fused_computation.5.clone.1 | convolution fusion | flops 803725312 | bytes 3440520 | tf_op jit(solution)/shard_map/while/body/eval_jaxpr/cmop,nmp->mocn/dot_general | solution.py:87
  74.6 2.7 %fusion.76 = f32[1,128,2,8,128]{1,4,3,2,0:T(8,128)S(1)} fusion(f32[2,255,128,8]{2,1,3,0:T(8,128)S(1)} %get-tuple-element.367, f32[2,8,128]{2,1,0:T(8,128)S(1)} %get-tuple-element.368, pred[128,255]{0,1:T(8,128)(4,1)S(1)} %and_and_fusion.2, f32[128,2,8]{0,2,1:T(8,128)S(1)} %bitcast.128, f32[1151,2,128]{0,2,1:T(8,128)} %get-tuple-element.413, ...), kind=kOutput, calls=%fused_computation.18.clone.1 | convolution fusion | flops 804511744 | bytes 3448708 | tf_op jit(solution)/shard_map/while/body/eval_jaxpr/xjpa,axf->pxjf/dot_general | solution.py:94
  78.9 3.3 %fusion.73 = f32[8,128,2,8,128]{1,4,3,2,0:T(8,128)} fusion(f32[8,128,2,8,128]{1,4,3,2,0:T(8,128)} %get-tuple-element.389, s32[]{:T(128)S(6)} %copy.77, f32[128,2,8,128]{0,3,2,1:T(8,128)S(1)} %convolution_bitcast_fusion.4, f32[1024,2,8,128]{0,3,2,1:T(8,128)} %get-tuple-element.412, s32[]{:T(128)S(6)} %select_n.86, ...), kind=kOutput, calls=%fused_computation.12.clone.1 | convolution fusion | flops 402915328 | bytes 3276808 | tf_op jit(solution)/shard_map/while/body/eval_jaxpr/tgrd,gde->tgre/dot_general | solution.py:69
  85.1 2.4 fusion.72
  87.4 1.9 convolution_bitcast_fusion.4
  89.3 3.4 %fusion.74 = (f32[2,8,128]{2,1,0:T(8,128)S(1)}, f32[2,255,128,8]{2,1,3,0:T(8,128)S(1)}) fusion(pred[128,255]{0,1:T(8,128)(4,1)S(1)} %and_and_fusion.2, f32[1024,2,8,128]{0,3,2,1:T(8,128)} %get-tuple-element.416, s32[]{:T(128)S(6)} %select_n.86, f32[1151,2,128]{0,2,1:T(8,128)} %get-tuple-element.415, s32[]{:T(128)S(6)} %select_n.87), kind=kOutput, calls=%fused_computation.5.clone.1 | convolution fusion | flops 803725312 | bytes 3440520 | tf_op jit(solution)/shard_map/while/body/eval_jaxpr/cmop,nmp->mocn/dot_general | solution.py:87
  93.3 2.7 fusion.76
  97.7 3.3 %fusion.73 = f32[8,128,2,8,128]{1,4,3,2,0:T(8,128)} fusion(f32[8,128,2,8,128]{1,4,3,2,0:T(8,128)} %get-tuple-element.389, s32[]{:T(128)S(6)} %copy.77, f32[128,2,8,128]{0,3,2,1:T(8,128)S(1)} %convolution_bitcast_fusion.4, f32[1024,2,8,128]{0,3,2,1:T(8,128)} %get-tuple-element.412, s32[]{:T(128)S(6)} %select_n.86, ...), kind=kOutput, calls=%fused_computation.12.clone.1 | convolution fusion | flops 402915328 | bytes 3276808 | tf_op jit(solution)/shard_map/while/body/eval_jaxpr/tgrd,gde->tgre/dot_general | solution.py:69
  103.8 2.4 fusion.72
  108.1 3.4 %fusion.74 = (f32[2,8,128]{2,1,0:T(8,128)S(1)}, f32[2,255,128,8]{2,1,3,0:T(8,128)S(1)}) fusion(pred[128,255]{0,1:T(8,128)(4,1)S(1)} %and_and_fusion.2, f32[1024,2,8,128]{0,3,2,1:T(8,128)} %get-tuple-element.416, s32[]{:T(128)S(6)} %select_n.86, f32[1151,2,128]{0,2,1:T(8,128)} %get-tuple-element.415, s32[]{:T(128)S(6)} %select_n.87), kind=kOutput, calls=%fused_computation.5.clone.1 | convolution fusion | flops 803725312 | bytes 3440520 | tf_op jit(solution)/shard_map/while/body/eval_jaxpr/cmop,nmp->mocn/dot_general | solution.py:87
  112.0 2.7 fusion.76
  116.3 3.3 %fusion.73 = f32[8,128,2,8,128]{1,4,3,2,0:T(8,128)} fusion(f32[8,128,2,8,128]{1,4,3,2,0:T(8,128)} %get-tuple-element.389, s32[]{:T(128)S(6)} %copy.77, f32[128,2,8,128]{0,3,2,1:T(8,128)S(1)} %convolution_bitcast_fusion.4, f32[1024,2,8,128]{0,3,2,1:T(8,128)} %get-tuple-element.412, s32[]{:T(128)S(6)} %select_n.86, ...), kind=kOutput, calls=%fused_computation.12.clone.1 | convolution fusion | flops 402915328 | bytes 3276808 | tf_op jit(solution)/shard_map/while/body/eval_jaxpr/tgrd,gde->tgre/dot_general | solution.py:69
  122.5 2.4 fusion.72
  126.8 3.4 %fusion.74 = (f32[2,8,128]{2,1,0:T(8,128)S(1)}, f32[2,255,128,8]{2,1,3,0:T(8,128)S(1)}) fusion(pred[128,255]{0,1:T(8,128)(4,1)S(1)} %and_and_fusion.2, f32[1024,2,8,128]{0,3,2,1:T(8,128)} %get-tuple-element.416, s32[]{:T(128)S(6)} %select_n.86, f32[1151,2,128]{0,2,1:T(8,128)} %get-tuple-element.415, s32[]{:T(128)S(6)} %select_n.87), kind=kOutput, calls=%fused_computation.5.clone.1 | convolution fusion | flops 803725312 | bytes 3440520 | tf_op jit(solution)/shard_map/while/body/eval_jaxpr/cmop,nmp->mocn/dot_general | solution.py:87
  130.7 2.7 fusion.76
  135.0 3.3 %fusion.73 = f32[8,128,2,8,128]{1,4,3,2,0:T(8,128)} fusion(f32[8,128,2,8,128]{1,4,3,2,0:T(8,128)} %get-tuple-element.389, s32[]{:T(128)S(6)} %copy.77, f32[128,2,8,128]{0,3,2,1:T(8,128)S(1)} %convolution_bitcast_fusion.4, f32[1024,2,8,128]{0,3,2,1:T(8,128)} %get-tuple-element.412, s32[]{:T(128)S(6)} %select_n.86, ...), kind=kOutput, calls=%fused_computation.12.clone.1 | convolution fusion | flops 402915328 | bytes 3276808 | tf_op jit(solution)/shard_map/while/body/eval_jaxpr/tgrd,gde->tgre/dot_general | solution.py:69
  141.2 2.4 fusion.72
  145.5 3.4 %fusion.74 = (f32[2,8,128]{2,1,0:T(8,128)S(1)}, f32[2,255,128,8]{2,1,3,0:T(8,128)S(1)}) fusion(pred[128,255]{0,1:T(8,128)(4,1)S(1)} %and_and_fusion.2, f32[1024,2,8,128]{0,3,2,1:T(8,128)} %get-tuple-element.416, s32[]{:T(128)S(6)} %select_n.86, f32[1151,2,128]{0,2,1:T(8,128)} %get-tuple-element.415, s32[]{:T(128)S(6)} %select_n.87), kind=kOutput, calls=%fused_computation.5.clone.1 | convolution fusion | flops 803725312 | bytes 3440520 | tf_op jit(solution)/shard_map/while/body/eval_jaxpr/cmop,nmp->mocn/dot_general | solution.py:87
  149.4 2.7 %fusion.76 = f32[1,128,2,8,128]{1,4,3,2,0:T(8,128)S(1)} fusion(f32[2,255,128,8]{2,1,3,0:T(8,128)S(1)} %get-tuple-element.367, f32[2,8,128]{2,1,0:T(8,128)S(1)} %get-tuple-element.368, pred[128,255]{0,1:T(8,128)(4,1)S(1)} %and_and_fusion.2, f32[128,2,8]{0,2,1:T(8,128)S(1)} %bitcast.128, f32[1151,2,128]{0,2,1:T(8,128)} %get-tuple-element.413, ...), kind=kOutput, calls=%fused_computation.18.clone.1 | convolution fusion | flops 804511744 | bytes 3448708 | tf_op jit(solution)/shard_map/while/body/eval_jaxpr/xjpa,axf->pxjf/dot_general | solution.py:94
  153.7 3.3 %fusion.73 = f32[8,128,2,8,128]{1,4,3,2,0:T(8,128)} fusion(f32[8,128,2,8,128]{1,4,3,2,0:T(8,128)} %get-tuple-element.389, s32[]{:T(128)S(6)} %copy.77, f32[128,2,8,128]{0,3,2,1:T(8,128)S(1)} %convolution_bitcast_fusion.4, f32[1024,2,8,128]{0,3,2,1:T(8,128)} %get-tuple-element.412, s32[]{:T(128)S(6)} %select_n.86, ...), kind=kOutput, calls=%fused_computation.12.clone.1 | convolution fusion | flops 402915328 | bytes 3276808 | tf_op jit(solution)/shard_map/while/body/eval_jaxpr/tgrd,gde->tgre/dot_general | solution.py:69
  159.9 2.4 fusion.72
  164.1 3.4 %fusion.74 = (f32[2,8,128]{2,1,0:T(8,128)S(1)}, f32[2,255,128,8]{2,1,3,0:T(8,128)S(1)}) fusion(pred[128,255]{0,1:T(8,128)(4,1)S(1)} %and_and_fusion.2, f32[1024,2,8,128]{0,3,2,1:T(8,128)} %get-tuple-element.416, s32[]{:T(128)S(6)} %select_n.86, f32[1151,2,128]{0,2,1:T(8,128)} %get-tuple-element.415, s32[]{:T(128)S(6)} %select_n.87), kind=kOutput, calls=%fused_computation.5.clone.1 | convolution fusion | flops 803725312 | bytes 3440520 | tf_op jit(solution)/shard_map/while/body/eval_jaxpr/cmop,nmp->mocn/dot_general | solution.py:87
  168.1 2.7 fusion.76
  172.4 3.3 %fusion.73 = f32[8,128,2,8,128]{1,4,3,2,0:T(8,128)} fusion(f32[8,128,2,8,128]{1,4,3,2,0:T(8,128)} %get-tuple-element.389, s32[]{:T(128)S(6)} %copy.77, f32[128,2,8,128]{0,3,2,1:T(8,128)S(1)} %convolution_bitcast_fusion.4, f32[1024,2,8,128]{0,3,2,1:T(8,128)} %get-tuple-element.412, s32[]{:T(128)S(6)} %select_n.86, ...), kind=kOutput, calls=%fused_computation.12.clone.1 | convolution fusion | flops 402915328 | bytes 3276808 | tf_op jit(solution)/shard_map/while/body/eval_jaxpr/tgrd,gde->tgre/dot_general | solution.py:69
  178.6 2.4 fusion.72
  182.8 3.4 %fusion.74 = (f32[2,8,128]{2,1,0:T(8,128)S(1)}, f32[2,255,128,8]{2,1,3,0:T(8,128)S(1)}) fusion(pred[128,255]{0,1:T(8,128)(4,1)S(1)} %and_and_fusion.2, f32[1024,2,8,128]{0,3,2,1:T(8,128)} %get-tuple-element.416, s32[]{:T(128)S(6)} %select_n.86, f32[1151,2,128]{0,2,1:T(8,128)} %get-tuple-element.415, s32[]{:T(128)S(6)} %select_n.87), kind=kOutput, calls=%fused_computation.5.clone.1 | convolution fusion | flops 803725312 | bytes 3440520 | tf_op jit(solution)/shard_map/while/body/eval_jaxpr/cmop,nmp->mocn/dot_general | solution.py:87
  186.8 2.7 %fusion.76 = f32[1,128,2,8,128]{1,4,3,2,0:T(8,128)S(1)} fusion(f32[2,255,128,8]{2,1,3,0:T(8,128)S(1)} %get-tuple-element.367, f32[2,8,128]{2,1,0:T(8,128)S(1)} %get-tuple-element.368, pred[128,255]{0,1:T(8,128)(4,1)S(1)} %and_and_fusion.2, f32[128,2,8]{0,2,1:T(8,128)S(1)} %bitcast.128, f32[1151,2,128]{0,2,1:T(8,128)} %get-tuple-element.413, ...), kind=kOutput, calls=%fused_computation.18.clone.1 | convolution fusion | flops 804511744 | bytes 3448708 | tf_op jit(solution)/shard_map/while/body/eval_jaxpr/xjpa,axf->pxjf/dot_general | solution.py:94
  191.1 3.3 %fusion.73 = f32[8,128,2,8,128]{1,4,3,2,0:T(8,128)} fusion(f32[8,128,2,8,128]{1,4,3,2,0:T(8,128)} %get-tuple-element.389, s32[]{:T(128)S(6)} %copy.77, f32[128,2,8,128]{0,3,2,1:T(8,128)S(1)} %convolution_bitcast_fusion.4, f32[1024,2,8,128]{0,3,2,1:T(8,128)} %get-tuple-element.412, s32[]{:T(128)S(6)} %select_n.86, ...), kind=kOutput, calls=%fused_computation.12.clone.1 | convolution fusion | flops 402915328 | bytes 3276808 | tf_op jit(solution)/shard_map/while/body/eval_jaxpr/tgrd,gde->tgre/dot_general | solution.py:69
  197.3 2.4 fusion.72
  201.6 3.4 %fusion.74 = (f32[2,8,128]{2,1,0:T(8,128)S(1)}, f32[2,255,128,8]{2,1,3,0:T(8,128)S(1)}) fusion(pred[128,255]{0,1:T(8,128)(4,1)S(1)} %and_and_fusion.2, f32[1024,2,8,128]{0,3,2,1:T(8,128)} %get-tuple-element.416, s32[]{:T(128)S(6)} %select_n.86, f32[1151,2,128]{0,2,1:T(8,128)} %get-tuple-element.415, s32[]{:T(128)S(6)} %select_n.87), kind=kOutput, calls=%fused_computation.5.clone.1 | convolution fusion | flops 803725312 | bytes 3440520 | tf_op jit(solution)/shard_map/while/body/eval_jaxpr/cmop,nmp->mocn/dot_general | solution.py:87
  205.5 2.7 fusion.76
  209.7 3.3 %fusion.73 = f32[8,128,2,8,128]{1,4,3,2,0:T(8,128)} fusion(f32[8,128,2,8,128]{1,4,3,2,0:T(8,128)} %get-tuple-element.389, s32[]{:T(128)S(6)} %copy.77, f32[128,2,8,128]{0,3,2,1:T(8,128)S(1)} %convolution_bitcast_fusion.4, f32[1024,2,8,128]{0,3,2,1:T(8,128)} %get-tuple-element.412, s32[]{:T(128)S(6)} %select_n.86, ...), kind=kOutput, calls=%fused_computation.12.clone.1 | convolution fusion | flops 402915328 | bytes 3276808 | tf_op jit(solution)/shard_map/while/body/eval_jaxpr/tgrd,gde->tgre/dot_general | solution.py:69
  214.4 4.3 %multiply_reduce_fusion = f32[8,128]{1,0:T(8,128)S(1)} fusion(f32[8,128,2,8,128]{1,4,3,2,0:T(8,128)} %get-tuple-element.192), kind=kLoop, calls=%fused_computation.56 | loop fusion | flops 4193280 | bytes 8392704 | tf_op jit(solution)/shard_map/reduce_sum | solution.py:104
  218.7 9.2 %copy.46 = f32[8,128,2,8,128]{4,3,2,1,0:T(8,128)} copy(f32[8,128,2,8,128]{1,4,3,2,0:T(8,128)} %get-tuple-element.192) | data formatting | bytes 16777216 | tf_op jit(solution)/shard_map/while | solution.py:101
  227.9 9.2 %reshape.136 = f32[1024,2048]{1,0:T(8,128)} reshape(f32[8,128,2,8,128]{4,3,2,1,0:T(8,128)} %get-tuple-element.193) | data formatting | bytes 16777216 | tf_op jit(solution)/shard_map/reshape | solution.py:103
  237.1 9.3 %reshape.135 = f32[1024,2048]{1,0:T(8,128)} reshape(f32[8,128,2,8,128]{4,3,2,1,0:T(8,128)} %copy.46) | data formatting | bytes 16777216 | tf_op jit(solution)/shard_map/reshape | solution.py:102
  246.4 10.6 %psum.7 = f32[1024]{0:T(1024)S(1)} all-reduce(f32[1024]{0:T(1024)S(1)} %bitcast.129), channel_id=1, replica_groups=mesh['seq'=32,'head'=4] {'head'}, use_global_device_ids=true, to_apply=%region_6.7 | all-reduce | flops 1024 | bytes 8192 | tf_op jit(solution)/shard_map/psum | solution.py:105
  257.1 9.3 %multiply_add_fusion = f32[1024,2048]{1,0:T(8,128)} fusion(f32[1024,2048]{1,0:T(8,128)} %reshape.136, f32[1024,2048]{1,0:T(8,128)} %reshape.135, f32[2048]{0:T(1024)S(1)} %copy-done, f32[1024]{0:T(1024)S(1)} %add_sqrt_fusion), kind=kLoop, calls=%fused_computation.55 | loop fusion | flops 6291456 | bytes 25178112 | tf_op jit(solution)/shard_map/add | solution.py:111
  (105 shorter events, 53.6 us)
Async XLA Ops:
  6.5 55.7 %all-gather.3.cloned.1.call-start = ((), (), s32[]{:S(2)}) async-start(), calls=%async_computation | async-start | bytes 4325376 | tf_op jit(solution)/shard_map/all_gather | solution.py:37
  14.6 25.5 %collective-permute-start = (f32[127,256]{1,0:T(8,128)S(1)}, f32[127,256]{1,0:T(8,128)S(1)}, u32[]{:S(2)}, u32[]{:S(2)}) collective-permute-start(f32[127,256]{1,0:T(8,128)S(1)} %slice.6), channel_id=1, source_target_pairs={{0,4},{4,8},{8,12},{12,16},{16,20},{20,24},{24,28},{28,32},{32,36}... | collective-permute-start | bytes 390152 | tf_op jit(solution)/shard_map/ppermute | solution.py:20
  16.8 23.3 %collective-permute-start.1 = (f32[127,256]{1,0:T(8,128)S(1)}, f32[127,256]{1,0:T(8,128)S(1)}, u32[]{:S(2)}, u32[]{:S(2)}) collective-permute-start(f32[127,256]{1,0:T(8,128)S(1)} %slice.7), channel_id=1, source_target_pairs={{0,4},{4,8},{8,12},{12,16},{16,20},{20,24},{24,28},{28,32},{32,36}... | collective-permute-start | bytes 390152 | tf_op jit(solution)/shard_map/ppermute | solution.py:20
  237.1 20.0 %copy-start = (f32[2048]{0:T(1024)S(1)}, f32[2048]{0:T(1024)}, u32[]{:S(2)}) copy-start(f32[2048]{0:T(1024)} %param.9) | copy-start | bytes 24580
Sparse Core Ops, SparseCore 0:
  13.8 48.3 all-gather.2
where the time goes:
time: 276 us; the launch traced here: 273 us
  matrix products  123 us (45%)
  local copies, waits for them, and re-layouts  70.7 us (26%)
  other arithmetic  25.1 us (9%)
  waiting for transfers between devices  18.6 us (7%)
  between operations  13.5 us (5%)
  blocking collectives  10.6 us (4%)
  loops' own time  5.97 us (2%)
  starting transfers between devices  5.54 us (2%)
    dot_general x8, matrix products, advance(): jnp.einsum('cmop,nmp->mocn', query_block, key_block, precision=HIGH_ACCUR...  27.4 us
    dot_general x8, matrix products, advance(): jnp.einsum('tgrd,gde->tgre', query_feature_block, state, precision=HIGH_A...  26 us
    dot_general x8, matrix products, advance(): jnp.einsum('xjpa,axf->pxjf', softmax_weights, key_value_block, precision=...  21.8 us
    dot_general x8, matrix products, advance(): jnp.einsum('cmop,nmp->mocn', query_feature_block, key_feature_block, prec...  18.9 us
    all_gather x1, waiting for transfers between devices, shards(): piece = lax.all_gather(own_state[None], 'seq', axis=0, tiled=True)  18.6 us
    dot_general x8, matrix products, advance(): jnp.einsum('xjpa,axf->pxjf', inner_product, value_block, precision=HIGH_A...  15.2 us
    unnamed x5, local copies, waits for them, and re-layouts  13.4 us
    dynamic_update_slice x16, local copies, waits for them, and re-layouts, shards(): _, (linear_branch, window_length) = lax.scan(advance, prior, numbers)  12.6 us
  transfers between devices with their start and end apart: 3, of which 1 were waited for; matrix products, arithmetic and copies ran while one was open for 9% of the time, Pallas kernels for 0%

commit v1 on v0

v1 whole, which is shorter than its diff:
```python
import math

import jax
import jax.numpy as jnp
from jax import lax
from jax.experimental import pallas as pl
from jax.experimental.pallas import tpu as pltpu
from jax.sharding import PartitionSpec as P

QUERY_HEADS = 64
KEY_VALUE_HEADS = 8
D = 128
G = QUERY_HEADS // KEY_VALUE_HEADS
BLOCK = 128
EPS = 1e-6
SCORE_SCALE = math.log2(math.e) / math.sqrt(D)

f32 = jnp.float32
bf = jnp.bfloat16
NT = (((1,), (1,)), ((), ()))
TN = (((0,), (0,)), ((), ()))


def split(x):
    hi = x.astype(bf)
    return hi, (x - hi.astype(f32)).astype(bf)


def lanes(*xs):
    return jnp.concatenate(xs, axis=1)


def rows(*xs):
    return jnp.concatenate(xs, axis=0)


def dot(a, b, dims=(((1,), (0,)), ((), ()))):
    return lax.dot_general(a, b, dims, preferred_element_type=f32)


def halves(x):
    return x[:, :D] + x[:, D:]


def params(mib):
    return pltpu.CompilerParams(
        vmem_limit_bytes=mib << 20, dimension_semantics=("arbitrary", "arbitrary")
    )


def state_body(k_ref, v_ref, before_ref, total_ref):
    state = jnp.zeros((D, D), f32)
    for b in range(k_ref.shape[0] // BLOCK):
        at = slice(b * BLOCK, (b + 1) * BLOCK)
        before_ref[b] = state
        fh, fl = split(jnp.tanh(k_ref[at, :]))
        vh, vl = split(v_ref[at, :])
        vv = lanes(vh, vl)
        state = state + halves(dot(rows(fh, fl), rows(vv, vv), TN))
    total_ref[0] = state


def local_states(keys, values):
    count, width = keys.shape
    kv, nb = width // D, count // BLOCK
    return pl.pallas_call(
        state_body,
        grid=(kv, 1),
        in_specs=[pl.BlockSpec((count, D), lambda g, _: (0, g))] * 2,
        out_specs=[
            pl.BlockSpec((pl.Squeezed(), nb, D, D), lambda g, _: (g, 0, 0, 0)),
            pl.BlockSpec((1, D, D), lambda g, _: (g, 0, 0)),
        ],
        out_shape=[
            jax.ShapeDtypeStruct((kv, nb, D, D), f32),
            jax.ShapeDtypeStruct((kv, D, D), f32),
        ],
        compiler_params=params(5),
        name="local_states",
    )(keys, values)


def block_body(wrap, *refs):
    q_ref, k_ref, v_ref, kp_ref, vp_ref, *refs = refs
    if wrap is not None:
        kw_ref, vw_ref, *refs = refs
    win_ref, lin_ref, fq_ref, kh, kl, vv = refs
    b = pl.program_id(1)

    def prepare(k, v, at):
        h, l = split(k * SCORE_SCALE)
        kh[at, :] = lanes(h, h)
        kl[at, :] = lanes(l, l)
        vv[at, :] = lanes(*split(v))

    here = slice(0, BLOCK)
    there = slice(BLOCK, 2 * BLOCK)

    @pl.when(b == 0)
    def _():
        prepare(kp_ref[...], vp_ref[...], there)

    @pl.when(b > 0)
    def _():
        for x in (kh, kl, vv):
            x[there, :] = x[here, :]

    if wrap is not None:

        @pl.when(b == wrap)
        def _():
            prepare(kw_ref[...], vw_ref[...], there)

    k = k_ref[...]
    prepare(k, v_ref[...], here)
    fh, fl = split(jnp.tanh(k))
    ff = rows(lanes(fh, fh), lanes(fl, fl))
    kk = lanes(kh[...], kl[...])
    v_both = vv[...]
    v_own = vv[here, :]
    row = lax.broadcasted_iota(jnp.int32, (BLOCK, BLOCK), 0)
    col = lax.broadcasted_iota(jnp.int32, (BLOCK, BLOCK), 1)
    own = rows(*[row >= col] * G)
    zero = jnp.zeros((BLOCK * G, BLOCK), bf)

    q = rows(*[q_ref[:, i * D : (i + 1) * D] for i in range(G)])
    qh, ql = split(q)
    s = dot(lanes(qh, ql, qh, ql), kk, NT)
    f2 = lanes(*split(jnp.tanh(q)))
    for i in range(G):
        fq_ref[i] = f2[i * BLOCK : (i + 1) * BLOCK]
    a = jnp.where(own, halves(dot(f2, ff, NT)), 0.0)
    lin = halves(dot(lanes(*split(a)), rows(v_own, v_own)))
    before = s[:, BLOCK:]
    if wrap is not None:
        before = jnp.where((lax.axis_index("seq") > 0) | (b != wrap), before, -1e30)
    t = jnp.where(own, s[:, :BLOCK], before)
    p = jnp.exp2(t - jnp.max(t, axis=1, keepdims=True))
    total = jnp.sum(p, axis=1, keepdims=True)
    ph, pl_ = split(p)
    p4 = lanes(
        jnp.where(own, ph, zero),
        jnp.where(own, zero, ph),
        jnp.where(own, pl_, zero),
        jnp.where(own, zero, pl_),
    )
    win = halves(dot(p4, rows(v_both, v_both))) * (1.0 / total)
    for i in range(G):
        win_ref[:, i * D : (i + 1) * D] = win[i * BLOCK : (i + 1) * BLOCK]
        lin_ref[:, i * D : (i + 1) * D] = lin[i * BLOCK : (i + 1) * BLOCK]


def block_part(queries, keys, values, first, nb, wrap=None):
    count, width = queries.shape
    kv = keys.shape[1] // D
    total = count // BLOCK
    own = lambda g, b: ((first + b) % total, g)
    prior = lambda g, b: (first - 1, g)
    small = lambda index: pl.BlockSpec((BLOCK, D), index)
    args = [queries, keys, values, keys, values]
    specs = [pl.BlockSpec((BLOCK, G * D), own), small(own), small(own), small(prior), small(prior)]
    step = None
    if wrap is not None:
        step = total - first
        last = lambda g, b: (0, g)
        args += wrap
        specs += [small(last), small(last)]
    big = pl.BlockSpec((BLOCK, G * D), lambda g, b: (b, g))
    return pl.pallas_call(
        lambda *refs: block_body(step, *refs),
        grid=(kv, nb),
        in_specs=specs,
        out_specs=[big, big, pl.BlockSpec((G, BLOCK, 2 * D), lambda g, b: (g, b, 0))],
        out_shape=[
            jax.ShapeDtypeStruct((nb * BLOCK, width), f32),
            jax.ShapeDtypeStruct((nb * BLOCK, width), f32),
            jax.ShapeDtypeStruct((kv * G, nb * BLOCK, 2 * D), bf),
        ],
        scratch_shapes=[pltpu.VMEM((2 * BLOCK, 2 * D), bf)] * 3,
        compiler_params=params(10),
        name=f"blocks_{first}_{nb}",
    )(*args)


class Pieces:
    def __init__(self, spans, total):
        self.spans = spans
        self.start = [sum(n for _, n in spans[:i]) for i in range(len(spans))]
        self.first, self.total = spans[0][0], total

    def block(self, j):
        return (j + self.first) % self.total

    def local(self, p):
        s, n = self.start[p], self.spans[p][1]
        return lambda j: jnp.clip(j - s, 0, n - 1)

    def when(self, p, j):
        s, n = self.start[p], self.spans[p][1]
        return pl.when((j >= s) & (j < s + n))


def linear_body(pieces, *refs):
    n = len(pieces.spans)
    fq_refs, part_refs = refs[:n], refs[n : 2 * n]
    before_ref, incl_ref, total_ref, lin_ref, sq_ref, acc = refs[2 * n :]
    j, g = pl.program_id(0), pl.program_id(1)
    ss = lanes(*split((incl_ref[0] - total_ref[0]) + before_ref[...]))
    ss = rows(ss, ss)

    def run(fq_ref, part_ref):
        lin = halves(dot(rows(*[fq_ref[i] for i in range(G)]), ss))
        sq = jnp.zeros((BLOCK, D), f32)
        for i in range(G):
            at = slice(i * D, (i + 1) * D)
            x = lin[i * BLOCK : (i + 1) * BLOCK] + part_ref[:, at]
            lin_ref[:, at] = x
            sq = sq + x * x

        @pl.when(g == 0)
        def _():
            acc[...] = sq

        @pl.when(g > 0)
        def _():
            sq_ref[0] = jnp.sum((acc[...] + sq).T, axis=0, keepdims=True)

    for p in range(n):

        @pieces.when(p, j)
        def _():
            run(fq_refs[p], part_refs[p])


def linear_part(pieces, fq, part, before, incl, total):
    width = part[0].shape[1]
    nb = pieces.total
    kv = total.shape[0]
    assert kv == 2
    fq_specs, part_specs = [], []
    for p in range(len(fq)):
        at = pieces.local(p)
        fq_specs.append(pl.BlockSpec((G, BLOCK, 2 * D), lambda j, g, at=at: (g, at(j), 0)))
        part_specs.append(pl.BlockSpec((BLOCK, G * D), lambda j, g, at=at: (at(j), g)))
    return pl.pallas_call(
        lambda *refs: linear_body(pieces, *refs),
        grid=(nb, kv),
        in_specs=fq_specs
        + part_specs
        + [
            pl.BlockSpec(
                (pl.Squeezed(), pl.Squeezed(), D, D), lambda j, g: (g, pieces.block(j), 0, 0)
            ),
            pl.BlockSpec((1, D, D), lambda j, g: (g, 0, 0)),
            pl.BlockSpec((1, D, D), lambda j, g: (g, 0, 0)),
        ],
        out_specs=[
            pl.BlockSpec((BLOCK, G * D), lambda j, g: (pieces.block(j), g)),
            pl.BlockSpec((1, 1, BLOCK), lambda j, g: (pieces.block(j), 0, 0)),
        ],
        out_shape=[
            jax.ShapeDtypeStruct((nb * BLOCK, width), f32),
            jax.ShapeDtypeStruct((nb, 1, BLOCK), f32),
        ],
        scratch_shapes=[pltpu.VMEM((BLOCK, D), f32)],
        compiler_params=params(12),
        name="linear",
    )(*fq, *part, before, incl, total)


def combine_body(pieces, *refs):
    n = len(pieces.spans)
    win_refs = refs[:n]
    lin_ref, sa_ref, sb_ref, gain_ref, out_ref = refs[n:]
    ms = (sa_ref[0] + sb_ref[0]) * (1.0 / (QUERY_HEADS * D))
    inv = lax.rsqrt(ms + EPS)
    inv = jnp.broadcast_to(inv, (BLOCK, BLOCK)).T
    for p in range(n):

        @pieces.when(p, pl.program_id(0))
        def _():
            for i in range(lin_ref.shape[1] // D):
                at = slice(i * D, (i + 1) * D)
                out_ref[:, at] = lin_ref[:, at] * inv * gain_ref[:, at] + win_refs[p][:, at]


def combine(pieces, win, lin, sa, sb, gain):
    count, width = lin.shape
    nb = count // BLOCK
    big = pl.BlockSpec((BLOCK, width), lambda j, _: (pieces.block(j), 0))
    small = pl.BlockSpec((1, 1, BLOCK), lambda j, _: (pieces.block(j), 0, 0))
    win_specs = []
    for p in range(len(win)):
        at = pieces.local(p)
        win_specs.append(pl.BlockSpec((BLOCK, width), lambda j, _, at=at: (at(j), 0)))
    return pl.pallas_call(
        lambda *refs: combine_body(pieces, *refs),
        grid=(nb, 1),
        in_specs=win_specs
        + [big, small, small, pl.BlockSpec((1, width), lambda j, _: (0, 0))],
        out_specs=big,
        out_shape=jax.ShapeDtypeStruct((count, width), f32),
        compiler_params=params(12),
        name="combine",
    )(*win, lin, sa, sb, gain)


def shards(queries, keys, values, gain):
    count, kv = keys.shape
    nb = count // BLOCK
    peers = lax.axis_size("seq")
    heads = lax.axis_size("head")
    assert heads == 4 and nb == 8 and peers == 32

    tail = jnp.concatenate([keys[count - BLOCK :], values[count - BLOCK :]], axis=1)
    halo = lax.ppermute(tail, "seq", [(i, i + 1) for i in range(peers - 1)])
    before, total = local_states(keys, values)

    def behind(x, by):
        return lax.ppermute(x, "seq", [(i, i + by) for i in range(peers - by)])

    pieces = Pieces([(1, 1), (2, 1), (3, 1), (4, 2), (6, 3)], nb)
    incl = total
    q = pltpu.with_memory_space_constraint(queries, pltpu.HBM)
    done = []
    for number, (first, n) in enumerate(pieces.spans):
        got = behind(incl, 1 << number)
        q, incl = lax.optimization_barrier((q, incl))
        wrap = None
        if first + n > nb:
            wrap = [halo[:, :kv], halo[:, kv:]]
        part = block_part(q, keys, values, first, n, wrap)
        *part, got = lax.optimization_barrier((*part, got))
        done.append(part)
        incl = incl + got
    win, part, fq = zip(*done)
    lin, sq = linear_part(pieces, fq, part, before, incl, total)
    sq = sq + lax.ppermute(sq, "head", [(i, i ^ 1) for i in range(heads)])
    other = lax.ppermute(sq, "head", [(i, i ^ 2) for i in range(heads)])
    return combine(pieces, win, lin, sq, other, gain[None, :])


def solution(mesh):
    in_specs = (P("seq", "head"), P("seq", "head"), P("seq", "head"), P("head"))
    return jax.shard_map(
        shards, mesh=mesh, in_specs=in_specs, out_specs=P("seq", "head"), check_vma=False
    )
```

time: 276 us -> 83 us (0.30)
  matrix products: 123 us -> 0 us
  local copies, waits for them, and re-layouts: 70.7 us -> 4.94 us
  Pallas kernels: 0 us -> 42.9 us
  starting transfers between devices: 5.54 us -> 30.9 us
  other arithmetic: 25.1 us -> 0.11 us
  waiting for transfers between devices: 18.6 us -> 3.29 us
  between operations: 13.5 us -> 0.28 us
  blocking collectives: 10.6 us -> 0 us
  loops' own time: 5.97 us -> 0 us
    dot_general x49 -> x0, matrix products: 123 us -> none  [the longest x8 27.4 us: advance(): jnp.einsum('cmop,nmp->mocn', query_block, key_block, precision=HIGH_ACCUR...]
    pallas_call x0 -> x8, Pallas kernels: none -> 42.9 us  [the longest x5 24.2 us: block_part(): pl.pallas_call(lambda *refs: block_body(step, *refs), grid=(kv, nb), in_s...]
    ppermute x2 -> x8, starting transfers between devices: 5.54 us -> 30.9 us  [the longest x5 23.1 us: behind(): return lax.ppermute(x, 'seq', [(i, i + by) for i in range(peers - by)])]
    all_gather x1 -> x0, waiting for transfers between devices: 18.6 us -> none  [shards(): piece = lax.all_gather(own_state[None], 'seq', axis=0, tiled=True)]
    reshape x2 -> x0, local copies, waits for them, and re-layouts: 18.5 us -> none  [the longest x1 9.29 us: shards(): linear_branch = linear_branch.reshape(count, queries.shape[1])]
    dynamic_update_slice x16 -> x0, local copies, waits for them, and re-layouts: 12.6 us -> none  [shards(): _, (linear_branch, window_length) = lax.scan(advance, prior, numbers)]
    reduce_sum x10 -> x0, other arithmetic: 11 us -> none  [the longest x1 4.31 us: shards(): squares = jnp.sum(linear_branch * linear_branch, axis=1)]
    psum x1 -> x0, blocking collectives: 10.6 us -> none  [shards(): squares = lax.psum(squares, 'head')]
  transfers between devices with their start and end apart: 3 -> 8, of which waited for: 1 -> 2; matrix products, arithmetic and copies ran while one was open for 9% -> 0% of each run, Pallas kernels for 0% -> 29%
where the time goes in v1:
time: 83 us; the launch traced here: 82.5 us
  Pallas kernels  42.9 us (52%)
  starting transfers between devices  30.9 us (37%)
  local copies, waits for them, and re-layouts  4.94 us (6%)
  waiting for transfers between devices  3.29 us (4%)
    pallas_call x5, Pallas kernels, block_part(): pl.pallas_call(lambda *refs: block_body(step, *refs), grid=(kv, nb), in_s...  24.2 us
    ppermute x5, starting transfers between devices, behind(): return lax.ppermute(x, 'seq', [(i, i + by) for i in range(peers - by)])  23.1 us
    pallas_call x1, Pallas kernels, linear_part(): pl.pallas_call(lambda *refs: linear_body(pieces, *refs), grid=(nb, kv), i...  12.3 us
    pallas_call x1, Pallas kernels, combine(): pl.pallas_call(lambda *refs: combine_body(pieces, *refs), grid=(nb, 1), i...  5.46 us
    unnamed x14, local copies, waits for them, and re-layouts  4.91 us
    ppermute x1, starting transfers between devices, shards(): other = lax.ppermute(sq, 'head', [(i, i ^ 2) for i in range(heads)])  3.88 us
    ppermute x1, starting transfers between devices, shards(): sq = sq + lax.ppermute(sq, 'head', [(i, i ^ 1) for i in range(heads)])  1.99 us
    ppermute x1, starting transfers between devices, shards(): halo = lax.ppermute(tail, 'seq', [(i, i + 1) for i in range(peers - 1)])  1.92 us
  transfers between devices with their start and end apart: 8, of which 2 were waited for; matrix products, arithmetic and copies ran while one was open for 0% of the time, Pallas kernels for 29%

profile of v1, /device:TPU:0, one launch (start us, length us, event | category | flops | bytes accessed | tf_op | source)
XLA Modules:
  0.0 82.5 jit_solution(14800042112938891154)
XLA Ops:
  0.0 0.0 copy-start
  0.0 1.2 %copy-done = f32[1024,256]{1,0:T(8,128)S(1)} copy-done((f32[1024,256]{1,0:T(8,128)S(1)}, f32[1024,256]{1,0:T(8,128)}, u32[]{:S(2)}) %copy-start) | copy-done | bytes 1048600
  1.2 0.0 copy-start.3
  1.2 1.2 %copy-done.3 = f32[1024,256]{1,0:T(8,128)S(1)} copy-done((f32[1024,256]{1,0:T(8,128)S(1)}, f32[1024,256]{1,0:T(8,128)}, u32[]{:S(2)}) %copy-start.3) | copy-done | bytes 1048600
  2.5 0.9 %local_states.1 = (f32[2,8,128,128]{3,2,1,0:T(8,128)S(1)}, f32[2,128,128]{2,1,0:T(8,128)S(1)}) custom-call(f32[1024,256]{1,0:T(8,128)S(1)} %copy-done, f32[1024,256]{1,0:T(8,128)S(1)} %copy-done.3), custom_call_target="tpu_custom_call" | custom-call | tf_op jit(solution)/shard_map/local_states/pallas_call | solution.py:66
  3.3 1.3 %collective-permute-start = (f32[2,128,128]{2,1,0:T(8,128)S(1)}, f32[2,128,128]{2,1,0:T(8,128)S(1)}, u32[]{:S(2)}, u32[]{:S(2)}) collective-permute-start(f32[2,128,128]{2,1,0:T(8,128)S(1)} %get-tuple-element.60.refs_12_), channel_id=1, source_target_pairs={{0,4},{4,8},{8,12},{12,16},{16,20},{20,24},{24,28},{28,32},{32,36}... | collective-permute-start | bytes 393224 | tf_op jit(solution)/shard_map/ppermute | solution.py:320
  4.6 0.0 copy-start.1
  4.7 1.2 %copy-done.1 = f32[1024,256]{1,0:T(8,128)S(1)} copy-done((f32[1024,256]{1,0:T(8,128)S(1)}, f32[1024,256]{1,0:T(8,128)}, u32[]{:S(2)}) %copy-start.1) | copy-done | bytes 1048600
  5.9 0.0 copy-start.4
  5.9 1.2 %copy-done.4 = f32[1024,256]{1,0:T(8,128)S(1)} copy-done((f32[1024,256]{1,0:T(8,128)S(1)}, f32[1024,256]{1,0:T(8,128)}, u32[]{:S(2)}) %copy-start.4) | copy-done | bytes 1048600
  7.1 0.0 copy-start.5
  7.1 3.3 %blocks_1_1.1 = (f32[128,2048]{1,0:T(8,128)S(1)}, f32[128,2048]{1,0:T(8,128)S(1)}, bf16[16,128,256]{2,1,0:T(8,128)(2,1)S(1)}) custom-call(f32[1024,2048]{1,0:T(8,128)} %refs_0_.4, f32[1024,256]{1,0:T(8,128)S(1)} %copy-done.1, f32[1024,256]{1,0:T(8,128)S(1)} %copy-done.4, f32[1024,256]{1,0:T(8,128)S(1)} %copy-done.1, f32[1024,256]{1,0:T(8,128)S(1)} %copy-done.4), custom_call_target="tpu_custom_call" | custom-call | tf_op jit(solution)/shard_map/blocks_1_1/pallas_call | solution.py:169
  10.4 0.0 collective-permute-done
  10.5 4.1 %collective-permute-start.1 = (f32[2,128,128]{2,1,0:T(8,128)S(1)}, f32[2,128,128]{2,1,0:T(8,128)S(1)}, u32[]{:S(2)}, u32[]{:S(2)}) collective-permute-start(f32[2,128,128]{2,1,0:T(8,128)S(1)} %add.18), channel_id=1, source_target_pairs={{0,8},{4,12},{8,16},{12,20},{16,24},{20,28},{24,32},{28,36},{32,40... | collective-permute-start | bytes 393224 | tf_op jit(solution)/shard_map/ppermute | solution.py:320
  14.6 0.0 copy-done.5
  14.6 0.0 slice-start
  14.6 0.0 slice-start.1
  14.7 3.3 %blocks_2_1.1 = (f32[128,2048]{1,0:T(8,128)S(1)}, f32[128,2048]{1,0:T(8,128)S(1)}, bf16[16,128,256]{2,1,0:T(8,128)(2,1)S(1)}) custom-call(f32[1024,2048]{1,0:T(8,128)} %refs_0_.4, f32[1024,256]{1,0:T(8,128)S(1)} %copy-done.1, f32[1024,256]{1,0:T(8,128)S(1)} %copy-done.5, f32[1024,256]{1,0:T(8,128)S(1)} %copy-done.1, f32[1024,256]{1,0:T(8,128)S(1)} %copy-done.5), custom_call_target="tpu_custom_call" | custom-call | tf_op jit(solution)/shard_map/blocks_2_1/pallas_call | solution.py:169
  18.0 0.0 collective-permute-done.1
  18.0 6.1 %collective-permute-start.2 = (f32[2,128,128]{2,1,0:T(8,128)S(1)}, f32[2,128,128]{2,1,0:T(8,128)S(1)}, u32[]{:S(2)}, u32[]{:S(2)}) collective-permute-start(f32[2,128,128]{2,1,0:T(8,128)S(1)} %add.19), channel_id=1, source_target_pairs={{0,16},{4,20},{8,24},{12,28},{16,32},{20,36},{24,40},{28,44},{32,4... | collective-permute-start | bytes 393224 | tf_op jit(solution)/shard_map/ppermute | solution.py:320
  24.1 0.0 slice-done
  24.1 0.0 slice-done.1
  24.2 0.0 copy-start.2
  24.2 1.9 %collective-permute-start.4 = (f32[128,512]{1,0:T(8,128)S(1)}, f32[128,512]{1,0:T(8,128)S(1)}, u32[]{:S(2)}, u32[]{:S(2)}) collective-permute-start(f32[128,512]{1,0:T(8,128)S(1)} %pad_maximum_fusion), channel_id=1, source_target_pairs={{0,4},{4,8},{8,12},{12,16},{16,20},{20,24},{24,28},{28,32},{32,36}... | collective-permute-start | bytes 786440 | tf_op jit(solution)/shard_map/ppermute | solution.py:316
  26.1 3.3 %blocks_3_1.1 = (f32[128,2048]{1,0:T(8,128)S(1)}, f32[128,2048]{1,0:T(8,128)S(1)}, bf16[16,128,256]{2,1,0:T(8,128)(2,1)S(1)}) custom-call(f32[1024,2048]{1,0:T(8,128)} %refs_0_.4, f32[1024,256]{1,0:T(8,128)S(1)} %copy-done.1, f32[1024,256]{1,0:T(8,128)S(1)} %copy-done.5, f32[1024,256]{1,0:T(8,128)S(1)} %copy-done.1, f32[1024,256]{1,0:T(8,128)S(1)} %copy-done.5), custom_call_target="tpu_custom_call" | custom-call | tf_op jit(solution)/shard_map/blocks_3_1/pallas_call | solution.py:169
  29.4 0.0 collective-permute-done.2
  29.4 6.8 %collective-permute-start.3 = (f32[2,128,128]{2,1,0:T(8,128)S(1)}, f32[2,128,128]{2,1,0:T(8,128)S(1)}, u32[]{:S(2)}, u32[]{:S(2)}) collective-permute-start(f32[2,128,128]{2,1,0:T(8,128)S(1)} %add.20), channel_id=1, source_target_pairs={{0,32},{4,36},{8,40},{12,44},{16,48},{20,52},{24,56},{28,60},{32,6... | collective-permute-start | bytes 393224 | tf_op jit(solution)/shard_map/ppermute | solution.py:320
  36.2 0.0 copy-done.2
  36.2 5.9 %blocks_4_2.1 = (f32[256,2048]{1,0:T(8,128)S(1)}, f32[256,2048]{1,0:T(8,128)S(1)}, bf16[16,256,256]{2,1,0:T(8,128)(2,1)S(1)}) custom-call(f32[1024,2048]{1,0:T(8,128)} %refs_0_.4, f32[1024,256]{1,0:T(8,128)S(1)} %copy-done.2, f32[1024,256]{1,0:T(8,128)S(1)} %copy-done.5, f32[1024,256]{1,0:T(8,128)S(1)} %copy-done.2, f32[1024,256]{1,0:T(8,128)S(1)} %copy-done.5), custom_call_target="tpu_custom_call" | custom-call | tf_op jit(solution)/shard_map/blocks_4_2/pallas_call | solution.py:169
  42.1 0.0 collective-permute-done.3
  42.2 4.8 %collective-permute-start.5 = (f32[2,128,128]{2,1,0:T(8,128)S(1)}, f32[2,128,128]{2,1,0:T(8,128)S(1)}, u32[]{:S(2)}, u32[]{:S(2)}) collective-permute-start(f32[2,128,128]{2,1,0:T(8,128)S(1)} %add.21), channel_id=1, source_target_pairs={{0,64},{4,68},{8,72},{12,76},{16,80},{20,84},{24,88},{28,92},{32,9... | collective-permute-start | bytes 393224 | tf_op jit(solution)/shard_map/ppermute | solution.py:320
  47.0 0.0 collective-permute-done.4
  47.0 8.4 %blocks_6_3.1 = (f32[384,2048]{1,0:T(8,128)S(1)}, f32[384,2048]{1,0:T(8,128)S(1)}, bf16[16,384,256]{2,1,0:T(8,128)(2,1)S(1)}) custom-call(f32[1024,2048]{1,0:T(8,128)} %refs_0_.4, f32[1024,256]{1,0:T(8,128)S(1)} %copy-done.2, f32[1024,256]{1,0:T(8,128)S(1)} %copy-done.5, f32[1024,256]{1,0:T(8,128)S(1)} %copy-done.2, f32[1024,256]{1,0:T(8,128)S(1)} %copy-done.5, ...), custom_call_target="tpu_custom_call" | custom-call | tf_op jit(solution)/shard_map/blocks_6_3/pallas_call | solution.py:169
  55.4 0.0 collective-permute-done.5
  55.5 0.0 copy-start.6
  55.5 12.3 %linear.1 = (f32[1024,2048]{1,0:T(8,128)S(1)}, f32[8,1,128]{2,1,0:T(1,128)S(1)}) custom-call(bf16[16,128,256]{2,1,0:T(8,128)(2,1)S(1)} %get-tuple-element.88.refs_0_, bf16[16,128,256]{2,1,0:T(8,128)(2,1)S(1)} %get-tuple-element.89.refs_1_, bf16[16,128,256]{2,1,0:T(8,128)(2,1)S(1)} %get-tuple-element.90.refs_2_, ...), custom_call_target="tpu_custom_call" | custom-call | tf_op jit(solution)/shard_map/linear/pallas_call | solution.py:245
  67.8 2.0 %collective-permute-start.6 = (f32[8,1,128]{2,1,0:T(1,128)S(1)}, f32[8,1,128]{2,1,0:T(1,128)S(1)}, u32[]{:S(2)}, u32[]{:S(2)}) collective-permute-start(f32[8,1,128]{2,1,0:T(1,128)S(1)} %get-tuple-element.102), channel_id=1, source_target_pairs={{0,1},{1,0},{2,3},{3,2},{4,5},{5,4},{6,7},{7,6},{8,9},{9,8},{10,11... | collective-permute-start | bytes 12296 | tf_op jit(solution)/shard_map/ppermute | solution.py:338
  69.8 1.7 %collective-permute-done.6 = f32[8,1,128]{2,1,0:T(1,128)S(1)} collective-permute-done((f32[8,1,128]{2,1,0:T(1,128)S(1)}, f32[8,1,128]{2,1,0:T(1,128)S(1)}, u32[]{:S(2)}, u32[]{:S(2)}) %collective-permute-start.6) | collective-permute-done | bytes 4128 | tf_op jit(solution)/shard_map/ppermute | solution.py:338
  71.5 3.9 %collective-permute-start.7 = (f32[8,1,128]{2,1,0:T(1,128)S(1)}, f32[8,1,128]{2,1,0:T(1,128)S(1)}, u32[]{:S(2)}, u32[]{:S(2)}) collective-permute-start(f32[8,1,128]{2,1,0:T(1,128)S(1)} %add.23.refs_6_), channel_id=1, source_target_pairs={{0,2},{1,3},{2,0},{3,1},{4,6},{5,7},{6,4},{7,5},{8,10},{9,11},{10,... | collective-permute-start | bytes 12296 | tf_op jit(solution)/shard_map/ppermute | solution.py:339
  75.4 1.6 %collective-permute-done.7.refs_7_ = f32[8,1,128]{2,1,0:T(1,128)S(1)} collective-permute-done((f32[8,1,128]{2,1,0:T(1,128)S(1)}, f32[8,1,128]{2,1,0:T(1,128)S(1)}, u32[]{:S(2)}, u32[]{:S(2)}) %collective-permute-start.7) | collective-permute-done | bytes 4128 | tf_op jit(solution)/shard_map/ppermute | solution.py:339
  77.0 0.0 copy-done.6
  77.0 5.5 %combine.1 = f32[1024,2048]{1,0:T(8,128)} custom-call(f32[128,2048]{1,0:T(8,128)S(1)} %get-tuple-element.59.refs_0_, f32[128,2048]{1,0:T(8,128)S(1)} %get-tuple-element.66.refs_1_, f32[128,2048]{1,0:T(8,128)S(1)} %get-tuple-element.73.refs_2_, f32[256,2048]{1,0:T(8,128)S(1)} %get-tuple-element.80.refs_3_, f32[384,2048]{1,0:T(8,128)S(1)} %get-tuple-element.87.refs_4_, ...), custom_call_target="tpu_custom_call" | custom-call | tf_op jit(solution)/shard_map/combine/pallas_call | solution.py:296
  (8 shorter events, 0.1 us)
Async XLA Ops:
  0.0 1.2 %copy-start = (f32[1024,256]{1,0:T(8,128)S(1)}, f32[1024,256]{1,0:T(8,128)}, u32[]{:S(2)}) copy-start(f32[1024,256]{1,0:T(8,128)} %refs_3_.9) | copy-start | bytes 3145732
  1.2 1.2 %copy-start.3 = (f32[1024,256]{1,0:T(8,128)S(1)}, f32[1024,256]{1,0:T(8,128)}, u32[]{:S(2)}) copy-start(f32[1024,256]{1,0:T(8,128)} %refs_4_.9) | copy-start | bytes 3145732
  3.3 7.1 %collective-permute-start = (f32[2,128,128]{2,1,0:T(8,128)S(1)}, f32[2,128,128]{2,1,0:T(8,128)S(1)}, u32[]{:S(2)}, u32[]{:S(2)}) collective-permute-start(f32[2,128,128]{2,1,0:T(8,128)S(1)} %get-tuple-element.60.refs_12_), channel_id=1, source_target_pairs={{0,4},{4,8},{8,12},{12,16},{16,20},{20,24},{24,28},{28,32},{32,36}... | collective-permute-start | bytes 393224 | tf_op jit(solution)/shard_map/ppermute | solution.py:320
  4.6 1.2 %copy-start.1 = (f32[1024,256]{1,0:T(8,128)S(1)}, f32[1024,256]{1,0:T(8,128)}, u32[]{:S(2)}) copy-start(f32[1024,256]{1,0:T(8,128)} %refs_3_.9) | copy-start | bytes 3145732
  5.9 1.2 %copy-start.4 = (f32[1024,256]{1,0:T(8,128)S(1)}, f32[1024,256]{1,0:T(8,128)}, u32[]{:S(2)}) copy-start(f32[1024,256]{1,0:T(8,128)} %refs_4_.9) | copy-start | bytes 3145732
  7.1 7.5 %copy-start.5 = (f32[1024,256]{1,0:T(8,128)S(1)}, f32[1024,256]{1,0:T(8,128)}, u32[]{:S(2)}) copy-start(f32[1024,256]{1,0:T(8,128)} %refs_4_.9) | copy-start | bytes 3145732
  10.5 7.5 %collective-permute-start.1 = (f32[2,128,128]{2,1,0:T(8,128)S(1)}, f32[2,128,128]{2,1,0:T(8,128)S(1)}, u32[]{:S(2)}, u32[]{:S(2)}) collective-permute-start(f32[2,128,128]{2,1,0:T(8,128)S(1)} %add.18), channel_id=1, source_target_pairs={{0,8},{4,12},{8,16},{12,20},{16,24},{20,28},{24,32},{28,36},{32,40... | collective-permute-start | bytes 393224 | tf_op jit(solution)/shard_map/ppermute | solution.py:320
  14.6 9.5 %slice-start = ((f32[1024,256]{1,0:T(8,128)}), f32[128,256]{1,0:T(8,128)S(1)}, s32[]{:S(2)}) async-start(f32[1024,256]{1,0:T(8,128)} %refs_3_.9), calls=%async_computation | async-start | bytes 262144 | tf_op jit(solution)/shard_map/slice | solution.py:315
  14.6 9.5 %slice-start.1 = ((f32[1024,256]{1,0:T(8,128)}), f32[128,256]{1,0:T(8,128)S(1)}, s32[]{:S(2)}) async-start(f32[1024,256]{1,0:T(8,128)} %refs_4_.9), calls=%async_computation.1 | async-start | bytes 262144 | tf_op jit(solution)/shard_map/slice | solution.py:315
  18.0 11.3 %collective-permute-start.2 = (f32[2,128,128]{2,1,0:T(8,128)S(1)}, f32[2,128,128]{2,1,0:T(8,128)S(1)}, u32[]{:S(2)}, u32[]{:S(2)}) collective-permute-start(f32[2,128,128]{2,1,0:T(8,128)S(1)} %add.19), channel_id=1, source_target_pairs={{0,16},{4,20},{8,24},{12,28},{16,32},{20,36},{24,40},{28,44},{32,4... | collective-permute-start | bytes 393224 | tf_op jit(solution)/shard_map/ppermute | solution.py:320
  24.2 12.1 %copy-start.2 = (f32[1024,256]{1,0:T(8,128)S(1)}, f32[1024,256]{1,0:T(8,128)}, u32[]{:S(2)}) copy-start(f32[1024,256]{1,0:T(8,128)} %refs_3_.9) | copy-start | bytes 3145732
  24.2 22.8 %collective-permute-start.4 = (f32[128,512]{1,0:T(8,128)S(1)}, f32[128,512]{1,0:T(8,128)S(1)}, u32[]{:S(2)}, u32[]{:S(2)}) collective-permute-start(f32[128,512]{1,0:T(8,128)S(1)} %pad_maximum_fusion), channel_id=1, source_target_pairs={{0,4},{4,8},{8,12},{12,16},{16,20},{20,24},{24,28},{28,32},{32,36}... | collective-permute-start | bytes 786440 | tf_op jit(solution)/shard_map/ppermute | solution.py:316
  29.4 12.7 %collective-permute-start.3 = (f32[2,128,128]{2,1,0:T(8,128)S(1)}, f32[2,128,128]{2,1,0:T(8,128)S(1)}, u32[]{:S(2)}, u32[]{:S(2)}) collective-permute-start(f32[2,128,128]{2,1,0:T(8,128)S(1)} %add.20), channel_id=1, source_target_pairs={{0,32},{4,36},{8,40},{12,44},{16,48},{20,52},{24,56},{28,60},{32,6... | collective-permute-start | bytes 393224 | tf_op jit(solution)/shard_map/ppermute | solution.py:320
  42.2 13.3 %collective-permute-start.5 = (f32[2,128,128]{2,1,0:T(8,128)S(1)}, f32[2,128,128]{2,1,0:T(8,128)S(1)}, u32[]{:S(2)}, u32[]{:S(2)}) collective-permute-start(f32[2,128,128]{2,1,0:T(8,128)S(1)} %add.21), channel_id=1, source_target_pairs={{0,64},{4,68},{8,72},{12,76},{16,80},{20,84},{24,88},{28,92},{32,9... | collective-permute-start | bytes 393224 | tf_op jit(solution)/shard_map/ppermute | solution.py:320
  55.5 21.5 %copy-start.6 = (f32[2048]{0:T(1024)S(1)}, f32[2048]{0:T(1024)}, u32[]{:S(2)}) copy-start(f32[2048]{0:T(1024)} %param.7) | copy-start | bytes 24580
  67.8 3.7 %collective-permute-start.6 = (f32[8,1,128]{2,1,0:T(1,128)S(1)}, f32[8,1,128]{2,1,0:T(1,128)S(1)}, u32[]{:S(2)}, u32[]{:S(2)}) collective-permute-start(f32[8,1,128]{2,1,0:T(1,128)S(1)} %get-tuple-element.102), channel_id=1, source_target_pairs={{0,1},{1,0},{2,3},{3,2},{4,5},{5,4},{6,7},{7,6},{8,9},{9,8},{10,11... | collective-permute-start | bytes 12296 | tf_op jit(solution)/shard_map/ppermute | solution.py:338
  71.5 5.5 %collective-permute-start.7 = (f32[8,1,128]{2,1,0:T(1,128)S(1)}, f32[8,1,128]{2,1,0:T(1,128)S(1)}, u32[]{:S(2)}, u32[]{:S(2)}) collective-permute-start(f32[8,1,128]{2,1,0:T(1,128)S(1)} %add.23.refs_6_), channel_id=1, source_target_pairs={{0,2},{1,3},{2,0},{3,1},{4,6},{5,7},{6,4},{7,5},{8,10},{9,11},{10,... | collective-permute-start | bytes 12296 | tf_op jit(solution)/shard_map/ppermute | solution.py:339

commit v2 on v0

v2 whole, which is shorter than its diff:
```python
import math

import jax
import jax.numpy as jnp
from jax import lax
from jax.experimental import pallas as pl
from jax.experimental.pallas import tpu as pltpu
from jax.sharding import PartitionSpec as P

QUERY_HEADS = 64
KEY_VALUE_HEADS = 8
D = 128
G = QUERY_HEADS // KEY_VALUE_HEADS
BLOCK = 128
EPS = 1e-6
SCORE_SCALE = math.log2(math.e) / math.sqrt(D)

f32 = jnp.float32
bf = jnp.bfloat16
NT = (((1,), (1,)), ((), ()))
TN = (((0,), (0,)), ((), ()))


def split(x):
    hi = x.astype(bf)
    return hi, (x - hi.astype(f32)).astype(bf)


def lanes(*xs):
    return jnp.concatenate(xs, axis=1)


def rows(*xs):
    return jnp.concatenate(xs, axis=0)


def dot(a, b, dims=(((1,), (0,)), ((), ()))):
    return lax.dot_general(a, b, dims, preferred_element_type=f32)


def halves(x):
    return x[:, :D] + x[:, D:]


def params(mib):
    return pltpu.CompilerParams(
        vmem_limit_bytes=mib << 20, dimension_semantics=("arbitrary",)
    )


def state_body(k_ref, v_ref, before_ref, pack_ref):
    count = k_ref.shape[0]
    state = jnp.zeros((D, D), f32)
    for b in range(count // BLOCK):
        at = slice(b * BLOCK, (b + 1) * BLOCK)
        before_ref[b] = state
        fh, fl = split(jnp.tanh(k_ref[at, :]))
        vh, vl = split(v_ref[at, :])
        vv = lanes(vh, vl)
        state = state + halves(dot(rows(fh, fl), rows(vv, vv), TN))
    pack_ref[:D] = state
    pack_ref[D : D + BLOCK] = k_ref[count - BLOCK :, :]
    pack_ref[D + BLOCK :] = v_ref[count - BLOCK :, :]


def local_states(keys, values):
    count, width = keys.shape
    kv, nb = width // D, count // BLOCK
    one = pl.Squeezed()
    return pl.pallas_call(
        state_body,
        grid=(kv,),
        in_specs=[pl.BlockSpec((count, D), lambda g: (0, g))] * 2,
        out_specs=[
            pl.BlockSpec((one, nb, D, D), lambda g: (g, 0, 0, 0)),
            pl.BlockSpec((one, D + 2 * BLOCK, D), lambda g: (g, 0, 0)),
        ],
        out_shape=[
            jax.ShapeDtypeStruct((kv, nb, D, D), f32),
            jax.ShapeDtypeStruct((kv, D + 2 * BLOCK, D), f32),
        ],
        compiler_params=params(8),
        name="local_states",
    )(keys, values)


def block_body(wrap, carried, *refs):
    q_ref, k_ref, v_ref, kp_ref, vp_ref, *refs = refs
    if wrap is not None:
        halo_ref, *refs = refs
    win_ref, lin_ref, fq_ref, kh, kl, vv = refs[carried:]
    kv = k_ref.shape[1] // D
    b = pl.program_id(0)
    here = slice(0, BLOCK)
    there = slice(BLOCK, 2 * BLOCK)

    def prepare(g, k, v, at):
        h, l = split(k * SCORE_SCALE)
        kh[g, at, :] = lanes(h, h)
        kl[g, at, :] = lanes(l, l)
        vv[g, at, :] = lanes(*split(v))

    @pl.when(b == 0)
    def _():
        for g in range(kv):
            head = slice(g * D, (g + 1) * D)
            prepare(g, kp_ref[:, head], vp_ref[:, head], there)

    @pl.when(b > 0)
    def _():
        for x in (kh, kl, vv):
            x[:, there, :] = x[:, here, :]

    if wrap is not None:

        @pl.when(b == wrap)
        def _():
            for g in range(kv):
                prepare(g, halo_ref[g, D : D + BLOCK], halo_ref[g, D + BLOCK :], there)

    row = lax.broadcasted_iota(jnp.int32, (BLOCK, BLOCK), 0)
    col = lax.broadcasted_iota(jnp.int32, (BLOCK, BLOCK), 1)
    own = rows(*[row >= col] * G)
    zero = jnp.zeros((BLOCK * G, BLOCK), bf)
    for g in range(kv):
        head = slice(g * D, (g + 1) * D)
        k = k_ref[:, head]
        prepare(g, k, v_ref[:, head], here)
        fh, fl = split(jnp.tanh(k))
        ff = rows(lanes(fh, fh), lanes(fl, fl))
        kk = lanes(kh[g], kl[g])
        v_both = vv[g]
        v_own = vv[g, here, :]
        heads = [slice(i * D, (i + 1) * D) for i in range(g * G, (g + 1) * G)]
        q = rows(*[q_ref[:, at] for at in heads])
        qh, ql = split(q)
        s = dot(lanes(qh, ql, qh, ql), kk, NT)
        f2 = lanes(*split(jnp.tanh(q)))
        fq_ref[0, g * G * BLOCK : (g + 1) * G * BLOCK, :] = f2
        a = jnp.where(own, halves(dot(f2, ff, NT)), 0.0)
        lin = halves(dot(lanes(*split(a)), rows(v_own, v_own)))
        before = s[:, BLOCK:]
        if wrap is not None:
            before = jnp.where((lax.axis_index("seq") > 0) | (b != wrap), before, -1e30)
        t = jnp.where(own, s[:, :BLOCK], before)
        p = jnp.exp2(t - jnp.max(t, axis=1, keepdims=True))
        total = jnp.sum(p, axis=1, keepdims=True)
        ph, pl_ = split(p)
        p4 = lanes(
            jnp.where(own, ph, zero),
            jnp.where(own, zero, ph),
            jnp.where(own, pl_, zero),
            jnp.where(own, zero, pl_),
        )
        win = halves(dot(p4, rows(v_both, v_both))) * (1.0 / total)
        for i, at in enumerate(heads):
            win_ref[:, at] = win[i * BLOCK : (i + 1) * BLOCK]
            lin_ref[:, at] = lin[i * BLOCK : (i + 1) * BLOCK]


def block_part(queries, keys, values, first, n, made, halo=None):
    count, width = queries.shape
    kv = keys.shape[1] // D
    nb = count // BLOCK
    own = lambda b: ((first + b) % nb, 0)
    prior = lambda b: (first - 1, 0)
    small = lambda index: pl.BlockSpec((BLOCK, kv * D), index)
    args = [queries, keys, values, keys, values]
    specs = [pl.BlockSpec((BLOCK, width), own), small(own), small(own), small(prior), small(prior)]
    wrap = None
    if halo is not None:
        wrap = nb - first
        args.append(halo)
        specs.append(pl.BlockSpec(halo.shape, lambda b: (0, 0, 0)))
    aliases = {len(args) + i: i for i in range(len(made))}
    big = pl.BlockSpec((BLOCK, width), own)
    return pl.pallas_call(
        lambda *refs: block_body(wrap, len(made), *refs),
        grid=(n,),
        in_specs=specs + [pl.BlockSpec(memory_space=pl.ANY)] * len(made),
        out_specs=[
            big,
            big,
            pl.BlockSpec((1, kv * G * BLOCK, 2 * D), lambda b: ((first + b) % nb, 0, 0)),
        ],
        out_shape=[
            pltpu.VMEM((count, width), f32),
            pltpu.VMEM((count, width), f32),
            pltpu.VMEM((nb, kv * G * BLOCK, 2 * D), bf),
        ],
        scratch_shapes=[pltpu.VMEM((kv, 2 * BLOCK, 2 * D), bf)] * 3,
        input_output_aliases=aliases,
        compiler_params=params(12),
        name=f"blocks_{first}_{n}",
    )(*args, *made)


def linear_body(fq_ref, part_ref, before_ref, incl_ref, pack_ref, lin_ref, sq_ref):
    sq = jnp.zeros((BLOCK, D), f32)
    for g in range(incl_ref.shape[0]):
        ss = lanes(*split((incl_ref[g] - pack_ref[g]) + before_ref[g, 0]))
        fq = fq_ref[0, g * G * BLOCK : (g + 1) * G * BLOCK, :]
        lin = halves(dot(fq, rows(ss, ss)))
        for i in range(G):
            at = slice((g * G + i) * D, (g * G + i + 1) * D)
            x = lin[i * BLOCK : (i + 1) * BLOCK] + part_ref[:, at]
            lin_ref[:, at] = x
            sq = sq + x * x
    sq_ref[0] = jnp.sum(sq.T, axis=0, keepdims=True)


def linear_part(fq, part, before, incl, pack):
    count, width = part.shape
    kv, nb = before.shape[:2]
    big = pl.BlockSpec((BLOCK, width), lambda b: (b, 0))
    return pl.pallas_call(
        linear_body,
        grid=(nb,),
        in_specs=[
            pl.BlockSpec((1,) + fq.shape[1:], lambda b: (b, 0, 0)),
            big,
            pl.BlockSpec((kv, 1, D, D), lambda b: (0, b, 0, 0)),
            pl.BlockSpec((kv, D, D), lambda b: (0, 0, 0)),
            pl.BlockSpec((kv, D, D), lambda b: (0, 0, 0)),
        ],
        out_specs=[big, pl.BlockSpec((1, 1, BLOCK), lambda b: (b, 0, 0))],
        out_shape=[
            pltpu.VMEM((count, width), f32),
            pltpu.VMEM((nb, 1, BLOCK), f32),
        ],
        compiler_params=params(8),
        name="linear",
    )(fq, part, before, incl, pack)


def combine_body(lin_ref, win_ref, sa_ref, sb_ref, gain_ref, out_ref):
    for r in range(lin_ref.shape[0] // BLOCK):
        ms = (sa_ref[r] + sb_ref[r]) * (1.0 / (QUERY_HEADS * D))
        inv = jnp.broadcast_to(lax.rsqrt(ms + EPS), (BLOCK, BLOCK)).T
        row = slice(r * BLOCK, (r + 1) * BLOCK)
        for i in range(lin_ref.shape[1] // D):
            at = slice(i * D, (i + 1) * D)
            out_ref[row, at] = lin_ref[row, at] * inv * gain_ref[:, at] + win_ref[row, at]


def combine(lin, win, sa, sb, gain):
    count, width = lin.shape
    n = 2
    big = pl.BlockSpec((n * BLOCK, width), lambda j: (j, 0))
    small = pl.BlockSpec((n, 1, BLOCK), lambda j: (j, 0, 0))
    return pl.pallas_call(
        combine_body,
        grid=(count // (n * BLOCK),),
        in_specs=[big, big, small, small, pl.BlockSpec((1, width), lambda j: (0, 0))],
        out_specs=big,
        out_shape=jax.ShapeDtypeStruct((count, width), f32),
        compiler_params=params(8),
        name="combine",
    )(lin, win, sa, sb, gain)


def shards(queries, keys, values, gain):
    count = queries.shape[0]
    nb = count // BLOCK
    peers = lax.axis_size("seq")
    heads = lax.axis_size("head")
    assert heads == 4 and nb == 8 and peers == 32
    queries, keys, values = (
        pltpu.with_memory_space_constraint(x, pltpu.HBM) for x in (queries, keys, values)
    )

    def behind(x, by):
        return lax.ppermute(x, "seq", [(i, i + by) for i in range(peers - by)])

    before, pack = local_states(keys, values)
    incl = pack
    made = []
    halo = None
    for number, (first, n) in enumerate([(1, 2), (3, 1), (4, 1), (5, 1), (6, 3)]):
        got = behind(incl, 1 << number)
        if made:
            *made, incl = lax.optimization_barrier((*made, incl))
        made = block_part(
            queries, keys, values, first, n, made, halo if first + n > nb else None
        )
        *made, got = lax.optimization_barrier((*made, got))
        if number == 0:
            halo = got
        incl = incl[:, :D] + got[:, :D]
    win, part, fq = made
    lin, sq = linear_part(fq, part, before, incl, pack)
    sq = sq + lax.ppermute(sq, "head", [(i, i ^ 1) for i in range(heads)])
    other = lax.ppermute(sq, "head", [(i, i ^ 2) for i in range(heads)])
    return combine(lin, win, sq, other, gain[None, :])


def solution(mesh):
    in_specs = (P("seq", "head"), P("seq", "head"), P("seq", "head"), P("head"))
    return jax.shard_map(
        shards, mesh=mesh, in_specs=in_specs, out_specs=P("seq", "head"), check_vma=False
    )
```

time: 276 us -> 69.7 us (0.25)
  matrix products: 123 us -> 0 us
  local copies, waits for them, and re-layouts: 70.7 us -> 0.01 us
  Pallas kernels: 0 us -> 34.3 us
  starting transfers between devices: 5.54 us -> 31.5 us
  other arithmetic: 25.1 us -> 0.09 us
  waiting for transfers between devices: 18.6 us -> 3.29 us
  between operations: 13.5 us -> 0.18 us
  blocking collectives: 10.6 us -> 0 us
  loops' own time: 5.97 us -> 0 us
    dot_general x49 -> x0, matrix products: 123 us -> none  [the longest x8 27.4 us: advance(): jnp.einsum('cmop,nmp->mocn', query_block, key_block, precision=HIGH_ACCUR...]
    pallas_call x0 -> x8, Pallas kernels: none -> 34.3 us  [the longest x5 23.8 us: block_part(): pl.pallas_call(lambda *refs: block_body(wrap, len(made), *refs), grid=(n,...]
    ppermute x2 -> x7, starting transfers between devices: 5.54 us -> 31.5 us  [the longest x5 25.6 us: behind(): return lax.ppermute(x, 'seq', [(i, i + by) for i in range(peers - by)])]
    all_gather x1 -> x0, waiting for transfers between devices: 18.6 us -> none  [shards(): piece = lax.all_gather(own_state[None], 'seq', axis=0, tiled=True)]
    reshape x2 -> x0, local copies, waits for them, and re-layouts: 18.5 us -> none  [the longest x1 9.29 us: shards(): linear_branch = linear_branch.reshape(count, queries.shape[1])]
    unnamed x5 -> x2, local copies, waits for them, and re-layouts: 13.4 us -> 0.01 us
    dynamic_update_slice x16 -> x0, local copies, waits for them, and re-layouts: 12.6 us -> none  [shards(): _, (linear_branch, window_length) = lax.scan(advance, prior, numbers)]
    reduce_sum x10 -> x0, other arithmetic: 11 us -> none  [the longest x1 4.31 us: shards(): squares = jnp.sum(linear_branch * linear_branch, axis=1)]
  transfers between devices with their start and end apart: 3 -> 7, of which waited for: 1 -> 2; matrix products, arithmetic and copies ran while one was open for 9% -> 0% of each run, Pallas kernels for 0% -> 34%
where the time goes in v2:
time: 69.7 us; the launch traced here: 69.3 us
  Pallas kernels  34.3 us (49%)
  starting transfers between devices  31.5 us (45%)
  waiting for transfers between devices  3.29 us (5%)
    ppermute x5, starting transfers between devices, behind(): return lax.ppermute(x, 'seq', [(i, i + by) for i in range(peers - by)])  25.6 us
    pallas_call x5, Pallas kernels, block_part(): pl.pallas_call(lambda *refs: block_body(wrap, len(made), *refs), grid=(n,...  23.8 us
    pallas_call x1, Pallas kernels, linear_part(): pl.pallas_call(linear_body, grid=(nb,), in_specs=[pl.BlockSpec((1,) + fq....  4.54 us
    pallas_call x1, Pallas kernels, combine(): pl.pallas_call(combine_body, grid=(count // (n * BLOCK),), in_specs=[big,...  3.98 us
    ppermute x1, starting transfers between devices, shards(): other = lax.ppermute(sq, 'head', [(i, i ^ 2) for i in range(heads)])  3.88 us
    ppermute x1, starting transfers between devices, shards(): sq = sq + lax.ppermute(sq, 'head', [(i, i ^ 1) for i in range(heads)])  1.99 us
    pallas_call x1, Pallas kernels, local_states(): pl.pallas_call(state_body, grid=(kv,), in_specs=[pl.BlockSpec((count, D),...  1.93 us
    ppermute x1, waiting for transfers between devices, shards(): sq = sq + lax.ppermute(sq, 'head', [(i, i ^ 1) for i in range(heads)])  1.7 us
  transfers between devices with their start and end apart: 7, of which 2 were waited for; matrix products, arithmetic and copies ran while one was open for 0% of the time, Pallas kernels for 34%

profile of v2, /device:TPU:0, one launch (start us, length us, event | category | flops | bytes accessed | tf_op | source)
XLA Modules:
  0.0 69.3 jit_solution(4267450308426564029)
XLA Ops:
  0.0 1.9 %local_states.1 = (f32[2,8,128,128]{3,2,1,0:T(8,128)S(1)}, f32[2,384,128]{2,1,0:T(8,128)S(1)}) custom-call(f32[1024,256]{1,0:T(8,128)} %refs_3_.9, f32[1024,256]{1,0:T(8,128)} %refs_4_.9), custom_call_target="tpu_custom_call" | custom-call | tf_op jit(solution)/shard_map/local_states/pallas_call | solution.py:70
  1.9 1.3 %collective-permute-start = (f32[2,384,128]{2,1,0:T(8,128)S(1)}, f32[2,384,128]{2,1,0:T(8,128)S(1)}, u32[]{:S(2)}, u32[]{:S(2)}) collective-permute-start(f32[2,384,128]{2,1,0:T(8,128)S(1)} %get-tuple-element.63.pack_ref), channel_id=1, source_target_pairs={{0,4},{4,8},{8,12},{12,16},{16,20},{20,24},{24,28},{28,32},{32,36}... | collective-permute-start | bytes 1179656 | tf_op jit(solution)/shard_map/ppermute | solution.py:273
  3.3 5.7 %blocks_1_2.1 = (f32[1024,2048]{1,0:T(8,128)S(1)}, f32[1024,2048]{1,0:T(8,128)S(1)}, bf16[8,2048,256]{2,1,0:T(8,128)(2,1)S(1)}) custom-call(f32[1024,2048]{1,0:T(8,128)} %refs_0_.9, f32[1024,256]{1,0:T(8,128)} %refs_3_.9, f32[1024,256]{1,0:T(8,128)} %refs_4_.9, f32[1024,256]{1,0:T(8,128)} %refs_3_.9, f32[1024,256]{1,0:T(8,128)} %refs_4_.9), custom_call_target="tpu_custom_call" | custom-call | tf_op jit(solution)/shard_map/blocks_1_2/pallas_call | solution.py:177
  8.9 0.0 collective-permute-done.refs_5_
  9.0 5.6 %collective-permute-start.1 = (f32[2,128,128]{2,1,0:T(8,128)S(1)}, f32[2,128,128]{2,1,0:T(8,128)S(1)}, u32[]{:S(2)}, u32[]{:S(2)}) collective-permute-start(f32[2,128,128]{2,1,0:T(8,128)S(1)} %slice_add_fusion), channel_id=1, source_target_pairs={{0,8},{4,12},{8,16},{12,20},{16,24},{20,28},{24,32},{28,36},{32,40... | collective-permute-start | bytes 393224 | tf_op jit(solution)/shard_map/ppermute | solution.py:273
  14.6 3.4 %blocks_3_1.1 = (f32[1024,2048]{1,0:T(8,128)S(1)}, f32[1024,2048]{1,0:T(8,128)S(1)}, bf16[8,2048,256]{2,1,0:T(8,128)(2,1)S(1)}) custom-call(f32[1024,2048]{1,0:T(8,128)} %refs_0_.9, f32[1024,256]{1,0:T(8,128)} %refs_3_.9, f32[1024,256]{1,0:T(8,128)} %refs_4_.9, f32[1024,256]{1,0:T(8,128)} %refs_3_.9, ...), custom_call_target="tpu_custom_call", output_to_operand_aliasing={{0}: (5, {}), {1}: (6, {}), {2}: (7, {})} | custom-call | tf_op jit(solution)/shard_map/blocks_3_1/pallas_call | solution.py:177
  18.0 0.0 collective-permute-done.1
  18.1 5.2 %collective-permute-start.2 = (f32[2,128,128]{2,1,0:T(8,128)S(1)}, f32[2,128,128]{2,1,0:T(8,128)S(1)}, u32[]{:S(2)}, u32[]{:S(2)}) collective-permute-start(f32[2,128,128]{2,1,0:T(8,128)S(1)} %add.19), channel_id=1, source_target_pairs={{0,16},{4,20},{8,24},{12,28},{16,32},{20,36},{24,40},{28,44},{32,4... | collective-permute-start | bytes 393224 | tf_op jit(solution)/shard_map/ppermute | solution.py:273
  23.2 3.4 %blocks_4_1.1 = (f32[1024,2048]{1,0:T(8,128)S(1)}, f32[1024,2048]{1,0:T(8,128)S(1)}, bf16[8,2048,256]{2,1,0:T(8,128)(2,1)S(1)}) custom-call(f32[1024,2048]{1,0:T(8,128)} %refs_0_.9, f32[1024,256]{1,0:T(8,128)} %refs_3_.9, f32[1024,256]{1,0:T(8,128)} %refs_4_.9, f32[1024,256]{1,0:T(8,128)} %refs_3_.9, ...), custom_call_target="tpu_custom_call", output_to_operand_aliasing={{0}: (5, {}), {1}: (6, {}), {2}: (7, {})} | custom-call | tf_op jit(solution)/shard_map/blocks_4_1/pallas_call | solution.py:177
  26.7 0.0 collective-permute-done.2
  26.7 8.3 %collective-permute-start.3 = (f32[2,128,128]{2,1,0:T(8,128)S(1)}, f32[2,128,128]{2,1,0:T(8,128)S(1)}, u32[]{:S(2)}, u32[]{:S(2)}) collective-permute-start(f32[2,128,128]{2,1,0:T(8,128)S(1)} %add.20), channel_id=1, source_target_pairs={{0,32},{4,36},{8,40},{12,44},{16,48},{20,52},{24,56},{28,60},{32,6... | collective-permute-start | bytes 393224 | tf_op jit(solution)/shard_map/ppermute | solution.py:273
  35.0 3.4 %blocks_5_1.1 = (f32[1024,2048]{1,0:T(8,128)S(1)}, f32[1024,2048]{1,0:T(8,128)S(1)}, bf16[8,2048,256]{2,1,0:T(8,128)(2,1)S(1)}) custom-call(f32[1024,2048]{1,0:T(8,128)} %refs_0_.9, f32[1024,256]{1,0:T(8,128)} %refs_3_.9, f32[1024,256]{1,0:T(8,128)} %refs_4_.9, f32[1024,256]{1,0:T(8,128)} %refs_3_.9, ...), custom_call_target="tpu_custom_call", output_to_operand_aliasing={{0}: (5, {}), {1}: (6, {}), {2}: (7, {})} | custom-call | tf_op jit(solution)/shard_map/blocks_5_1/pallas_call | solution.py:177
  38.5 0.0 collective-permute-done.3
  38.5 5.2 %collective-permute-start.4 = (f32[2,128,128]{2,1,0:T(8,128)S(1)}, f32[2,128,128]{2,1,0:T(8,128)S(1)}, u32[]{:S(2)}, u32[]{:S(2)}) collective-permute-start(f32[2,128,128]{2,1,0:T(8,128)S(1)} %add.21), channel_id=1, source_target_pairs={{0,64},{4,68},{8,72},{12,76},{16,80},{20,84},{24,88},{28,92},{32,9... | collective-permute-start | bytes 393224 | tf_op jit(solution)/shard_map/ppermute | solution.py:273
  43.7 7.8 %blocks_6_3.1 = (f32[1024,2048]{1,0:T(8,128)S(1)}, f32[1024,2048]{1,0:T(8,128)S(1)}, bf16[8,2048,256]{2,1,0:T(8,128)(2,1)S(1)}) custom-call(f32[1024,2048]{1,0:T(8,128)} %refs_0_.9, f32[1024,256]{1,0:T(8,128)} %refs_3_.9, f32[1024,256]{1,0:T(8,128)} %refs_4_.9, f32[1024,256]{1,0:T(8,128)} %refs_3_.9, ...), custom_call_target="tpu_custom_call", output_to_operand_aliasing={{0}: (6, {}), {1}: (7, {}), {2}: (8, {})} | custom-call | tf_op jit(solution)/shard_map/blocks_6_3/pallas_call | solution.py:177
  51.6 0.0 collective-permute-done.4
  51.6 0.0 copy-start
  51.6 4.5 %linear.1 = (f32[1024,2048]{1,0:T(8,128)S(1)}, f32[8,1,128]{2,1,0:T(1,128)S(1)}) custom-call(bf16[8,2048,256]{2,1,0:T(8,128)(2,1)S(1)} %get-tuple-element.107.fq_ref, f32[1024,2048]{1,0:T(8,128)S(1)} %get-tuple-element.108.part_ref, f32[2,8,128,128]{3,2,1,0:T(8,128)S(1)} %get-tuple-element.109.before_ref, f32[2,128,128]{2,1,0:T(8,128)S(1)} %add.22.incl_ref, ...), custom_call_target="tpu_custom_call" | custom-call | tf_op jit(solution)/shard_map/linear/pallas_call | solution.py:216
  56.2 2.0 %collective-permute-start.5 = (f32[8,1,128]{2,1,0:T(1,128)S(1)}, f32[8,1,128]{2,1,0:T(1,128)S(1)}, u32[]{:S(2)}, u32[]{:S(2)}) collective-permute-start(f32[8,1,128]{2,1,0:T(1,128)S(1)} %get-tuple-element.114), channel_id=1, source_target_pairs={{0,1},{1,0},{2,3},{3,2},{4,5},{5,4},{6,7},{7,6},{8,9},{9,8},{10,11... | collective-permute-start | bytes 12296 | tf_op jit(solution)/shard_map/ppermute | solution.py:292
  58.2 1.7 %collective-permute-done.5 = f32[8,1,128]{2,1,0:T(1,128)S(1)} collective-permute-done((f32[8,1,128]{2,1,0:T(1,128)S(1)}, f32[8,1,128]{2,1,0:T(1,128)S(1)}, u32[]{:S(2)}, u32[]{:S(2)}) %collective-permute-start.5) | collective-permute-done | bytes 4128 | tf_op jit(solution)/shard_map/ppermute | solution.py:292
  59.9 3.9 %collective-permute-start.6 = (f32[8,1,128]{2,1,0:T(1,128)S(1)}, f32[8,1,128]{2,1,0:T(1,128)S(1)}, u32[]{:S(2)}, u32[]{:S(2)}) collective-permute-start(f32[8,1,128]{2,1,0:T(1,128)S(1)} %add.23.sa_ref), channel_id=1, source_target_pairs={{0,2},{1,3},{2,0},{3,1},{4,6},{5,7},{6,4},{7,5},{8,10},{9,11},{10,... | collective-permute-start | bytes 12296 | tf_op jit(solution)/shard_map/ppermute | solution.py:293
  63.7 1.6 %collective-permute-done.6.sb_ref = f32[8,1,128]{2,1,0:T(1,128)S(1)} collective-permute-done((f32[8,1,128]{2,1,0:T(1,128)S(1)}, f32[8,1,128]{2,1,0:T(1,128)S(1)}, u32[]{:S(2)}, u32[]{:S(2)}) %collective-permute-start.6) | collective-permute-done | bytes 4128 | tf_op jit(solution)/shard_map/ppermute | solution.py:293
  65.3 0.0 copy-done
  65.3 4.0 %combine.1 = f32[1024,2048]{1,0:T(8,128)} custom-call(f32[1024,2048]{1,0:T(8,128)S(1)} %get-tuple-element.112.lin_ref, f32[1024,2048]{1,0:T(8,128)S(1)} %get-tuple-element.113.win_ref, f32[8,1,128]{2,1,0:T(1,128)S(1)} %add.23.sa_ref, f32[8,1,128]{2,1,0:T(1,128)S(1)} %collective-permute-done.6.sb_ref, f32[1,2048]{1,0:T(1,128)S(1)} %bitcast.1), custom_call_target="tpu_custom_call" | custom-call | tf_op jit(solution)/shard_map/combine/pallas_call | solution.py:251
  (6 shorter events, 0.1 us)
Async XLA Ops:
  1.9 7.0 %collective-permute-start = (f32[2,384,128]{2,1,0:T(8,128)S(1)}, f32[2,384,128]{2,1,0:T(8,128)S(1)}, u32[]{:S(2)}, u32[]{:S(2)}) collective-permute-start(f32[2,384,128]{2,1,0:T(8,128)S(1)} %get-tuple-element.63.pack_ref), channel_id=1, source_target_pairs={{0,4},{4,8},{8,12},{12,16},{16,20},{20,24},{24,28},{28,32},{32,36}... | collective-permute-start | bytes 1179656 | tf_op jit(solution)/shard_map/ppermute | solution.py:273
  9.0 9.1 %collective-permute-start.1 = (f32[2,128,128]{2,1,0:T(8,128)S(1)}, f32[2,128,128]{2,1,0:T(8,128)S(1)}, u32[]{:S(2)}, u32[]{:S(2)}) collective-permute-start(f32[2,128,128]{2,1,0:T(8,128)S(1)} %slice_add_fusion), channel_id=1, source_target_pairs={{0,8},{4,12},{8,16},{12,20},{16,24},{20,28},{24,32},{28,36},{32,40... | collective-permute-start | bytes 393224 | tf_op jit(solution)/shard_map/ppermute | solution.py:273
  18.1 8.6 %collective-permute-start.2 = (f32[2,128,128]{2,1,0:T(8,128)S(1)}, f32[2,128,128]{2,1,0:T(8,128)S(1)}, u32[]{:S(2)}, u32[]{:S(2)}) collective-permute-start(f32[2,128,128]{2,1,0:T(8,128)S(1)} %add.19), channel_id=1, source_target_pairs={{0,16},{4,20},{8,24},{12,28},{16,32},{20,36},{24,40},{28,44},{32,4... | collective-permute-start | bytes 393224 | tf_op jit(solution)/shard_map/ppermute | solution.py:273
  26.7 11.8 %collective-permute-start.3 = (f32[2,128,128]{2,1,0:T(8,128)S(1)}, f32[2,128,128]{2,1,0:T(8,128)S(1)}, u32[]{:S(2)}, u32[]{:S(2)}) collective-permute-start(f32[2,128,128]{2,1,0:T(8,128)S(1)} %add.20), channel_id=1, source_target_pairs={{0,32},{4,36},{8,40},{12,44},{16,48},{20,52},{24,56},{28,60},{32,6... | collective-permute-start | bytes 393224 | tf_op jit(solution)/shard_map/ppermute | solution.py:273
  38.5 13.0 %collective-permute-start.4 = (f32[2,128,128]{2,1,0:T(8,128)S(1)}, f32[2,128,128]{2,1,0:T(8,128)S(1)}, u32[]{:S(2)}, u32[]{:S(2)}) collective-permute-start(f32[2,128,128]{2,1,0:T(8,128)S(1)} %add.21), channel_id=1, source_target_pairs={{0,64},{4,68},{8,72},{12,76},{16,80},{20,84},{24,88},{28,92},{32,9... | collective-permute-start | bytes 393224 | tf_op jit(solution)/shard_map/ppermute | solution.py:273
  51.6 13.7 %copy-start = (f32[2048]{0:T(1024)S(1)}, f32[2048]{0:T(1024)}, u32[]{:S(2)}) copy-start(f32[2048]{0:T(1024)} %param.7) | copy-start | bytes 24580
  56.2 3.7 %collective-permute-start.5 = (f32[8,1,128]{2,1,0:T(1,128)S(1)}, f32[8,1,128]{2,1,0:T(1,128)S(1)}, u32[]{:S(2)}, u32[]{:S(2)}) collective-permute-start(f32[8,1,128]{2,1,0:T(1,128)S(1)} %get-tuple-element.114), channel_id=1, source_target_pairs={{0,1},{1,0},{2,3},{3,2},{4,5},{5,4},{6,7},{7,6},{8,9},{9,8},{10,11... | collective-permute-start | bytes 12296 | tf_op jit(solution)/shard_map/ppermute | solution.py:292
  59.9 5.5 %collective-permute-start.6 = (f32[8,1,128]{2,1,0:T(1,128)S(1)}, f32[8,1,128]{2,1,0:T(1,128)S(1)}, u32[]{:S(2)}, u32[]{:S(2)}) collective-permute-start(f32[8,1,128]{2,1,0:T(1,128)S(1)} %add.23.sa_ref), channel_id=1, source_target_pairs={{0,2},{1,3},{2,0},{3,1},{4,6},{5,7},{6,4},{7,5},{8,10},{9,11},{10,... | collective-permute-start | bytes 12296 | tf_op jit(solution)/shard_map/ppermute | solution.py:293

commit v3 on v2

--- a/solution.py
+++ b/solution.py
@@ -48,7 +48,7 @@
     )
 
 
-def state_body(k_ref, v_ref, before_ref, pack_ref):
+def state_body(k_ref, v_ref, before_ref, total_ref, tail_ref):
     count = k_ref.shape[0]
     state = jnp.zeros((D, D), f32)
     for b in range(count // BLOCK):
@@ -58,9 +58,9 @@
         vh, vl = split(v_ref[at, :])
         vv = lanes(vh, vl)
         state = state + halves(dot(rows(fh, fl), rows(vv, vv), TN))
-    pack_ref[:D] = state
-    pack_ref[D : D + BLOCK] = k_ref[count - BLOCK :, :]
-    pack_ref[D + BLOCK :] = v_ref[count - BLOCK :, :]
+    total_ref[...] = state
+    tail_ref[:BLOCK] = k_ref[count - BLOCK :, :]
+    tail_ref[BLOCK:] = v_ref[count - BLOCK :, :]
 
 
 def local_states(keys, values):
@@ -73,15 +73,47 @@
         in_specs=[pl.BlockSpec((count, D), lambda g: (0, g))] * 2,
         out_specs=[
             pl.BlockSpec((one, nb, D, D), lambda g: (g, 0, 0, 0)),
-            pl.BlockSpec((one, D + 2 * BLOCK, D), lambda g: (g, 0, 0)),
+            pl.BlockSpec((one, D, D), lambda g: (g, 0, 0)),
+            pl.BlockSpec((one, 2 * BLOCK, D), lambda g: (g, 0, 0)),
         ],
         out_shape=[
             jax.ShapeDtypeStruct((kv, nb, D, D), f32),
-            jax.ShapeDtypeStruct((kv, D + 2 * BLOCK, D), f32),
+            jax.ShapeDtypeStruct((kv, D, D), f32),
+            jax.ShapeDtypeStruct((kv, 2 * BLOCK, D), f32),
         ],
         compiler_params=params(8),
         name="local_states",
     )(keys, values)
+
+
+def place():
+    i = lax.axis_index("seq")
+    return i // 8, (i // 2) % 4, i % 2
+
+
+def chip_body(own_ref, other_ref, out_ref):
+    core = place()[2]
+    out_ref[...] = own_ref[core] + other_ref[core]
+
+
+def row_body(own_ref, one_ref, two_ref, three_ref, sum_ref, before_ref):
+    x = place()[1]
+    got = [one_ref[...], two_ref[...], three_ref[...]]
+    sum_ref[...] = own_ref[...] + got[0] + got[1] + got[2]
+    before = jnp.zeros((D, D), f32)
+    for by, state in enumerate(got, 1):
+        before = before + jnp.where(x >= by, state, 0.0)
+    before_ref[...] = before
+
+
+def small_call(body, outs, name, *args):
+    shape = jax.ShapeDtypeStruct((D, D), f32)
+    return pl.pallas_call(
+        body,
+        out_shape=[shape] * outs,
+        compiler_params=pltpu.CompilerParams(vmem_limit_bytes=2 << 20),
+        name=name,
+    )(*args)
 
 
 def block_body(wrap, carried, *refs):
@@ -116,7 +148,7 @@
         @pl.when(b == wrap)
         def _():
             for g in range(kv):
-                prepare(g, halo_ref[g, D : D + BLOCK], halo_ref[g, D + BLOCK :], there)
+                prepare(g, halo_ref[g, :BLOCK], halo_ref[g, BLOCK:], there)
 
     row = lax.broadcasted_iota(jnp.int32, (BLOCK, BLOCK), 0)
     col = lax.broadcasted_iota(jnp.int32, (BLOCK, BLOCK), 1)
@@ -195,10 +227,13 @@
     )(*args, *made)
 
 
-def linear_body(fq_ref, part_ref, before_ref, incl_ref, pack_ref, lin_ref, sq_ref):
+def linear_body(fq_ref, part_ref, inner_ref, mine_ref, their_ref, other_ref, lin_ref, sq_ref):
+    core = place()[2]
     sq = jnp.zeros((BLOCK, D), f32)
-    for g in range(incl_ref.shape[0]):
-        ss = lanes(*split((incl_ref[g] - pack_ref[g]) + before_ref[g, 0]))
+    for g in range(other_ref.shape[0]):
+        state = jnp.where(core == g, mine_ref[...], their_ref[...])
+        state = state + jnp.where(core == 1, other_ref[g], 0.0) + inner_ref[g, 0]
+        ss = lanes(*split(state))
         fq = fq_ref[0, g * G * BLOCK : (g + 1) * G * BLOCK, :]
         lin = halves(dot(fq, rows(ss, ss)))
         for i in range(G):
@@ -209,10 +244,11 @@
     sq_ref[0] = jnp.sum(sq.T, axis=0, keepdims=True)
 
 
-def linear_part(fq, part, before, incl, pack):
+def linear_part(fq, part, inner, mine, theirs, other):
     count, width = part.shape
-    kv, nb = before.shape[:2]
+    kv, nb = inner.shape[:2]
     big = pl.BlockSpec((BLOCK, width), lambda b: (b, 0))
+    state = pl.BlockSpec((D, D), lambda b: (0, 0))
     return pl.pallas_call(
         linear_body,
         grid=(nb,),
@@ -220,7 +256,8 @@
             pl.BlockSpec((1,) + fq.shape[1:], lambda b: (b, 0, 0)),
             big,
             pl.BlockSpec((kv, 1, D, D), lambda b: (0, b, 0, 0)),
-            pl.BlockSpec((kv, D, D), lambda b: (0, 0, 0)),
+            state,
+            state,
             pl.BlockSpec((kv, D, D), lambda b: (0, 0, 0)),
         ],
         out_specs=[big, pl.BlockSpec((1, 1, BLOCK), lambda b: (b, 0, 0))],
@@ -230,7 +267,7 @@
         ],
         compiler_params=params(8),
         name="linear",
-    )(fq, part, before, incl, pack)
+    )(fq, part, inner, mine, theirs, other)
 
 
 def combine_body(lin_ref, win_ref, sa_ref, sb_ref, gain_ref, out_ref):
@@ -259,39 +296,54 @@
     )(lin, win, sa, sb, gain)
 
 
+def chips(dy, dx, wrap):
+    pairs = []
+    for i in range(32):
+        y, x, core = i // 8 + dy, (i // 2) % 4 + dx, i % 2
+        if wrap or (y < 4 and x < 4):
+            pairs.append((i, (y % 4) * 8 + (x % 4) * 2 + core))
+    return pairs
+
+
+SWAP = [(i, i ^ 1) for i in range(32)]
+
+
 def shards(queries, keys, values, gain):
     count = queries.shape[0]
     nb = count // BLOCK
-    peers = lax.axis_size("seq")
     heads = lax.axis_size("head")
-    assert heads == 4 and nb == 8 and peers == 32
+    assert heads == 4 and nb == 8 and lax.axis_size("seq") == 32
     queries, keys, values = (
         pltpu.with_memory_space_constraint(x, pltpu.HBM) for x in (queries, keys, values)
     )
 
-    def behind(x, by):
-        return lax.ppermute(x, "seq", [(i, i + by) for i in range(peers - by)])
-
-    before, pack = local_states(keys, values)
-    incl = pack
-    made = []
-    halo = None
-    for number, (first, n) in enumerate([(1, 2), (3, 1), (4, 1), (5, 1), (6, 3)]):
-        got = behind(incl, 1 << number)
-        if made:
-            *made, incl = lax.optimization_barrier((*made, incl))
-        made = block_part(
-            queries, keys, values, first, n, made, halo if first + n > nb else None
-        )
-        *made, got = lax.optimization_barrier((*made, got))
-        if number == 0:
-            halo = got
-        incl = incl[:, :D] + got[:, :D]
-    win, part, fq = made
-    lin, sq = linear_part(fq, part, before, incl, pack)
+    def move(x, pairs):
+        return lax.ppermute(x, "seq", pairs)
+
+    def tie(*xs):
+        return lax.optimization_barrier(xs)
+
+    inner, total, tail = local_states(keys, values)
+    other = move(total, SWAP)
+    (chip,) = small_call(chip_body, 1, "chip_sum", total, other)
+    along_x = [move(chip, chips(0, by, True)) for by in (1, 2, 3)]
+    halo = move(tail, [(i, i + 1) for i in range(31)])
+    tail, chip = tie(tail, chip)
+    made = block_part(queries, keys, values, 1, 3, ())
+    *made, one, two, three = tie(*made, *along_x)
+    row, before = small_call(row_body, 2, "row_sum", chip, one, two, three)
+    along_y = [move(row, chips(by, 0, False)) for by in (1, 2, 3)]
+    *made, before = tie(*made, before)
+    made = block_part(queries, keys, values, 4, 2, made)
+    *made, one, two, three = tie(*made, *along_y)
+    mine = before + one + two + three
+    theirs = move(mine, SWAP)
+    *made, mine = tie(*made, mine)
+    win, part, fq = block_part(queries, keys, values, 6, 3, made, halo)
+    lin, sq = linear_part(fq, part, inner, mine, theirs, other)
     sq = sq + lax.ppermute(sq, "head", [(i, i ^ 1) for i in range(heads)])
-    other = lax.ppermute(sq, "head", [(i, i ^ 2) for i in range(heads)])
-    return combine(lin, win, sq, other, gain[None, :])
+    across = lax.ppermute(sq, "head", [(i, i ^ 2) for i in range(heads)])
+    return combine(lin, win, sq, across, gain[None, :])
 
 
 def solution(mesh):

time: 69.7 us -> 60.3 us (0.87)
  starting transfers between devices: 31.5 us -> 23.5 us
  Pallas kernels: 34.3 us -> 31.8 us
  waiting for transfers between devices: 3.29 us -> 4.62 us
    ppermute x6 -> x10, starting transfers between devices: 29.5 us -> 21.5 us  [the longest x9 17.6 us: move(): return lax.ppermute(x, 'seq', pairs)]
    pallas_call x5 -> x3, Pallas kernels: 23.8 us -> 21.2 us  [block_part(): pl.pallas_call(lambda *refs: block_body(wrap, len(made), *refs), grid=(n,...]
    ppermute x6 -> x10, waiting for transfers between devices: 1.6 us -> 2.94 us  [the longest x1 1.58 us: shards(): across = lax.ppermute(sq, 'head', [(i, i ^ 2) for i in range(heads)])]
  transfers between devices with their start and end apart: 7 -> 11, of which waited for: 2 -> 3; matrix products, arithmetic and copies ran while one was open for 0% -> 0% of each run, Pallas kernels for 34% -> 35%
where the time goes in v3:
time: 60.3 us; the launch traced here: 60.1 us
  Pallas kernels  31.8 us (53%)
  starting transfers between devices  23.5 us (39%)
  waiting for transfers between devices  4.62 us (8%)
    pallas_call x3, Pallas kernels, block_part(): pl.pallas_call(lambda *refs: block_body(wrap, len(made), *refs), grid=(n,...  21.2 us
    ppermute x9, starting transfers between devices, move(): return lax.ppermute(x, 'seq', pairs)  17.6 us
    pallas_call x1, Pallas kernels, linear_part(): pl.pallas_call(linear_body, grid=(nb,), in_specs=[pl.BlockSpec((1,) + fq....  4.57 us
    pallas_call x1, Pallas kernels, combine(): pl.pallas_call(combine_body, grid=(count // (n * BLOCK),), in_specs=[big,...  3.98 us
    ppermute x1, starting transfers between devices, shards(): across = lax.ppermute(sq, 'head', [(i, i ^ 2) for i in range(heads)])  3.89 us
    ppermute x1, starting transfers between devices, shards(): sq = sq + lax.ppermute(sq, 'head', [(i, i ^ 1) for i in range(heads)])  2 us
    pallas_call x1, Pallas kernels, local_states(): pl.pallas_call(state_body, grid=(kv,), in_specs=[pl.BlockSpec((count, D),...  1.94 us
    ppermute x1, waiting for transfers between devices, shards(): sq = sq + lax.ppermute(sq, 'head', [(i, i ^ 1) for i in range(heads)])  1.68 us
  transfers between devices with their start and end apart: 11, of which 3 were waited for; matrix products, arithmetic and copies ran while one was open for 0% of the time, Pallas kernels for 35%

profile of v3, /device:TPU:0, one launch (start us, length us, event | category | flops | bytes accessed | tf_op | source)
XLA Modules:
  0.0 60.1 jit_solution(8017395295211539230)
XLA Ops:
  0.0 1.9 %local_states.1 = (f32[2,8,128,128]{3,2,1,0:T(8,128)S(1)}, f32[2,128,128]{2,1,0:T(8,128)S(1)}, f32[2,256,128]{2,1,0:T(8,128)S(1)}) custom-call(f32[1024,256]{1,0:T(8,128)} %refs_3_.5, f32[1024,256]{1,0:T(8,128)} %refs_4_.5), custom_call_target="tpu_custom_call" | custom-call | tf_op jit(solution)/shard_map/local_states/pallas_call | solution.py:70
  2.0 0.1 collective-permute-start.1
  2.0 1.3 %collective-permute-done.1.other_ref = f32[2,128,128]{2,1,0:T(8,128)S(1)} collective-permute-done((f32[2,128,128]{2,1,0:T(8,128)S(1)}, f32[2,128,128]{2,1,0:T(8,128)S(1)}, u32[]{:S(2)}, u32[]{:S(2)}) %collective-permute-start.1) | collective-permute-done | bytes 131104 | tf_op jit(solution)/shard_map/ppermute | solution.py:321
  3.4 2.9 %collective-permute-start.4 = (f32[128,128]{1,0:T(8,128)S(1)}, f32[128,128]{1,0:T(8,128)S(1)}, u32[]{:S(2)}, u32[]{:S(2)}) collective-permute-start(f32[128,128]{1,0:T(8,128)S(1)} %chip_sum.1.own_ref), channel_id=1, source_target_pairs={{0,24},{4,28},{8,0},{12,4},{16,8},{20,12},{24,16},{28,20},{32,56},... | collective-permute-start | bytes 196616 | tf_op jit(solution)/shard_map/ppermute | solution.py:321
  6.3 0.8 %collective-permute-start.3 = (f32[128,128]{1,0:T(8,128)S(1)}, f32[128,128]{1,0:T(8,128)S(1)}, u32[]{:S(2)}, u32[]{:S(2)}) collective-permute-start(f32[128,128]{1,0:T(8,128)S(1)} %chip_sum.1.own_ref), channel_id=1, source_target_pairs={{0,16},{4,20},{8,24},{12,28},{16,0},{20,4},{24,8},{28,12},{32,48},... | collective-permute-start | bytes 196616 | tf_op jit(solution)/shard_map/ppermute | solution.py:321
  7.1 0.9 %collective-permute-start.2 = (f32[128,128]{1,0:T(8,128)S(1)}, f32[128,128]{1,0:T(8,128)S(1)}, u32[]{:S(2)}, u32[]{:S(2)}) collective-permute-start(f32[128,128]{1,0:T(8,128)S(1)} %chip_sum.1.own_ref), channel_id=1, source_target_pairs={{0,8},{4,12},{8,16},{12,20},{16,24},{20,28},{24,0},{28,4},{32,40},... | collective-permute-start | bytes 196616 | tf_op jit(solution)/shard_map/ppermute | solution.py:321
  8.0 7.7 %blocks_1_3.1 = (f32[1024,2048]{1,0:T(8,128)S(1)}, f32[1024,2048]{1,0:T(8,128)S(1)}, bf16[8,2048,256]{2,1,0:T(8,128)(2,1)S(1)}) custom-call(f32[1024,2048]{1,0:T(8,128)} %refs_0_.5, f32[1024,256]{1,0:T(8,128)} %refs_3_.5, f32[1024,256]{1,0:T(8,128)} %refs_4_.5, f32[1024,256]{1,0:T(8,128)} %refs_3_.5, f32[1024,256]{1,0:T(8,128)} %refs_4_.5), custom_call_target="tpu_custom_call" | custom-call | tf_op jit(solution)/shard_map/blocks_1_3/pallas_call | solution.py:209
  15.8 0.0 collective-permute-done.4.three_ref
  15.8 0.0 collective-permute-done.3.two_ref
  15.8 0.0 collective-permute-done.2.one_ref
  15.9 4.9 %collective-permute-start.7 = (f32[128,128]{1,0:T(8,128)S(1)}, f32[128,128]{1,0:T(8,128)S(1)}, u32[]{:S(2)}, u32[]{:S(2)}) collective-permute-start(f32[128,128]{1,0:T(8,128)S(1)} %get-tuple-element.61), channel_id=1, source_target_pairs={{0,96},{4,100},{8,104},{12,108},{16,112},{20,116},{24,120},{28,124... | collective-permute-start | bytes 196616 | tf_op jit(solution)/shard_map/ppermute | solution.py:321
  20.8 1.3 %collective-permute-start.6 = (f32[128,128]{1,0:T(8,128)S(1)}, f32[128,128]{1,0:T(8,128)S(1)}, u32[]{:S(2)}, u32[]{:S(2)}) collective-permute-start(f32[128,128]{1,0:T(8,128)S(1)} %get-tuple-element.61), channel_id=1, source_target_pairs={{0,64},{4,68},{8,72},{12,76},{16,80},{20,84},{24,88},{28,92},{32,9... | collective-permute-start | bytes 196616 | tf_op jit(solution)/shard_map/ppermute | solution.py:321
  22.1 2.8 %collective-permute-start.5 = (f32[128,128]{1,0:T(8,128)S(1)}, f32[128,128]{1,0:T(8,128)S(1)}, u32[]{:S(2)}, u32[]{:S(2)}) collective-permute-start(f32[128,128]{1,0:T(8,128)S(1)} %get-tuple-element.61), channel_id=1, source_target_pairs={{0,32},{4,36},{8,40},{12,44},{16,48},{20,52},{24,56},{28,60},{32,6... | collective-permute-start | bytes 196616 | tf_op jit(solution)/shard_map/ppermute | solution.py:321
  24.9 1.3 %collective-permute-start = (f32[2,256,128]{2,1,0:T(8,128)S(1)}, f32[2,256,128]{2,1,0:T(8,128)S(1)}, u32[]{:S(2)}, u32[]{:S(2)}) collective-permute-start(f32[2,256,128]{2,1,0:T(8,128)S(1)} %get-tuple-element.42), channel_id=1, source_target_pairs={{0,4},{4,8},{8,12},{12,16},{16,20},{20,24},{24,28},{28,32},{32,36}... | collective-permute-start | bytes 786440 | tf_op jit(solution)/shard_map/ppermute | solution.py:321
  26.2 5.7 %blocks_4_2.1 = (f32[1024,2048]{1,0:T(8,128)S(1)}, f32[1024,2048]{1,0:T(8,128)S(1)}, bf16[8,2048,256]{2,1,0:T(8,128)(2,1)S(1)}) custom-call(f32[1024,2048]{1,0:T(8,128)} %refs_0_.5, f32[1024,256]{1,0:T(8,128)} %refs_3_.5, f32[1024,256]{1,0:T(8,128)} %refs_4_.5, f32[1024,256]{1,0:T(8,128)} %refs_3_.5, ...), custom_call_target="tpu_custom_call", output_to_operand_aliasing={{0}: (5, {}), {1}: (6, {}), {2}: (7, {})} | custom-call | tf_op jit(solution)/shard_map/blocks_4_2/pallas_call | solution.py:209
  31.8 0.0 collective-permute-done.7
  31.9 0.0 collective-permute-done.6
  31.9 0.0 collective-permute-done.5
  31.9 2.6 %collective-permute-start.8 = (f32[128,128]{1,0:T(8,128)S(1)}, f32[128,128]{1,0:T(8,128)S(1)}, u32[]{:S(2)}, u32[]{:S(2)}) collective-permute-start(f32[128,128]{1,0:T(8,128)S(1)} %add_add_fusion.mine_ref), channel_id=1, source_target_pairs={{0,4},{4,0},{8,12},{12,8},{16,20},{20,16},{24,28},{28,24},{32,36},... | collective-permute-start | bytes 196616 | tf_op jit(solution)/shard_map/ppermute | solution.py:321
  34.5 0.0 collective-permute-done.refs_5_
  34.5 7.8 %blocks_6_3.1 = (f32[1024,2048]{1,0:T(8,128)S(1)}, f32[1024,2048]{1,0:T(8,128)S(1)}, bf16[8,2048,256]{2,1,0:T(8,128)(2,1)S(1)}) custom-call(f32[1024,2048]{1,0:T(8,128)} %refs_0_.5, f32[1024,256]{1,0:T(8,128)} %refs_3_.5, f32[1024,256]{1,0:T(8,128)} %refs_4_.5, f32[1024,256]{1,0:T(8,128)} %refs_3_.5, ...), custom_call_target="tpu_custom_call", output_to_operand_aliasing={{0}: (6, {}), {1}: (7, {}), {2}: (8, {})} | custom-call | tf_op jit(solution)/shard_map/blocks_6_3/pallas_call | solution.py:209
  42.3 0.0 collective-permute-done.8.their_ref
  42.3 0.0 copy-start
  42.3 4.6 %linear.1 = (f32[1024,2048]{1,0:T(8,128)S(1)}, f32[8,1,128]{2,1,0:T(1,128)S(1)}) custom-call(bf16[8,2048,256]{2,1,0:T(8,128)(2,1)S(1)} %get-tuple-element.72.fq_ref, f32[1024,2048]{1,0:T(8,128)S(1)} %get-tuple-element.73.part_ref, f32[2,8,128,128]{3,2,1,0:T(8,128)S(1)} %get-tuple-element.74.inner_ref, f32[128,128]{1,0:T(8,128)S(1)} %add_add_fusion.mine_ref, ...), custom_call_target="tpu_custom_call" | custom-call | tf_op jit(solution)/shard_map/linear/pallas_call | solution.py:252
  46.9 2.0 %collective-permute-start.9 = (f32[8,1,128]{2,1,0:T(1,128)S(1)}, f32[8,1,128]{2,1,0:T(1,128)S(1)}, u32[]{:S(2)}, u32[]{:S(2)}) collective-permute-start(f32[8,1,128]{2,1,0:T(1,128)S(1)} %get-tuple-element.78), channel_id=1, source_target_pairs={{0,1},{1,0},{2,3},{3,2},{4,5},{5,4},{6,7},{7,6},{8,9},{9,8},{10,11... | collective-permute-start | bytes 12296 | tf_op jit(solution)/shard_map/ppermute | solution.py:344
  48.9 1.7 %collective-permute-done.9 = f32[8,1,128]{2,1,0:T(1,128)S(1)} collective-permute-done((f32[8,1,128]{2,1,0:T(1,128)S(1)}, f32[8,1,128]{2,1,0:T(1,128)S(1)}, u32[]{:S(2)}, u32[]{:S(2)}) %collective-permute-start.9) | collective-permute-done | bytes 4128 | tf_op jit(solution)/shard_map/ppermute | solution.py:344
  50.6 3.9 %collective-permute-start.10 = (f32[8,1,128]{2,1,0:T(1,128)S(1)}, f32[8,1,128]{2,1,0:T(1,128)S(1)}, u32[]{:S(2)}, u32[]{:S(2)}) collective-permute-start(f32[8,1,128]{2,1,0:T(1,128)S(1)} %add.15.sa_ref), channel_id=1, source_target_pairs={{0,2},{1,3},{2,0},{3,1},{4,6},{5,7},{6,4},{7,5},{8,10},{9,11},{10,... | collective-permute-start | bytes 12296 | tf_op jit(solution)/shard_map/ppermute | solution.py:345
  54.5 1.6 %collective-permute-done.10.sb_ref = f32[8,1,128]{2,1,0:T(1,128)S(1)} collective-permute-done((f32[8,1,128]{2,1,0:T(1,128)S(1)}, f32[8,1,128]{2,1,0:T(1,128)S(1)}, u32[]{:S(2)}, u32[]{:S(2)}) %collective-permute-start.10) | collective-permute-done | bytes 4128 | tf_op jit(solution)/shard_map/ppermute | solution.py:345
  56.1 0.0 copy-done
  56.1 4.0 %combine.1 = f32[1024,2048]{1,0:T(8,128)} custom-call(f32[1024,2048]{1,0:T(8,128)S(1)} %get-tuple-element.76.lin_ref, f32[1024,2048]{1,0:T(8,128)S(1)} %get-tuple-element.77.win_ref, f32[8,1,128]{2,1,0:T(1,128)S(1)} %add.15.sa_ref, f32[8,1,128]{2,1,0:T(1,128)S(1)} %collective-permute-done.10.sb_ref, f32[1,2048]{1,0:T(1,128)S(1)} %bitcast.1), custom_call_target="tpu_custom_call" | custom-call | tf_op jit(solution)/shard_map/combine/pallas_call | solution.py:288
  (4 shorter events, 0.1 us)
Async XLA Ops:
  2.0 1.4 %collective-permute-start.1 = (f32[2,128,128]{2,1,0:T(8,128)S(1)}, f32[2,128,128]{2,1,0:T(8,128)S(1)}, u32[]{:S(2)}, u32[]{:S(2)}) collective-permute-start(f32[2,128,128]{2,1,0:T(8,128)S(1)} %get-tuple-element.46.own_ref), channel_id=1, source_target_pairs={{0,4},{4,0},{8,12},{12,8},{16,20},{20,16},{24,28},{28,24},{32,36},... | collective-permute-start | bytes 393224 | tf_op jit(solution)/shard_map/ppermute | solution.py:321
  3.4 12.4 %collective-permute-start.4 = (f32[128,128]{1,0:T(8,128)S(1)}, f32[128,128]{1,0:T(8,128)S(1)}, u32[]{:S(2)}, u32[]{:S(2)}) collective-permute-start(f32[128,128]{1,0:T(8,128)S(1)} %chip_sum.1.own_ref), channel_id=1, source_target_pairs={{0,24},{4,28},{8,0},{12,4},{16,8},{20,12},{24,16},{28,20},{32,56},... | collective-permute-start | bytes 196616 | tf_op jit(solution)/shard_map/ppermute | solution.py:321
  6.3 9.5 %collective-permute-start.3 = (f32[128,128]{1,0:T(8,128)S(1)}, f32[128,128]{1,0:T(8,128)S(1)}, u32[]{:S(2)}, u32[]{:S(2)}) collective-permute-start(f32[128,128]{1,0:T(8,128)S(1)} %chip_sum.1.own_ref), channel_id=1, source_target_pairs={{0,16},{4,20},{8,24},{12,28},{16,0},{20,4},{24,8},{28,12},{32,48},... | collective-permute-start | bytes 196616 | tf_op jit(solution)/shard_map/ppermute | solution.py:321
  7.1 8.7 %collective-permute-start.2 = (f32[128,128]{1,0:T(8,128)S(1)}, f32[128,128]{1,0:T(8,128)S(1)}, u32[]{:S(2)}, u32[]{:S(2)}) collective-permute-start(f32[128,128]{1,0:T(8,128)S(1)} %chip_sum.1.own_ref), channel_id=1, source_target_pairs={{0,8},{4,12},{8,16},{12,20},{16,24},{20,28},{24,0},{28,4},{32,40},... | collective-permute-start | bytes 196616 | tf_op jit(solution)/shard_map/ppermute | solution.py:321
  15.9 16.0 %collective-permute-start.7 = (f32[128,128]{1,0:T(8,128)S(1)}, f32[128,128]{1,0:T(8,128)S(1)}, u32[]{:S(2)}, u32[]{:S(2)}) collective-permute-start(f32[128,128]{1,0:T(8,128)S(1)} %get-tuple-element.61), channel_id=1, source_target_pairs={{0,96},{4,100},{8,104},{12,108},{16,112},{20,116},{24,120},{28,124... | collective-permute-start | bytes 196616 | tf_op jit(solution)/shard_map/ppermute | solution.py:321
  20.8 11.1 %collective-permute-start.6 = (f32[128,128]{1,0:T(8,128)S(1)}, f32[128,128]{1,0:T(8,128)S(1)}, u32[]{:S(2)}, u32[]{:S(2)}) collective-permute-start(f32[128,128]{1,0:T(8,128)S(1)} %get-tuple-element.61), channel_id=1, source_target_pairs={{0,64},{4,68},{8,72},{12,76},{16,80},{20,84},{24,88},{28,92},{32,9... | collective-permute-start | bytes 196616 | tf_op jit(solution)/shard_map/ppermute | solution.py:321
  22.1 9.8 %collective-permute-start.5 = (f32[128,128]{1,0:T(8,128)S(1)}, f32[128,128]{1,0:T(8,128)S(1)}, u32[]{:S(2)}, u32[]{:S(2)}) collective-permute-start(f32[128,128]{1,0:T(8,128)S(1)} %get-tuple-element.61), channel_id=1, source_target_pairs={{0,32},{4,36},{8,40},{12,44},{16,48},{20,52},{24,56},{28,60},{32,6... | collective-permute-start | bytes 196616 | tf_op jit(solution)/shard_map/ppermute | solution.py:321
  24.9 9.6 %collective-permute-start = (f32[2,256,128]{2,1,0:T(8,128)S(1)}, f32[2,256,128]{2,1,0:T(8,128)S(1)}, u32[]{:S(2)}, u32[]{:S(2)}) collective-permute-start(f32[2,256,128]{2,1,0:T(8,128)S(1)} %get-tuple-element.42), channel_id=1, source_target_pairs={{0,4},{4,8},{8,12},{12,16},{16,20},{20,24},{24,28},{28,32},{32,36}... | collective-permute-start | bytes 786440 | tf_op jit(solution)/shard_map/ppermute | solution.py:321
  31.9 10.4 %collective-permute-start.8 = (f32[128,128]{1,0:T(8,128)S(1)}, f32[128,128]{1,0:T(8,128)S(1)}, u32[]{:S(2)}, u32[]{:S(2)}) collective-permute-start(f32[128,128]{1,0:T(8,128)S(1)} %add_add_fusion.mine_ref), channel_id=1, source_target_pairs={{0,4},{4,0},{8,12},{12,8},{16,20},{20,16},{24,28},{28,24},{32,36},... | collective-permute-start | bytes 196616 | tf_op jit(solution)/shard_map/ppermute | solution.py:321
  42.3 13.8 %copy-start = (f32[2048]{0:T(1024)S(1)}, f32[2048]{0:T(1024)}, u32[]{:S(2)}) copy-start(f32[2048]{0:T(1024)} %param.7) | copy-start | bytes 24580
  46.9 3.7 %collective-permute-start.9 = (f32[8,1,128]{2,1,0:T(1,128)S(1)}, f32[8,1,128]{2,1,0:T(1,128)S(1)}, u32[]{:S(2)}, u32[]{:S(2)}) collective-permute-start(f32[8,1,128]{2,1,0:T(1,128)S(1)} %get-tuple-element.78), channel_id=1, source_target_pairs={{0,1},{1,0},{2,3},{3,2},{4,5},{5,4},{6,7},{7,6},{8,9},{9,8},{10,11... | collective-permute-start | bytes 12296 | tf_op jit(solution)/shard_map/ppermute | solution.py:344
  50.6 5.5 %collective-permute-start.10 = (f32[8,1,128]{2,1,0:T(1,128)S(1)}, f32[8,1,128]{2,1,0:T(1,128)S(1)}, u32[]{:S(2)}, u32[]{:S(2)}) collective-permute-start(f32[8,1,128]{2,1,0:T(1,128)S(1)} %add.15.sa_ref), channel_id=1, source_target_pairs={{0,2},{1,3},{2,0},{3,1},{4,6},{5,7},{6,4},{7,5},{8,10},{9,11},{10,... | collective-permute-start | bytes 12296 | tf_op jit(solution)/shard_map/ppermute | solution.py:345

commit v4 on v3

--- a/solution.py
+++ b/solution.py
@@ -296,13 +296,12 @@
     )(lin, win, sa, sb, gain)
 
 
-def chips(dy, dx, wrap):
-    pairs = []
-    for i in range(32):
-        y, x, core = i // 8 + dy, (i // 2) % 4 + dx, i % 2
-        if wrap or (y < 4 and x < 4):
-            pairs.append((i, (y % 4) * 8 + (x % 4) * 2 + core))
-    return pairs
+def shift_x(by):
+    return [(i, i // 8 * 8 + (i + 2 * by) % 8) for i in range(32)]
+
+
+def down_from(y):
+    return [(y * 8 + i, (y + 1) * 8 + i) for i in range(8)]
 
 
 SWAP = [(i, i ^ 1) for i in range(32)]
@@ -326,20 +325,19 @@
     inner, total, tail = local_states(keys, values)
     other = move(total, SWAP)
     (chip,) = small_call(chip_body, 1, "chip_sum", total, other)
-    along_x = [move(chip, chips(0, by, True)) for by in (1, 2, 3)]
+    along_x = [move(chip, shift_x(by)) for by in (1, 2, 3)]
     halo = move(tail, [(i, i + 1) for i in range(31)])
-    tail, chip = tie(tail, chip)
-    made = block_part(queries, keys, values, 1, 3, ())
+    made = block_part(queries, keys, values, 1, 2, ())
     *made, one, two, three = tie(*made, *along_x)
-    row, before = small_call(row_body, 2, "row_sum", chip, one, two, three)
-    along_y = [move(row, chips(by, 0, False)) for by in (1, 2, 3)]
-    *made, before = tie(*made, before)
-    made = block_part(queries, keys, values, 4, 2, made)
-    *made, one, two, three = tie(*made, *along_y)
-    mine = before + one + two + three
+    row, mine = small_call(row_body, 2, "row_sum", chip, one, two, three)
+    for y, first in enumerate((3, 5, 7)):
+        got = move(row, down_from(y))
+        *made, mine = tie(*made, mine)
+        made = block_part(queries, keys, values, first, 2, made, halo if first == 7 else None)
+        *made, got = tie(*made, got)
+        row, mine = row + got, mine + got
     theirs = move(mine, SWAP)
-    *made, mine = tie(*made, mine)
-    win, part, fq = block_part(queries, keys, values, 6, 3, made, halo)
+    win, part, fq = made
     lin, sq = linear_part(fq, part, inner, mine, theirs, other)
     sq = sq + lax.ppermute(sq, "head", [(i, i ^ 1) for i in range(heads)])
     across = lax.ppermute(sq, "head", [(i, i ^ 2) for i in range(heads)])

time: 60.3 us -> 58.6 us (0.972)
  starting transfers between devices: 23.5 us -> 19.3 us
  Pallas kernels: 31.8 us -> 33.2 us
  waiting for transfers between devices: 4.62 us -> 5.52 us
    ppermute x9, starting transfers between devices: 17.6 us -> 13.4 us  [move(): return lax.ppermute(x, 'seq', pairs)]
    pallas_call x3 -> x4, Pallas kernels: 21.2 us -> 22.7 us  [block_part(): pl.pallas_call(lambda *refs: block_body(wrap, len(made), *refs), grid=(n,...]
    ppermute x9, waiting for transfers between devices: 1.36 us -> 2.26 us  [move(): return lax.ppermute(x, 'seq', pairs)]
  transfers between devices with their start and end apart: 11 -> 11, of which waited for: 3 -> 4; matrix products, arithmetic and copies ran while one was open for 0% -> 0% of each run, Pallas kernels for 35% -> 39%
where the time goes in v4:
time: 58.6 us; the launch traced here: 58.3 us
  Pallas kernels  33.2 us (57%)
  starting transfers between devices  19.3 us (33%)
  waiting for transfers between devices  5.52 us (9%)
    pallas_call x4, Pallas kernels, block_part(): pl.pallas_call(lambda *refs: block_body(wrap, len(made), *refs), grid=(n,...  22.7 us
    ppermute x9, starting transfers between devices, move(): return lax.ppermute(x, 'seq', pairs)  13.4 us
    pallas_call x1, Pallas kernels, linear_part(): pl.pallas_call(linear_body, grid=(nb,), in_specs=[pl.BlockSpec((1,) + fq....  4.57 us
    pallas_call x1, Pallas kernels, combine(): pl.pallas_call(combine_body, grid=(count // (n * BLOCK),), in_specs=[big,...  3.98 us
    ppermute x1, starting transfers between devices, shards(): across = lax.ppermute(sq, 'head', [(i, i ^ 2) for i in range(heads)])  3.88 us
    ppermute x9, waiting for transfers between devices, move(): return lax.ppermute(x, 'seq', pairs)  2.26 us
    ppermute x1, starting transfers between devices, shards(): sq = sq + lax.ppermute(sq, 'head', [(i, i ^ 1) for i in range(heads)])  2 us
    pallas_call x1, Pallas kernels, local_states(): pl.pallas_call(state_body, grid=(kv,), in_specs=[pl.BlockSpec((count, D),...  1.94 us
  transfers between devices with their start and end apart: 11, of which 4 were waited for; matrix products, arithmetic and copies ran while one was open for 0% of the time, Pallas kernels for 39%

profile of v4, /device:TPU:0, one launch (start us, length us, event | category | flops | bytes accessed | tf_op | source)
XLA Modules:
  0.0 58.3 jit_solution(4702307300166952003)
XLA Ops:
  0.0 1.9 %local_states.1 = (f32[2,8,128,128]{3,2,1,0:T(8,128)S(1)}, f32[2,128,128]{2,1,0:T(8,128)S(1)}, f32[2,256,128]{2,1,0:T(8,128)S(1)}) custom-call(f32[1024,256]{1,0:T(8,128)} %refs_3_.7, f32[1024,256]{1,0:T(8,128)} %refs_4_.7), custom_call_target="tpu_custom_call" | custom-call | tf_op jit(solution)/shard_map/local_states/pallas_call | solution.py:70
  2.0 0.1 collective-permute-start.1
  2.0 1.3 %collective-permute-done.1.other_ref = f32[2,128,128]{2,1,0:T(8,128)S(1)} collective-permute-done((f32[2,128,128]{2,1,0:T(8,128)S(1)}, f32[2,128,128]{2,1,0:T(8,128)S(1)}, u32[]{:S(2)}, u32[]{:S(2)}) %collective-permute-start.1) | collective-permute-done | bytes 131104 | tf_op jit(solution)/shard_map/ppermute | solution.py:320
  3.4 2.9 %collective-permute-start.4 = (f32[128,128]{1,0:T(8,128)S(1)}, f32[128,128]{1,0:T(8,128)S(1)}, u32[]{:S(2)}, u32[]{:S(2)}) collective-permute-start(f32[128,128]{1,0:T(8,128)S(1)} %chip_sum.1.own_ref), channel_id=1, source_target_pairs={{0,24},{4,28},{8,0},{12,4},{16,8},{20,12},{24,16},{28,20},{32,56},... | collective-permute-start | bytes 196616 | tf_op jit(solution)/shard_map/ppermute | solution.py:320
  6.3 0.8 %collective-permute-start.3 = (f32[128,128]{1,0:T(8,128)S(1)}, f32[128,128]{1,0:T(8,128)S(1)}, u32[]{:S(2)}, u32[]{:S(2)}) collective-permute-start(f32[128,128]{1,0:T(8,128)S(1)} %chip_sum.1.own_ref), channel_id=1, source_target_pairs={{0,16},{4,20},{8,24},{12,28},{16,0},{20,4},{24,8},{28,12},{32,48},... | collective-permute-start | bytes 196616 | tf_op jit(solution)/shard_map/ppermute | solution.py:320
  7.1 0.9 %collective-permute-start.2 = (f32[128,128]{1,0:T(8,128)S(1)}, f32[128,128]{1,0:T(8,128)S(1)}, u32[]{:S(2)}, u32[]{:S(2)}) collective-permute-start(f32[128,128]{1,0:T(8,128)S(1)} %chip_sum.1.own_ref), channel_id=1, source_target_pairs={{0,8},{4,12},{8,16},{12,20},{16,24},{20,28},{24,0},{28,4},{32,40},... | collective-permute-start | bytes 196616 | tf_op jit(solution)/shard_map/ppermute | solution.py:320
  8.0 5.6 %blocks_1_2.1 = (f32[1024,2048]{1,0:T(8,128)S(1)}, f32[1024,2048]{1,0:T(8,128)S(1)}, bf16[8,2048,256]{2,1,0:T(8,128)(2,1)S(1)}) custom-call(f32[1024,2048]{1,0:T(8,128)} %refs_0_.7, f32[1024,256]{1,0:T(8,128)} %refs_3_.7, f32[1024,256]{1,0:T(8,128)} %refs_4_.7, f32[1024,256]{1,0:T(8,128)} %refs_3_.7, f32[1024,256]{1,0:T(8,128)} %refs_4_.7), custom_call_target="tpu_custom_call" | custom-call | tf_op jit(solution)/shard_map/blocks_1_2/pallas_call | solution.py:209
  13.7 0.0 collective-permute-done.4.three_ref
  13.7 0.0 collective-permute-done.3.two_ref
  13.7 0.0 collective-permute-done.2.one_ref
  13.7 3.5 %collective-permute-start.5 = (f32[128,128]{1,0:T(8,128)S(1)}, f32[128,128]{1,0:T(8,128)S(1)}, u32[]{:S(2)}, u32[]{:S(2)}) collective-permute-start(f32[128,128]{1,0:T(8,128)S(1)} %get-tuple-element.72), channel_id=1, source_target_pairs={{0,32},{4,36},{8,40},{12,44},{16,48},{20,52},{24,56},{28,60},{1,33... | collective-permute-start | bytes 196616 | tf_op jit(solution)/shard_map/ppermute | solution.py:320
  17.2 5.7 %blocks_3_2.1 = (f32[1024,2048]{1,0:T(8,128)S(1)}, f32[1024,2048]{1,0:T(8,128)S(1)}, bf16[8,2048,256]{2,1,0:T(8,128)(2,1)S(1)}) custom-call(f32[1024,2048]{1,0:T(8,128)} %refs_0_.7, f32[1024,256]{1,0:T(8,128)} %refs_3_.7, f32[1024,256]{1,0:T(8,128)} %refs_4_.7, f32[1024,256]{1,0:T(8,128)} %refs_3_.7, ...), custom_call_target="tpu_custom_call", output_to_operand_aliasing={{0}: (5, {}), {1}: (6, {}), {2}: (7, {})} | custom-call | tf_op jit(solution)/shard_map/blocks_3_2/pallas_call | solution.py:209
  22.9 0.0 collective-permute-done.5
  22.9 0.7 %collective-permute-start.6 = (f32[128,128]{1,0:T(8,128)S(1)}, f32[128,128]{1,0:T(8,128)S(1)}, u32[]{:S(2)}, u32[]{:S(2)}) collective-permute-start(f32[128,128]{1,0:T(8,128)S(1)} %get-tuple-element.105), channel_id=1, source_target_pairs={{32,64},{36,68},{40,72},{44,76},{48,80},{52,84},{56,88},{60,92},{3... | collective-permute-start | bytes 196616 | tf_op jit(solution)/shard_map/ppermute | solution.py:320
  23.6 1.3 %collective-permute-start = (f32[2,256,128]{2,1,0:T(8,128)S(1)}, f32[2,256,128]{2,1,0:T(8,128)S(1)}, u32[]{:S(2)}, u32[]{:S(2)}) collective-permute-start(f32[2,256,128]{2,1,0:T(8,128)S(1)} %get-tuple-element.54), channel_id=1, source_target_pairs={{0,4},{4,8},{8,12},{12,16},{16,20},{20,24},{24,28},{28,32},{32,36}... | collective-permute-start | bytes 786440 | tf_op jit(solution)/shard_map/ppermute | solution.py:320
  24.9 5.7 %blocks_5_2.1 = (f32[1024,2048]{1,0:T(8,128)S(1)}, f32[1024,2048]{1,0:T(8,128)S(1)}, bf16[8,2048,256]{2,1,0:T(8,128)(2,1)S(1)}) custom-call(f32[1024,2048]{1,0:T(8,128)} %refs_0_.7, f32[1024,256]{1,0:T(8,128)} %refs_3_.7, f32[1024,256]{1,0:T(8,128)} %refs_4_.7, f32[1024,256]{1,0:T(8,128)} %refs_3_.7, ...), custom_call_target="tpu_custom_call", output_to_operand_aliasing={{0}: (5, {}), {1}: (6, {}), {2}: (7, {})} | custom-call | tf_op jit(solution)/shard_map/blocks_5_2/pallas_call | solution.py:209
  30.6 0.0 collective-permute-done.6
  30.6 0.7 %collective-permute-start.7 = (f32[128,128]{1,0:T(8,128)S(1)}, f32[128,128]{1,0:T(8,128)S(1)}, u32[]{:S(2)}, u32[]{:S(2)}) collective-permute-start(f32[128,128]{1,0:T(8,128)S(1)} %get-tuple-element.103), channel_id=1, source_target_pairs={{64,96},{68,100},{72,104},{76,108},{80,112},{84,116},{88,120},{92,... | collective-permute-start | bytes 196616 | tf_op jit(solution)/shard_map/ppermute | solution.py:320
  31.3 0.0 collective-permute-done.refs_5_
  31.3 5.7 %blocks_7_2.1 = (f32[1024,2048]{1,0:T(8,128)S(1)}, f32[1024,2048]{1,0:T(8,128)S(1)}, bf16[8,2048,256]{2,1,0:T(8,128)(2,1)S(1)}) custom-call(f32[1024,2048]{1,0:T(8,128)} %refs_0_.7, f32[1024,256]{1,0:T(8,128)} %refs_3_.7, f32[1024,256]{1,0:T(8,128)} %refs_4_.7, f32[1024,256]{1,0:T(8,128)} %refs_3_.7, ...), custom_call_target="tpu_custom_call", output_to_operand_aliasing={{0}: (6, {}), {1}: (7, {}), {2}: (8, {})} | custom-call | tf_op jit(solution)/shard_map/blocks_7_2/pallas_call | solution.py:209
  37.1 0.0 collective-permute-done.7
  37.1 2.6 %collective-permute-start.8 = (f32[128,128]{1,0:T(8,128)S(1)}, f32[128,128]{1,0:T(8,128)S(1)}, u32[]{:S(2)}, u32[]{:S(2)}) collective-permute-start(f32[128,128]{1,0:T(8,128)S(1)} %add.22.mine_ref), channel_id=1, source_target_pairs={{0,4},{4,0},{8,12},{12,8},{16,20},{20,16},{24,28},{28,24},{32,36},... | collective-permute-start | bytes 196616 | tf_op jit(solution)/shard_map/ppermute | solution.py:320
  39.7 0.9 %collective-permute-done.8.their_ref = f32[128,128]{1,0:T(8,128)S(1)} collective-permute-done((f32[128,128]{1,0:T(8,128)S(1)}, f32[128,128]{1,0:T(8,128)S(1)}, u32[]{:S(2)}, u32[]{:S(2)}) %collective-permute-start.8) | collective-permute-done | bytes 65568 | tf_op jit(solution)/shard_map/ppermute | solution.py:320
  40.6 0.0 copy-start
  40.6 4.6 %linear.1 = (f32[1024,2048]{1,0:T(8,128)S(1)}, f32[8,1,128]{2,1,0:T(1,128)S(1)}) custom-call(bf16[8,2048,256]{2,1,0:T(8,128)(2,1)S(1)} %get-tuple-element.95.fq_ref, f32[1024,2048]{1,0:T(8,128)S(1)} %get-tuple-element.96.part_ref, f32[2,8,128,128]{3,2,1,0:T(8,128)S(1)} %get-tuple-element.97.inner_ref, f32[128,128]{1,0:T(8,128)S(1)} %add.22.mine_ref, ...), custom_call_target="tpu_custom_call" | custom-call | tf_op jit(solution)/shard_map/linear/pallas_call | solution.py:252
  45.2 2.0 %collective-permute-start.9 = (f32[8,1,128]{2,1,0:T(1,128)S(1)}, f32[8,1,128]{2,1,0:T(1,128)S(1)}, u32[]{:S(2)}, u32[]{:S(2)}) collective-permute-start(f32[8,1,128]{2,1,0:T(1,128)S(1)} %get-tuple-element.102), channel_id=1, source_target_pairs={{0,1},{1,0},{2,3},{3,2},{4,5},{5,4},{6,7},{7,6},{8,9},{9,8},{10,11... | collective-permute-start | bytes 12296 | tf_op jit(solution)/shard_map/ppermute | solution.py:342
  47.2 1.7 %collective-permute-done.9 = f32[8,1,128]{2,1,0:T(1,128)S(1)} collective-permute-done((f32[8,1,128]{2,1,0:T(1,128)S(1)}, f32[8,1,128]{2,1,0:T(1,128)S(1)}, u32[]{:S(2)}, u32[]{:S(2)}) %collective-permute-start.9) | collective-permute-done | bytes 4128 | tf_op jit(solution)/shard_map/ppermute | solution.py:342
  48.9 3.9 %collective-permute-start.10 = (f32[8,1,128]{2,1,0:T(1,128)S(1)}, f32[8,1,128]{2,1,0:T(1,128)S(1)}, u32[]{:S(2)}, u32[]{:S(2)}) collective-permute-start(f32[8,1,128]{2,1,0:T(1,128)S(1)} %add.23.sa_ref), channel_id=1, source_target_pairs={{0,2},{1,3},{2,0},{3,1},{4,6},{5,7},{6,4},{7,5},{8,10},{9,11},{10,... | collective-permute-start | bytes 12296 | tf_op jit(solution)/shard_map/ppermute | solution.py:343
  52.7 1.6 %collective-permute-done.10.sb_ref = f32[8,1,128]{2,1,0:T(1,128)S(1)} collective-permute-done((f32[8,1,128]{2,1,0:T(1,128)S(1)}, f32[8,1,128]{2,1,0:T(1,128)S(1)}, u32[]{:S(2)}, u32[]{:S(2)}) %collective-permute-start.10) | collective-permute-done | bytes 4128 | tf_op jit(solution)/shard_map/ppermute | solution.py:343
  54.3 0.0 copy-done
  54.3 4.0 %combine.1 = f32[1024,2048]{1,0:T(8,128)} custom-call(f32[1024,2048]{1,0:T(8,128)S(1)} %get-tuple-element.100.lin_ref, f32[1024,2048]{1,0:T(8,128)S(1)} %get-tuple-element.101.win_ref, f32[8,1,128]{2,1,0:T(1,128)S(1)} %add.23.sa_ref, f32[8,1,128]{2,1,0:T(1,128)S(1)} %collective-permute-done.10.sb_ref, f32[1,2048]{1,0:T(1,128)S(1)} %bitcast.1), custom_call_target="tpu_custom_call" | custom-call | tf_op jit(solution)/shard_map/combine/pallas_call | solution.py:288
  (6 shorter events, 0.1 us)
Async XLA Ops:
  2.0 1.4 %collective-permute-start.1 = (f32[2,128,128]{2,1,0:T(8,128)S(1)}, f32[2,128,128]{2,1,0:T(8,128)S(1)}, u32[]{:S(2)}, u32[]{:S(2)}) collective-permute-start(f32[2,128,128]{2,1,0:T(8,128)S(1)} %get-tuple-element.58.own_ref), channel_id=1, source_target_pairs={{0,4},{4,0},{8,12},{12,8},{16,20},{20,16},{24,28},{28,24},{32,36},... | collective-permute-start | bytes 393224 | tf_op jit(solution)/shard_map/ppermute | solution.py:320
  3.4 10.3 %collective-permute-start.4 = (f32[128,128]{1,0:T(8,128)S(1)}, f32[128,128]{1,0:T(8,128)S(1)}, u32[]{:S(2)}, u32[]{:S(2)}) collective-permute-start(f32[128,128]{1,0:T(8,128)S(1)} %chip_sum.1.own_ref), channel_id=1, source_target_pairs={{0,24},{4,28},{8,0},{12,4},{16,8},{20,12},{24,16},{28,20},{32,56},... | collective-permute-start | bytes 196616 | tf_op jit(solution)/shard_map/ppermute | solution.py:320
  6.3 7.3 %collective-permute-start.3 = (f32[128,128]{1,0:T(8,128)S(1)}, f32[128,128]{1,0:T(8,128)S(1)}, u32[]{:S(2)}, u32[]{:S(2)}) collective-permute-start(f32[128,128]{1,0:T(8,128)S(1)} %chip_sum.1.own_ref), channel_id=1, source_target_pairs={{0,16},{4,20},{8,24},{12,28},{16,0},{20,4},{24,8},{28,12},{32,48},... | collective-permute-start | bytes 196616 | tf_op jit(solution)/shard_map/ppermute | solution.py:320
  7.1 6.6 %collective-permute-start.2 = (f32[128,128]{1,0:T(8,128)S(1)}, f32[128,128]{1,0:T(8,128)S(1)}, u32[]{:S(2)}, u32[]{:S(2)}) collective-permute-start(f32[128,128]{1,0:T(8,128)S(1)} %chip_sum.1.own_ref), channel_id=1, source_target_pairs={{0,8},{4,12},{8,16},{12,20},{16,24},{20,28},{24,0},{28,4},{32,40},... | collective-permute-start | bytes 196616 | tf_op jit(solution)/shard_map/ppermute | solution.py:320
  13.7 9.2 %collective-permute-start.5 = (f32[128,128]{1,0:T(8,128)S(1)}, f32[128,128]{1,0:T(8,128)S(1)}, u32[]{:S(2)}, u32[]{:S(2)}) collective-permute-start(f32[128,128]{1,0:T(8,128)S(1)} %get-tuple-element.72), channel_id=1, source_target_pairs={{0,32},{4,36},{8,40},{12,44},{16,48},{20,52},{24,56},{28,60},{1,33... | collective-permute-start | bytes 196616 | tf_op jit(solution)/shard_map/ppermute | solution.py:320
  22.9 7.7 %collective-permute-start.6 = (f32[128,128]{1,0:T(8,128)S(1)}, f32[128,128]{1,0:T(8,128)S(1)}, u32[]{:S(2)}, u32[]{:S(2)}) collective-permute-start(f32[128,128]{1,0:T(8,128)S(1)} %get-tuple-element.105), channel_id=1, source_target_pairs={{32,64},{36,68},{40,72},{44,76},{48,80},{52,84},{56,88},{60,92},{3... | collective-permute-start | bytes 196616 | tf_op jit(solution)/shard_map/ppermute | solution.py:320
  23.6 7.7 %collective-permute-start = (f32[2,256,128]{2,1,0:T(8,128)S(1)}, f32[2,256,128]{2,1,0:T(8,128)S(1)}, u32[]{:S(2)}, u32[]{:S(2)}) collective-permute-start(f32[2,256,128]{2,1,0:T(8,128)S(1)} %get-tuple-element.54), channel_id=1, source_target_pairs={{0,4},{4,8},{8,12},{12,16},{16,20},{20,24},{24,28},{28,32},{32,36}... | collective-permute-start | bytes 786440 | tf_op jit(solution)/shard_map/ppermute | solution.py:320
  30.6 6.4 %collective-permute-start.7 = (f32[128,128]{1,0:T(8,128)S(1)}, f32[128,128]{1,0:T(8,128)S(1)}, u32[]{:S(2)}, u32[]{:S(2)}) collective-permute-start(f32[128,128]{1,0:T(8,128)S(1)} %get-tuple-element.103), channel_id=1, source_target_pairs={{64,96},{68,100},{72,104},{76,108},{80,112},{84,116},{88,120},{92,... | collective-permute-start | bytes 196616 | tf_op jit(solution)/shard_map/ppermute | solution.py:320
  37.1 3.5 %collective-permute-start.8 = (f32[128,128]{1,0:T(8,128)S(1)}, f32[128,128]{1,0:T(8,128)S(1)}, u32[]{:S(2)}, u32[]{:S(2)}) collective-permute-start(f32[128,128]{1,0:T(8,128)S(1)} %add.22.mine_ref), channel_id=1, source_target_pairs={{0,4},{4,0},{8,12},{12,8},{16,20},{20,16},{24,28},{28,24},{32,36},... | collective-permute-start | bytes 196616 | tf_op jit(solution)/shard_map/ppermute | solution.py:320
  40.6 13.7 %copy-start = (f32[2048]{0:T(1024)S(1)}, f32[2048]{0:T(1024)}, u32[]{:S(2)}) copy-start(f32[2048]{0:T(1024)} %param.7) | copy-start | bytes 24580
  45.2 3.7 %collective-permute-start.9 = (f32[8,1,128]{2,1,0:T(1,128)S(1)}, f32[8,1,128]{2,1,0:T(1,128)S(1)}, u32[]{:S(2)}, u32[]{:S(2)}) collective-permute-start(f32[8,1,128]{2,1,0:T(1,128)S(1)} %get-tuple-element.102), channel_id=1, source_target_pairs={{0,1},{1,0},{2,3},{3,2},{4,5},{5,4},{6,7},{7,6},{8,9},{9,8},{10,11... | collective-permute-start | bytes 12296 | tf_op jit(solution)/shard_map/ppermute | solution.py:342
  48.9 5.5 %collective-permute-start.10 = (f32[8,1,128]{2,1,0:T(1,128)S(1)}, f32[8,1,128]{2,1,0:T(1,128)S(1)}, u32[]{:S(2)}, u32[]{:S(2)}) collective-permute-start(f32[8,1,128]{2,1,0:T(1,128)S(1)} %add.23.sa_ref), channel_id=1, source_target_pairs={{0,2},{1,3},{2,0},{3,1},{4,6},{5,7},{6,4},{7,5},{8,10},{9,11},{10,... | collective-permute-start | bytes 12296 | tf_op jit(solution)/shard_map/ppermute | solution.py:343

commit v5 on v4

v5 whole, which is shorter than its diff:
```python
import functools
import math

import jax
import jax.numpy as jnp
from jax import lax
from jax.experimental import pallas as pl
from jax.experimental.pallas import tpu as pltpu
from jax.sharding import PartitionSpec as P

QUERY_HEADS = 64
KEY_VALUE_HEADS = 8
D = 128
G = QUERY_HEADS // KEY_VALUE_HEADS
BLOCK = 128
STEP = 2
EPS = 1e-6
SCORE_SCALE = math.log2(math.e) / math.sqrt(D)

f32 = jnp.float32
bf = jnp.bfloat16
NT = (((1,), (1,)), ((), ()))
TN = (((0,), (0,)), ((), ()))


def split(x):
    hi = x.astype(bf)
    return hi, (x - hi.astype(f32)).astype(bf)


def lanes(*xs):
    return jnp.concatenate(xs, axis=1)


def rows(*xs):
    return jnp.concatenate(xs, axis=0)


def dot(a, b, dims=(((1,), (0,)), ((), ()))):
    return lax.dot_general(a, b, dims, preferred_element_type=f32)


def halves(x):
    return x[:, :D] + x[:, D:]


def params(mib):
    return pltpu.CompilerParams(
        vmem_limit_bytes=mib << 20, dimension_semantics=("arbitrary",)
    )


def state_body(
    k_ref, v_ref, q_hbm, before_ref, total_ref, tail_ref, kp_ref, vp_ref, q_ref, sem, *, ahead
):
    count = k_ref.shape[0]
    g = pl.program_id(0)
    fetch = pltpu.make_async_copy(q_hbm.at[pl.ds(ahead, q_ref.shape[0])], q_ref, sem)

    @pl.when(g == 0)
    def _():
        fetch.start()

    state = jnp.zeros((D, D), f32)
    for b in range(count // BLOCK):
        at = slice(b * BLOCK, (b + 1) * BLOCK)
        before_ref[b] = state
        k = k_ref[at, :]
        fh, fl = split(jnp.tanh(k))
        vv = lanes(*split(v_ref[at, :]))
        kp_ref[at, :] = lanes(*split(k * SCORE_SCALE), fh, fl)
        vp_ref[at, :] = vv
        state = state + halves(dot(rows(fh, fl), rows(vv, vv), TN))
    total_ref[...] = state
    tail_ref[:BLOCK] = k_ref[count - BLOCK :, :]
    tail_ref[BLOCK:] = v_ref[count - BLOCK :, :]

    @pl.when(g == pl.num_programs(0) - 1)
    def _():
        fetch.wait()


def local_states(queries, keys, values, ahead):
    count, width = keys.shape
    kv, nb = width // D, count // BLOCK
    one = pl.Squeezed()
    whole = lambda *shape: pl.BlockSpec((one, *shape), lambda g: (g,) + (0,) * len(shape))
    q_shape = (STEP * BLOCK, queries.shape[1])
    return pl.pallas_call(
        functools.partial(state_body, ahead=ahead * STEP * BLOCK),
        grid=(kv,),
        in_specs=[pl.BlockSpec((count, D), lambda g: (0, g))] * 2
        + [pl.BlockSpec(memory_space=pl.ANY)],
        out_specs=[
            whole(nb, D, D),
            whole(D, D),
            whole(2 * BLOCK, D),
            whole(count, 4 * D),
            whole(count, 2 * D),
            pl.BlockSpec(q_shape, lambda g: (0, 0)),
        ],
        out_shape=[
            pltpu.VMEM((kv, nb, D, D), f32),
            pltpu.VMEM((kv, D, D), f32),
            pltpu.VMEM((kv, 2 * BLOCK, D), f32),
            pltpu.VMEM((kv, count, 4 * D), bf),
            pltpu.VMEM((kv, count, 2 * D), bf),
            pltpu.VMEM(q_shape, f32),
        ],
        scratch_shapes=[pltpu.SemaphoreType.DMA(())],
        compiler_params=params(4),
        name="local_states",
    )(keys, values, queries)


def place():
    i = lax.axis_index("seq")
    return i // 8, (i // 2) % 4, i % 2


def chip_body(own_ref, other_ref, out_ref):
    core = place()[2]
    out_ref[...] = own_ref[core] + other_ref[core]


def row_body(own_ref, one_ref, two_ref, three_ref, sum_ref, before_ref):
    x = place()[1]
    got = [one_ref[...], two_ref[...], three_ref[...]]
    sum_ref[...] = own_ref[...] + got[0] + got[1] + got[2]
    before = jnp.zeros((D, D), f32)
    for by, state in enumerate(got, 1):
        before = before + jnp.where(x >= by, state, 0.0)
    before_ref[...] = before


def small_call(body, outs, name, *args):
    shape = jax.ShapeDtypeStruct((D, D), f32)
    return pl.pallas_call(
        body,
        out_shape=[shape] * outs,
        compiler_params=pltpu.CompilerParams(vmem_limit_bytes=2 << 20),
        name=name,
    )(*args)


def block_body(piece, ahead, carried, *refs):
    q_ref, kp_ref, vp_ref, *refs = refs
    if piece == 0:
        halo_ref, *refs = refs
    if ahead is not None:
        q_hbm, *refs = refs
    win_ref, lin_ref, fq_ref, *refs = refs[carried:]
    kv = kp_ref.shape[0]
    if ahead is not None:
        next_ref, sem = refs
        fetch = pltpu.make_async_copy(
            q_hbm.at[pl.ds(ahead * STEP * BLOCK, STEP * BLOCK)], next_ref, sem
        )
        fetch.start()
    row = lax.broadcasted_iota(jnp.int32, (BLOCK, BLOCK), 0)
    col = lax.broadcasted_iota(jnp.int32, (BLOCK, BLOCK), 1)
    own = rows(*[row >= col] * G)
    zero = jnp.zeros((BLOCK * G, BLOCK), bf)
    for j in range(STEP):
        block = piece * STEP + j
        tokens = slice(j * BLOCK, (j + 1) * BLOCK)
        here = slice(block * BLOCK, (block + 1) * BLOCK)
        there = slice((block - 1) * BLOCK, block * BLOCK)
        for g in range(kv):
            kh, kl = kp_ref[g, here, :D], kp_ref[g, here, D : 2 * D]
            fh, fl = kp_ref[g, here, 2 * D : 3 * D], kp_ref[g, here, 3 * D :]
            v_own = vp_ref[g, here, :]
            if block:
                ph, pl_ = kp_ref[g, there, :D], kp_ref[g, there, D : 2 * D]
                v_prior = vp_ref[g, there, :]
            else:
                ph, pl_ = split(halo_ref[g, :BLOCK] * SCORE_SCALE)
                v_prior = lanes(*split(halo_ref[g, BLOCK:]))
            kk = rows(lanes(kh, kh, kl, kl), lanes(ph, ph, pl_, pl_))
            ff = rows(lanes(fh, fh), lanes(fl, fl))
            v_both = rows(v_own, v_prior)
            heads = [slice(i * D, (i + 1) * D) for i in range(g * G, (g + 1) * G)]
            q = rows(*[q_ref[tokens, at] for at in heads])
            qh, ql = split(q)
            s = dot(lanes(qh, ql, qh, ql), kk, NT)
            f2 = lanes(*split(jnp.tanh(q)))
            fq_ref[j, g * G * BLOCK : (g + 1) * G * BLOCK, :] = f2
            a = jnp.where(own, halves(dot(f2, ff, NT)), 0.0)
            lin = halves(dot(lanes(*split(a)), rows(v_own, v_own)))
            before = s[:, BLOCK:]
            if block == 0:
                before = jnp.where(lax.axis_index("seq") > 0, before, -1e30)
            t = jnp.where(own, s[:, :BLOCK], before)
            p = jnp.exp2(t - jnp.max(t, axis=1, keepdims=True))
            total = jnp.sum(p, axis=1, keepdims=True)
            wh, wl = split(p)
            p4 = lanes(
                jnp.where(own, wh, zero),
                jnp.where(own, zero, wh),
                jnp.where(own, wl, zero),
                jnp.where(own, zero, wl),
            )
            win = halves(dot(p4, rows(v_both, v_both))) * (1.0 / total)
            for i, at in enumerate(heads):
                win_ref[tokens, at] = win[i * BLOCK : (i + 1) * BLOCK]
                lin_ref[tokens, at] = lin[i * BLOCK : (i + 1) * BLOCK]
    if ahead is not None:
        fetch.wait()


def block_part(piece, q, kp, vp, made, ahead=None, queries=None, halo=None):
    kv, count, _ = kp.shape
    nb = count // BLOCK
    width = q.shape[1]
    whole = lambda x: pl.BlockSpec(x.shape, lambda _: (0,) * x.ndim)
    args = [q, kp, vp]
    if halo is not None:
        args.append(halo)
    specs = [whole(x) for x in args]
    if ahead is not None:
        args.append(queries)
        specs.append(pl.BlockSpec(memory_space=pl.ANY))
    aliases = {len(args) + i: i for i in range(len(made))}
    big = pl.BlockSpec((STEP * BLOCK, width), lambda _: (piece, 0))
    out_specs = [big, big, pl.BlockSpec((STEP, kv * G * BLOCK, 2 * D), lambda _: (piece, 0, 0))]
    out_shape = [
        pltpu.VMEM((count, width), f32),
        pltpu.VMEM((count, width), f32),
        pltpu.VMEM((nb, kv * G * BLOCK, 2 * D), bf),
    ]
    scratch = []
    if ahead is not None:
        out_specs.append(whole(q))
        out_shape.append(pltpu.VMEM(q.shape, f32))
        scratch.append(pltpu.SemaphoreType.DMA(()))
    return pl.pallas_call(
        lambda *refs: block_body(piece, ahead, len(made), *refs),
        grid=(1,),
        in_specs=specs + [pl.BlockSpec(memory_space=pl.ANY)] * len(made),
        out_specs=out_specs,
        out_shape=out_shape,
        scratch_shapes=scratch,
        input_output_aliases=aliases,
        compiler_params=params(6),
        name=f"blocks_{piece}",
    )(*args, *made)


def linear_body(fq_ref, part_ref, inner_ref, mine_ref, their_ref, other_ref, lin_ref, sq_ref):
    core = place()[2]
    for j in range(STEP):
        tokens = slice(j * BLOCK, (j + 1) * BLOCK)
        sq = jnp.zeros((BLOCK, D), f32)
        for g in range(other_ref.shape[0]):
            state = jnp.where(core == g, mine_ref[...], their_ref[...])
            state = state + jnp.where(core == 1, other_ref[g], 0.0) + inner_ref[g, j]
            ss = lanes(*split(state))
            fq = fq_ref[j, g * G * BLOCK : (g + 1) * G * BLOCK, :]
            lin = halves(dot(fq, rows(ss, ss)))
            for i in range(G):
                at = slice((g * G + i) * D, (g * G + i + 1) * D)
                x = lin[i * BLOCK : (i + 1) * BLOCK] + part_ref[tokens, at]
                lin_ref[tokens, at] = x
                sq = sq + x * x
        sq_ref[j] = jnp.sum(sq.T, axis=0, keepdims=True)


def linear_part(fq, part, inner, mine, theirs, other):
    count, width = part.shape
    kv, nb = inner.shape[:2]
    big = pl.BlockSpec((STEP * BLOCK, width), lambda b: (b, 0))
    state = pl.BlockSpec((D, D), lambda b: (0, 0))
    return pl.pallas_call(
        linear_body,
        grid=(nb // STEP,),
        in_specs=[
            pl.BlockSpec((STEP,) + fq.shape[1:], lambda b: (b, 0, 0)),
            big,
            pl.BlockSpec((kv, STEP, D, D), lambda b: (0, b, 0, 0)),
            state,
            state,
            pl.BlockSpec((kv, D, D), lambda b: (0, 0, 0)),
        ],
        out_specs=[big, pl.BlockSpec((STEP, 1, BLOCK), lambda b: (b, 0, 0))],
        out_shape=[
            pltpu.VMEM((count, width), f32),
            pltpu.VMEM((nb, 1, BLOCK), f32),
        ],
        compiler_params=params(4),
        name="linear",
    )(fq, part, inner, mine, theirs, other)


def combine_body(lin_ref, win_ref, sa_ref, sb_ref, gain_ref, out_ref):
    for r in range(lin_ref.shape[0] // BLOCK):
        ms = (sa_ref[r] + sb_ref[r]) * (1.0 / (QUERY_HEADS * D))
        inv = jnp.broadcast_to(lax.rsqrt(ms + EPS), (BLOCK, BLOCK)).T
        row = slice(r * BLOCK, (r + 1) * BLOCK)
        for i in range(lin_ref.shape[1] // D):
            at = slice(i * D, (i + 1) * D)
            out_ref[row, at] = lin_ref[row, at] * inv * gain_ref[:, at] + win_ref[row, at]


def combine(lin, win, sa, sb, gain):
    count, width = lin.shape
    n = 2
    big = pl.BlockSpec((n * BLOCK, width), lambda j: (j, 0))
    small = pl.BlockSpec((n, 1, BLOCK), lambda j: (j, 0, 0))
    return pl.pallas_call(
        combine_body,
        grid=(count // (n * BLOCK),),
        in_specs=[big, big, small, small, pl.BlockSpec((1, width), lambda j: (0, 0))],
        out_specs=big,
        out_shape=jax.ShapeDtypeStruct((count, width), f32),
        compiler_params=params(6),
        name="combine",
    )(lin, win, sa, sb, gain)


def shift_x(by):
    return [(i, i // 8 * 8 + (i + 2 * by) % 8) for i in range(32)]


def down_from(y):
    return [(y * 8 + i, (y + 1) * 8 + i) for i in range(8)]


SWAP = [(i, i ^ 1) for i in range(32)]


def shards(queries, keys, values, gain):
    count = queries.shape[0]
    nb = count // BLOCK
    heads = lax.axis_size("head")
    assert heads == 4 and nb == 8 and lax.axis_size("seq") == 32
    queries, keys, values = (
        pltpu.with_memory_space_constraint(x, pltpu.HBM) for x in (queries, keys, values)
    )

    def move(x, pairs):
        return lax.ppermute(x, "seq", pairs)

    def tie(*xs):
        return lax.optimization_barrier(xs)

    order = (1, 2, 3, 0)
    inner, total, tail, kp, vp, q = local_states(queries, keys, values, order[0])
    other = move(total, SWAP)
    (chip,) = small_call(chip_body, 1, "chip_sum", total, other)
    along_x = [move(chip, shift_x(by)) for by in (1, 2, 3)]
    halo = move(tail, [(i, i + 1) for i in range(31)])
    *made, q = block_part(order[0], q, kp, vp, (), order[1], queries)
    *made, one, two, three = tie(*made, *along_x)
    row, mine = small_call(row_body, 2, "row_sum", chip, one, two, three)
    for y in range(3):
        got = move(row, down_from(y))
        *made, mine = tie(*made, mine)
        if y < 2:
            *made, q = block_part(order[y + 1], q, kp, vp, made, order[y + 2], queries)
        else:
            made = block_part(0, q, kp, vp, made, halo=halo)
        *made, got = tie(*made, got)
        row, mine = row + got, mine + got
    theirs = move(mine, SWAP)
    win, part, fq = made
    lin, sq = linear_part(fq, part, inner, mine, theirs, other)
    sq = sq + lax.ppermute(sq, "head", [(i, i ^ 1) for i in range(heads)])
    across = lax.ppermute(sq, "head", [(i, heads - 1 - i) for i in range(heads)])
    return combine(lin, win, sq, across, gain[None, :])


def solution(mesh):
    in_specs = (P("seq", "head"), P("seq", "head"), P("seq", "head"), P("head"))
    return jax.shard_map(
        shards, mesh=mesh, in_specs=in_specs, out_specs=P("seq", "head"), check_vma=False
    )
```

time: 58.6 us -> 55.6 us (0.949)
  Pallas kernels: 33.2 us -> 29.7 us
    pallas_call x6, Pallas kernels: 29.2 us -> 25.6 us  [the longest x4 19 us: block_part(): pl.pallas_call(lambda *refs: block_body(piece, ahead, len(made), *refs),...]
  transfers between devices with their start and end apart: 11 -> 11, of which waited for: 4 -> 4; matrix products, arithmetic and copies ran while one was open for 0% -> 0% of each run, Pallas kernels for 39% -> 34%
where the time goes in v5:
time: 55.6 us; the launch traced here: 55.1 us
  Pallas kernels  29.7 us (53%)
  starting transfers between devices  19.6 us (35%)
  waiting for transfers between devices  5.52 us (10%)
    pallas_call x4, Pallas kernels, block_part(): pl.pallas_call(lambda *refs: block_body(piece, ahead, len(made), *refs),...  19 us
    ppermute x9, starting transfers between devices, move(): return lax.ppermute(x, 'seq', pairs)  13.6 us
    pallas_call x1, Pallas kernels, combine(): pl.pallas_call(combine_body, grid=(count // (n * BLOCK),), in_specs=[big,...  4.05 us
    ppermute x1, starting transfers between devices, shards(): lax.ppermute(sq, 'head', [(i, heads - 1 - i) for i in range(heads)])  4.05 us
    pallas_call x1, Pallas kernels, linear_part(): pl.pallas_call(linear_body, grid=(nb // STEP,), in_specs=[pl.BlockSpec((S...  3.56 us
    pallas_call x1, Pallas kernels, local_states(): pl.pallas_call(functools.partial(state_body, ahead=ahead * STEP * BLOCK),...  3.05 us
    ppermute x9, waiting for transfers between devices, move(): return lax.ppermute(x, 'seq', pairs)  2.26 us
    ppermute x1, starting transfers between devices, shards(): sq = sq + lax.ppermute(sq, 'head', [(i, i ^ 1) for i in range(heads)])  2 us
  transfers between devices with their start and end apart: 11, of which 4 were waited for; matrix products, arithmetic and copies ran while one was open for 0% of the time, Pallas kernels for 34%

profile of v5, /device:TPU:0, one launch (start us, length us, event | category | flops | bytes accessed | tf_op | source)
XLA Modules:
  0.0 55.1 jit_solution(15142391346709428956)
XLA Ops:
  0.0 3.0 %local_states.1 = (f32[2,8,128,128]{3,2,1,0:T(8,128)S(1)}, f32[2,128,128]{2,1,0:T(8,128)S(1)}, f32[2,256,128]{2,1,0:T(8,128)S(1)}, bf16[2,1024,512]{2,1,0:T(8,12...) custom-call(f32[1024,256]{1,0:T(8,128)} %k_ref.1, f32[1024,256]{1,0:T(8,128)} %v_ref.1, ...), custom_call_target="tpu_custom_call" | custom-call | tf_op jit(solution)/shard_map/local_states/pallas_call | solution.py:89
  3.1 0.1 collective-permute-start
  3.1 1.3 %collective-permute-done.other_ref = f32[2,128,128]{2,1,0:T(8,128)S(1)} collective-permute-done((f32[2,128,128]{2,1,0:T(8,128)S(1)}, f32[2,128,128]{2,1,0:T(8,128)S(1)}, u32[]{:S(2)}, u32[]{:S(2)}) %collective-permute-start) | collective-permute-done | bytes 131104 | tf_op jit(solution)/shard_map/ppermute | solution.py:341
  4.5 2.9 %collective-permute-start.3 = (f32[128,128]{1,0:T(8,128)S(1)}, f32[128,128]{1,0:T(8,128)S(1)}, u32[]{:S(2)}, u32[]{:S(2)}) collective-permute-start(f32[128,128]{1,0:T(8,128)S(1)} %chip_sum.1.own_ref), channel_id=1, source_target_pairs={{0,24},{4,28},{8,0},{12,4},{16,8},{20,12},{24,16},{28,20},{32,56},... | collective-permute-start | bytes 196616 | tf_op jit(solution)/shard_map/ppermute | solution.py:341
  7.4 0.8 %collective-permute-start.2 = (f32[128,128]{1,0:T(8,128)S(1)}, f32[128,128]{1,0:T(8,128)S(1)}, u32[]{:S(2)}, u32[]{:S(2)}) collective-permute-start(f32[128,128]{1,0:T(8,128)S(1)} %chip_sum.1.own_ref), channel_id=1, source_target_pairs={{0,16},{4,20},{8,24},{12,28},{16,0},{20,4},{24,8},{28,12},{32,48},... | collective-permute-start | bytes 196616 | tf_op jit(solution)/shard_map/ppermute | solution.py:341
  8.2 0.9 %collective-permute-start.1 = (f32[128,128]{1,0:T(8,128)S(1)}, f32[128,128]{1,0:T(8,128)S(1)}, u32[]{:S(2)}, u32[]{:S(2)}) collective-permute-start(f32[128,128]{1,0:T(8,128)S(1)} %chip_sum.1.own_ref), channel_id=1, source_target_pairs={{0,8},{4,12},{8,16},{12,20},{16,24},{20,28},{24,0},{28,4},{32,40},... | collective-permute-start | bytes 196616 | tf_op jit(solution)/shard_map/ppermute | solution.py:341
  9.1 5.1 %blocks_1.1 = (f32[1024,2048]{1,0:T(8,128)S(1)}, f32[1024,2048]{1,0:T(8,128)S(1)}, bf16[8,2048,256]{2,1,0:T(8,128)(2,1)S(1)}, f32[256,2048]{1,0:T(8,128)S(1)}) custom-call(f32[256,2048]{1,0:T(8,128)S(1)} %get-tuple-element.60.refs_0_, bf16[2,1024,512]{2,1,0:T(8,128)(2,1)S(1)} %get-tuple-element.61.refs_1_, ...), custom_call_target="tpu_custom_call" | custom-call | tf_op jit(solution)/shard_map/blocks_1/pallas_call | solution.py:236
  14.2 0.0 collective-permute-done.3.three_ref
  14.2 0.0 collective-permute-done.2.two_ref
  14.2 0.0 collective-permute-done.1.one_ref
  14.3 3.5 %collective-permute-start.4 = (f32[128,128]{1,0:T(8,128)S(1)}, f32[128,128]{1,0:T(8,128)S(1)}, u32[]{:S(2)}, u32[]{:S(2)}) collective-permute-start(f32[128,128]{1,0:T(8,128)S(1)} %get-tuple-element.82), channel_id=1, source_target_pairs={{0,32},{4,36},{8,40},{12,44},{16,48},{20,52},{24,56},{28,60},{1,33... | collective-permute-start | bytes 196616 | tf_op jit(solution)/shard_map/ppermute | solution.py:341
  17.8 5.1 %blocks_2.1 = (f32[1024,2048]{1,0:T(8,128)S(1)}, f32[1024,2048]{1,0:T(8,128)S(1)}, bf16[8,2048,256]{2,1,0:T(8,128)(2,1)S(1)}, f32[256,2048]{1,0:T(8,128)S(1)}) custom-call(f32[256,2048]{1,0:T(8,128)S(1)} %get-tuple-element.63.refs_0_, ...), custom_call_target="tpu_custom_call", output_to_operand_aliasing={{0}: (4, {}), {1}: (5, {}), {2}: (6, {})} | custom-call | tf_op jit(solution)/shard_map/blocks_2/pallas_call | solution.py:236
  22.9 0.0 collective-permute-done.4
  22.9 0.7 %collective-permute-start.6 = (f32[128,128]{1,0:T(8,128)S(1)}, f32[128,128]{1,0:T(8,128)S(1)}, u32[]{:S(2)}, u32[]{:S(2)}) collective-permute-start(f32[128,128]{1,0:T(8,128)S(1)} %get-tuple-element.117), channel_id=1, source_target_pairs={{32,64},{36,68},{40,72},{44,76},{48,80},{52,84},{56,88},{60,92},{3... | collective-permute-start | bytes 196616 | tf_op jit(solution)/shard_map/ppermute | solution.py:341
  23.6 1.5 %collective-permute-start.5 = (f32[2,256,128]{2,1,0:T(8,128)S(1)}, f32[2,256,128]{2,1,0:T(8,128)S(1)}, u32[]{:S(2)}, u32[]{:S(2)}) collective-permute-start(f32[2,256,128]{2,1,0:T(8,128)S(1)} %get-tuple-element.92), channel_id=1, source_target_pairs={{0,4},{4,8},{8,12},{12,16},{16,20},{20,24},{24,28},{28,32},{32,36}... | collective-permute-start | bytes 786440 | tf_op jit(solution)/shard_map/ppermute | solution.py:341
  25.1 5.1 %blocks_3.1 = (f32[1024,2048]{1,0:T(8,128)S(1)}, f32[1024,2048]{1,0:T(8,128)S(1)}, bf16[8,2048,256]{2,1,0:T(8,128)(2,1)S(1)}, f32[256,2048]{1,0:T(8,128)S(1)}) custom-call(f32[256,2048]{1,0:T(8,128)S(1)} %get-tuple-element.78.refs_0_, ...), custom_call_target="tpu_custom_call", output_to_operand_aliasing={{0}: (4, {}), {1}: (5, {}), {2}: (6, {})} | custom-call | tf_op jit(solution)/shard_map/blocks_3/pallas_call | solution.py:236
  30.2 0.0 collective-permute-done.6
  30.2 0.7 %collective-permute-start.7 = (f32[128,128]{1,0:T(8,128)S(1)}, f32[128,128]{1,0:T(8,128)S(1)}, u32[]{:S(2)}, u32[]{:S(2)}) collective-permute-start(f32[128,128]{1,0:T(8,128)S(1)} %get-tuple-element.115), channel_id=1, source_target_pairs={{64,96},{68,100},{72,104},{76,108},{80,112},{84,116},{88,120},{92,... | collective-permute-start | bytes 196616 | tf_op jit(solution)/shard_map/ppermute | solution.py:341
  30.9 0.0 collective-permute-done.5.refs_3_
  30.9 3.7 %blocks_0.1 = (f32[1024,2048]{1,0:T(8,128)S(1)}, f32[1024,2048]{1,0:T(8,128)S(1)}, bf16[8,2048,256]{2,1,0:T(8,128)(2,1)S(1)}) custom-call(f32[256,2048]{1,0:T(8,128)S(1)} %get-tuple-element.91.refs_0_, bf16[2,1024,512]{2,1,0:T(8,128)(2,1)S(1)} %get-tuple-element.61.refs_1_, ...), custom_call_target="tpu_custom_call", output_to_operand_aliasing={{0}: (4, {}), {1}: (5, {}), {2}: (6, {})} | custom-call | tf_op jit(solution)/shard_map/blocks_0/pallas_call | solution.py:236
  34.6 0.0 collective-permute-done.7
  34.7 2.6 %collective-permute-start.8 = (f32[128,128]{1,0:T(8,128)S(1)}, f32[128,128]{1,0:T(8,128)S(1)}, u32[]{:S(2)}, u32[]{:S(2)}) collective-permute-start(f32[128,128]{1,0:T(8,128)S(1)} %add.22.mine_ref), channel_id=1, source_target_pairs={{0,4},{4,0},{8,12},{12,8},{16,20},{20,16},{24,28},{28,24},{32,36},... | collective-permute-start | bytes 196616 | tf_op jit(solution)/shard_map/ppermute | solution.py:341
  37.2 0.9 %collective-permute-done.8.their_ref = f32[128,128]{1,0:T(8,128)S(1)} collective-permute-done((f32[128,128]{1,0:T(8,128)S(1)}, f32[128,128]{1,0:T(8,128)S(1)}, u32[]{:S(2)}, u32[]{:S(2)}) %collective-permute-start.8) | collective-permute-done | bytes 65568 | tf_op jit(solution)/shard_map/ppermute | solution.py:341
  38.1 0.0 copy-start
  38.2 3.6 %linear.1 = (f32[1024,2048]{1,0:T(8,128)S(1)}, f32[8,1,128]{2,1,0:T(1,128)S(1)}) custom-call(bf16[8,2048,256]{2,1,0:T(8,128)(2,1)S(1)} %get-tuple-element.107.fq_ref, f32[1024,2048]{1,0:T(8,128)S(1)} %get-tuple-element.108.part_ref, f32[2,8,128,128]{3,2,1,0:T(8,128)S(1)} %get-tuple-element.109.inner_ref, f32[128,128]{1,0:T(8,128)S(1)} %add.22.mine_ref, ...), custom_call_target="tpu_custom_call" | custom-call | tf_op jit(solution)/shard_map/linear/pallas_call | solution.py:273
  41.7 2.0 %collective-permute-start.9 = (f32[8,1,128]{2,1,0:T(1,128)S(1)}, f32[8,1,128]{2,1,0:T(1,128)S(1)}, u32[]{:S(2)}, u32[]{:S(2)}) collective-permute-start(f32[8,1,128]{2,1,0:T(1,128)S(1)} %get-tuple-element.114), channel_id=1, source_target_pairs={{0,1},{1,0},{2,3},{3,2},{4,5},{5,4},{6,7},{7,6},{8,9},{9,8},{10,11... | collective-permute-start | bytes 12296 | tf_op jit(solution)/shard_map/ppermute | solution.py:367
  43.7 1.7 %collective-permute-done.9 = f32[8,1,128]{2,1,0:T(1,128)S(1)} collective-permute-done((f32[8,1,128]{2,1,0:T(1,128)S(1)}, f32[8,1,128]{2,1,0:T(1,128)S(1)}, u32[]{:S(2)}, u32[]{:S(2)}) %collective-permute-start.9) | collective-permute-done | bytes 4128 | tf_op jit(solution)/shard_map/ppermute | solution.py:367
  45.4 4.1 %collective-permute-start.10 = (f32[8,1,128]{2,1,0:T(1,128)S(1)}, f32[8,1,128]{2,1,0:T(1,128)S(1)}, u32[]{:S(2)}, u32[]{:S(2)}) collective-permute-start(f32[8,1,128]{2,1,0:T(1,128)S(1)} %add.23.sa_ref), channel_id=1, source_target_pairs={{0,3},{1,2},{2,1},{3,0},{4,7},{5,6},{6,5},{7,4},{8,11},{9,10},{10,... | collective-permute-start | bytes 12296 | tf_op jit(solution)/shard_map/ppermute | solution.py:368
  49.5 1.6 %collective-permute-done.10.sb_ref = f32[8,1,128]{2,1,0:T(1,128)S(1)} collective-permute-done((f32[8,1,128]{2,1,0:T(1,128)S(1)}, f32[8,1,128]{2,1,0:T(1,128)S(1)}, u32[]{:S(2)}, u32[]{:S(2)}) %collective-permute-start.10) | collective-permute-done | bytes 4128 | tf_op jit(solution)/shard_map/ppermute | solution.py:368
  51.0 0.0 copy-done
  51.0 4.1 %combine.1 = f32[1024,2048]{1,0:T(8,128)} custom-call(f32[1024,2048]{1,0:T(8,128)S(1)} %get-tuple-element.112.lin_ref, f32[1024,2048]{1,0:T(8,128)S(1)} %get-tuple-element.113.win_ref, f32[8,1,128]{2,1,0:T(1,128)S(1)} %add.23.sa_ref, f32[8,1,128]{2,1,0:T(1,128)S(1)} %collective-permute-done.10.sb_ref, f32[1,2048]{1,0:T(1,128)S(1)} %bitcast.1), custom_call_target="tpu_custom_call" | custom-call | tf_op jit(solution)/shard_map/combine/pallas_call | solution.py:309
  (6 shorter events, 0.1 us)
Async XLA Ops:
  3.1 1.4 %collective-permute-start = (f32[2,128,128]{2,1,0:T(8,128)S(1)}, f32[2,128,128]{2,1,0:T(8,128)S(1)}, u32[]{:S(2)}, u32[]{:S(2)}) collective-permute-start(f32[2,128,128]{2,1,0:T(8,128)S(1)} %get-tuple-element.67.own_ref), channel_id=1, source_target_pairs={{0,4},{4,0},{8,12},{12,8},{16,20},{20,16},{24,28},{28,24},{32,36},... | collective-permute-start | bytes 393224 | tf_op jit(solution)/shard_map/ppermute | solution.py:341
  4.5 9.7 %collective-permute-start.3 = (f32[128,128]{1,0:T(8,128)S(1)}, f32[128,128]{1,0:T(8,128)S(1)}, u32[]{:S(2)}, u32[]{:S(2)}) collective-permute-start(f32[128,128]{1,0:T(8,128)S(1)} %chip_sum.1.own_ref), channel_id=1, source_target_pairs={{0,24},{4,28},{8,0},{12,4},{16,8},{20,12},{24,16},{28,20},{32,56},... | collective-permute-start | bytes 196616 | tf_op jit(solution)/shard_map/ppermute | solution.py:341
  7.4 6.8 %collective-permute-start.2 = (f32[128,128]{1,0:T(8,128)S(1)}, f32[128,128]{1,0:T(8,128)S(1)}, u32[]{:S(2)}, u32[]{:S(2)}) collective-permute-start(f32[128,128]{1,0:T(8,128)S(1)} %chip_sum.1.own_ref), channel_id=1, source_target_pairs={{0,16},{4,20},{8,24},{12,28},{16,0},{20,4},{24,8},{28,12},{32,48},... | collective-permute-start | bytes 196616 | tf_op jit(solution)/shard_map/ppermute | solution.py:341
  8.2 6.0 %collective-permute-start.1 = (f32[128,128]{1,0:T(8,128)S(1)}, f32[128,128]{1,0:T(8,128)S(1)}, u32[]{:S(2)}, u32[]{:S(2)}) collective-permute-start(f32[128,128]{1,0:T(8,128)S(1)} %chip_sum.1.own_ref), channel_id=1, source_target_pairs={{0,8},{4,12},{8,16},{12,20},{16,24},{20,28},{24,0},{28,4},{32,40},... | collective-permute-start | bytes 196616 | tf_op jit(solution)/shard_map/ppermute | solution.py:341
  14.3 8.6 %collective-permute-start.4 = (f32[128,128]{1,0:T(8,128)S(1)}, f32[128,128]{1,0:T(8,128)S(1)}, u32[]{:S(2)}, u32[]{:S(2)}) collective-permute-start(f32[128,128]{1,0:T(8,128)S(1)} %get-tuple-element.82), channel_id=1, source_target_pairs={{0,32},{4,36},{8,40},{12,44},{16,48},{20,52},{24,56},{28,60},{1,33... | collective-permute-start | bytes 196616 | tf_op jit(solution)/shard_map/ppermute | solution.py:341
  22.9 7.3 %collective-permute-start.6 = (f32[128,128]{1,0:T(8,128)S(1)}, f32[128,128]{1,0:T(8,128)S(1)}, u32[]{:S(2)}, u32[]{:S(2)}) collective-permute-start(f32[128,128]{1,0:T(8,128)S(1)} %get-tuple-element.117), channel_id=1, source_target_pairs={{32,64},{36,68},{40,72},{44,76},{48,80},{52,84},{56,88},{60,92},{3... | collective-permute-start | bytes 196616 | tf_op jit(solution)/shard_map/ppermute | solution.py:341
  23.6 7.3 %collective-permute-start.5 = (f32[2,256,128]{2,1,0:T(8,128)S(1)}, f32[2,256,128]{2,1,0:T(8,128)S(1)}, u32[]{:S(2)}, u32[]{:S(2)}) collective-permute-start(f32[2,256,128]{2,1,0:T(8,128)S(1)} %get-tuple-element.92), channel_id=1, source_target_pairs={{0,4},{4,8},{8,12},{12,16},{16,20},{20,24},{24,28},{28,32},{32,36}... | collective-permute-start | bytes 786440 | tf_op jit(solution)/shard_map/ppermute | solution.py:341
  30.2 4.4 %collective-permute-start.7 = (f32[128,128]{1,0:T(8,128)S(1)}, f32[128,128]{1,0:T(8,128)S(1)}, u32[]{:S(2)}, u32[]{:S(2)}) collective-permute-start(f32[128,128]{1,0:T(8,128)S(1)} %get-tuple-element.115), channel_id=1, source_target_pairs={{64,96},{68,100},{72,104},{76,108},{80,112},{84,116},{88,120},{92,... | collective-permute-start | bytes 196616 | tf_op jit(solution)/shard_map/ppermute | solution.py:341
  34.7 3.5 %collective-permute-start.8 = (f32[128,128]{1,0:T(8,128)S(1)}, f32[128,128]{1,0:T(8,128)S(1)}, u32[]{:S(2)}, u32[]{:S(2)}) collective-permute-start(f32[128,128]{1,0:T(8,128)S(1)} %add.22.mine_ref), channel_id=1, source_target_pairs={{0,4},{4,0},{8,12},{12,8},{16,20},{20,16},{24,28},{28,24},{32,36},... | collective-permute-start | bytes 196616 | tf_op jit(solution)/shard_map/ppermute | solution.py:341
  38.1 12.9 %copy-start = (f32[2048]{0:T(1024)S(1)}, f32[2048]{0:T(1024)}, u32[]{:S(2)}) copy-start(f32[2048]{0:T(1024)} %param.7) | copy-start | bytes 24580
  41.7 3.7 %collective-permute-start.9 = (f32[8,1,128]{2,1,0:T(1,128)S(1)}, f32[8,1,128]{2,1,0:T(1,128)S(1)}, u32[]{:S(2)}, u32[]{:S(2)}) collective-permute-start(f32[8,1,128]{2,1,0:T(1,128)S(1)} %get-tuple-element.114), channel_id=1, source_target_pairs={{0,1},{1,0},{2,3},{3,2},{4,5},{5,4},{6,7},{7,6},{8,9},{9,8},{10,11... | collective-permute-start | bytes 12296 | tf_op jit(solution)/shard_map/ppermute | solution.py:367
  45.4 5.6 %collective-permute-start.10 = (f32[8,1,128]{2,1,0:T(1,128)S(1)}, f32[8,1,128]{2,1,0:T(1,128)S(1)}, u32[]{:S(2)}, u32[]{:S(2)}) collective-permute-start(f32[8,1,128]{2,1,0:T(1,128)S(1)} %add.23.sa_ref), channel_id=1, source_target_pairs={{0,3},{1,2},{2,1},{3,0},{4,7},{5,6},{6,5},{7,4},{8,11},{9,10},{10,... | collective-permute-start | bytes 12296 | tf_op jit(solution)/shard_map/ppermute | solution.py:368

commit v6 on v5

--- a/solution.py
+++ b/solution.py
@@ -14,6 +14,7 @@
 G = QUERY_HEADS // KEY_VALUE_HEADS
 BLOCK = 128
 STEP = 2
+WIDE = 4
 EPS = 1e-6
 SCORE_SCALE = math.log2(math.e) / math.sqrt(D)
 
@@ -51,15 +52,21 @@
 
 
 def state_body(
-    k_ref, v_ref, q_hbm, before_ref, total_ref, tail_ref, kp_ref, vp_ref, q_ref, sem, *, ahead
+    k_ref, v_ref, q_hbm, before_ref, total_ref, tail_ref, kp_ref, vp_ref, q_ref, sems, *, ahead
 ):
     count = k_ref.shape[0]
     g = pl.program_id(0)
-    fetch = pltpu.make_async_copy(q_hbm.at[pl.ds(ahead, q_ref.shape[0])], q_ref, sem)
+
+    def fetch(j):
+        to = pl.ds(pl.multiple_of(j * BLOCK, BLOCK), BLOCK)
+        at = pl.ds(pl.multiple_of((ahead * STEP + j) * BLOCK, BLOCK), BLOCK)
+        return pltpu.make_async_copy(q_hbm.at[at], q_ref.at[to], sems.at[j])
 
     @pl.when(g == 0)
     def _():
-        fetch.start()
+        @pl.loop(0, STEP)
+        def _(j):
+            fetch(j).start()
 
     state = jnp.zeros((D, D), f32)
     for b in range(count // BLOCK):
@@ -77,7 +84,8 @@
 
     @pl.when(g == pl.num_programs(0) - 1)
     def _():
-        fetch.wait()
+        for j in range(STEP):
+            fetch(j).wait()
 
 
 def local_states(queries, keys, values, ahead):
@@ -87,7 +95,7 @@
     whole = lambda *shape: pl.BlockSpec((one, *shape), lambda g: (g,) + (0,) * len(shape))
     q_shape = (STEP * BLOCK, queries.shape[1])
     return pl.pallas_call(
-        functools.partial(state_body, ahead=ahead * STEP * BLOCK),
+        functools.partial(state_body, ahead=ahead),
         grid=(kv,),
         in_specs=[pl.BlockSpec((count, D), lambda g: (0, g))] * 2
         + [pl.BlockSpec(memory_space=pl.ANY)],
@@ -97,7 +105,7 @@
             whole(2 * BLOCK, D),
             whole(count, 4 * D),
             whole(count, 2 * D),
-            pl.BlockSpec(q_shape, lambda g: (0, 0)),
+            pl.BlockSpec(memory_space=pl.ANY),
         ],
         out_shape=[
             pltpu.VMEM((kv, nb, D, D), f32),
@@ -107,7 +115,7 @@
             pltpu.VMEM((kv, count, 2 * D), bf),
             pltpu.VMEM(q_shape, f32),
         ],
-        scratch_shapes=[pltpu.SemaphoreType.DMA(())],
+        scratch_shapes=[pltpu.SemaphoreType.DMA((STEP,))],
         compiler_params=params(4),
         name="local_states",
     )(keys, values, queries)
@@ -152,11 +160,17 @@
     win_ref, lin_ref, fq_ref, *refs = refs[carried:]
     kv = kp_ref.shape[0]
     if ahead is not None:
-        next_ref, sem = refs
-        fetch = pltpu.make_async_copy(
-            q_hbm.at[pl.ds(ahead * STEP * BLOCK, STEP * BLOCK)], next_ref, sem
-        )
-        fetch.start()
+        next_ref, sems = refs
+
+        def fetch(j):
+            to = pl.ds(pl.multiple_of(j * BLOCK, BLOCK), BLOCK)
+            at = pl.ds(pl.multiple_of((ahead * STEP + j) * BLOCK, BLOCK), BLOCK)
+            return pltpu.make_async_copy(q_hbm.at[at], next_ref.at[to], sems.at[j])
+
+        @pl.loop(0, STEP)
+        def _(j):
+            fetch(j).start()
+
     row = lax.broadcasted_iota(jnp.int32, (BLOCK, BLOCK), 0)
     col = lax.broadcasted_iota(jnp.int32, (BLOCK, BLOCK), 1)
     own = rows(*[row >= col] * G)
@@ -205,7 +219,8 @@
                 win_ref[tokens, at] = win[i * BLOCK : (i + 1) * BLOCK]
                 lin_ref[tokens, at] = lin[i * BLOCK : (i + 1) * BLOCK]
     if ahead is not None:
-        fetch.wait()
+        for j in range(STEP):
+            fetch(j).wait()
 
 
 def block_part(piece, q, kp, vp, made, ahead=None, queries=None, halo=None):
@@ -230,9 +245,9 @@
     ]
     scratch = []
     if ahead is not None:
-        out_specs.append(whole(q))
+        out_specs.append(pl.BlockSpec(memory_space=pl.ANY))
         out_shape.append(pltpu.VMEM(q.shape, f32))
-        scratch.append(pltpu.SemaphoreType.DMA(()))
+        scratch.append(pltpu.SemaphoreType.DMA((STEP,)))
     return pl.pallas_call(
         lambda *refs: block_body(piece, ahead, len(made), *refs),
         grid=(1,),
@@ -248,7 +263,7 @@
 
 def linear_body(fq_ref, part_ref, inner_ref, mine_ref, their_ref, other_ref, lin_ref, sq_ref):
     core = place()[2]
-    for j in range(STEP):
+    for j in range(WIDE):
         tokens = slice(j * BLOCK, (j + 1) * BLOCK)
         sq = jnp.zeros((BLOCK, D), f32)
         for g in range(other_ref.shape[0]):
@@ -268,53 +283,64 @@
 def linear_part(fq, part, inner, mine, theirs, other):
     count, width = part.shape
     kv, nb = inner.shape[:2]
-    big = pl.BlockSpec((STEP * BLOCK, width), lambda b: (b, 0))
+    big = pl.BlockSpec((WIDE * BLOCK, width), lambda b: (b, 0))
     state = pl.BlockSpec((D, D), lambda b: (0, 0))
     return pl.pallas_call(
         linear_body,
-        grid=(nb // STEP,),
+        grid=(nb // WIDE,),
         in_specs=[
-            pl.BlockSpec((STEP,) + fq.shape[1:], lambda b: (b, 0, 0)),
+            pl.BlockSpec((WIDE,) + fq.shape[1:], lambda b: (b, 0, 0)),
             big,
-            pl.BlockSpec((kv, STEP, D, D), lambda b: (0, b, 0, 0)),
+            pl.BlockSpec((kv, WIDE, D, D), lambda b: (0, b, 0, 0)),
             state,
             state,
             pl.BlockSpec((kv, D, D), lambda b: (0, 0, 0)),
         ],
-        out_specs=[big, pl.BlockSpec((STEP, 1, BLOCK), lambda b: (b, 0, 0))],
+        out_specs=[big, pl.BlockSpec((WIDE, 1, BLOCK), lambda b: (b, 0, 0))],
         out_shape=[
             pltpu.VMEM((count, width), f32),
             pltpu.VMEM((nb, 1, BLOCK), f32),
         ],
-        compiler_params=params(4),
+        compiler_params=params(6),
         name="linear",
     )(fq, part, inner, mine, theirs, other)
 
 
-def combine_body(lin_ref, win_ref, sa_ref, sb_ref, gain_ref, out_ref):
-    for r in range(lin_ref.shape[0] // BLOCK):
-        ms = (sa_ref[r] + sb_ref[r]) * (1.0 / (QUERY_HEADS * D))
+def combine_body(lin_ref, win_ref, s0, s1, s2, s3, gain_ref, out_hbm, out_ref, sems):
+    def send(b):
+        row = pl.ds(pl.multiple_of(b * BLOCK, BLOCK), BLOCK)
+        return row, pltpu.make_async_copy(out_ref.at[row], out_hbm.at[row], sems.at[b])
+
+    @pl.loop(0, s0.shape[0])
+    def _(b):
+        ms = ((s0[b] + s1[b]) + (s2[b] + s3[b])) * (1.0 / (QUERY_HEADS * D))
         inv = jnp.broadcast_to(lax.rsqrt(ms + EPS), (BLOCK, BLOCK)).T
-        row = slice(r * BLOCK, (r + 1) * BLOCK)
+        row, copy = send(b)
         for i in range(lin_ref.shape[1] // D):
             at = slice(i * D, (i + 1) * D)
             out_ref[row, at] = lin_ref[row, at] * inv * gain_ref[:, at] + win_ref[row, at]
-
-
-def combine(lin, win, sa, sb, gain):
-    count, width = lin.shape
-    n = 2
-    big = pl.BlockSpec((n * BLOCK, width), lambda j: (j, 0))
-    small = pl.BlockSpec((n, 1, BLOCK), lambda j: (j, 0, 0))
+        copy.start()
+
+    @pl.loop(0, s0.shape[0])
+    def _(b):
+        send(b)[1].wait()
+
+
+def combine(lin, win, squares, gain):
+    args = [lin, win, *squares, gain]
     return pl.pallas_call(
         combine_body,
-        grid=(count // (n * BLOCK),),
-        in_specs=[big, big, small, small, pl.BlockSpec((1, width), lambda j: (0, 0))],
-        out_specs=big,
-        out_shape=jax.ShapeDtypeStruct((count, width), f32),
-        compiler_params=params(6),
+        grid=(1,),
+        in_specs=[pl.BlockSpec(x.shape, lambda _, x=x: (0,) * x.ndim) for x in args],
+        out_specs=pl.BlockSpec(memory_space=pl.ANY),
+        out_shape=pltpu.HBM(lin.shape, f32),
+        scratch_shapes=[
+            pltpu.VMEM(lin.shape, f32),
+            pltpu.SemaphoreType.DMA((squares[0].shape[0],)),
+        ],
+        compiler_params=params(10),
         name="combine",
-    )(lin, win, sa, sb, gain)
+    )(*args)
 
 
 def shift_x(by):
@@ -364,9 +390,10 @@
     theirs = move(mine, SWAP)
     win, part, fq = made
     lin, sq = linear_part(fq, part, inner, mine, theirs, other)
-    sq = sq + lax.ppermute(sq, "head", [(i, i ^ 1) for i in range(heads)])
-    across = lax.ppermute(sq, "head", [(i, heads - 1 - i) for i in range(heads)])
-    return combine(lin, win, sq, across, gain[None, :])
+    squares = [sq]
+    for by in range(1, heads):
+        squares.append(lax.ppermute(sq, "head", [(i, (i + by) % heads) for i in range(heads)]))
+    return combine(lin, win, squares, gain[None, :])
 
 
 def solution(mesh):

time: 55.6 us -> 53 us (0.953)
  the two profiles are of different devices: /device:TPU:0 before, /device:TPU:8 now
where the time goes in v6:
time: 53 us; the launch traced here: 52.7 us
  Pallas kernels  24.4 us (46%)
  starting transfers between devices  15.9 us (30%)
  waiting for transfers between devices  12.1 us (23%)
    pallas_call x4, Pallas kernels, block_part(): pl.pallas_call(lambda *refs: block_body(piece, ahead, len(made), *refs),...  14.9 us
    ppermute x9, starting transfers between devices, move(): return lax.ppermute(x, 'seq', pairs)  10.5 us
    ppermute x9, waiting for transfers between devices, move(): return lax.ppermute(x, 'seq', pairs)  8.24 us
    ppermute x3, starting transfers between devices, shards(): lax.ppermute(sq, 'head', [(i, (i + by) % heads) for i in range(heads)])  5.37 us
    ppermute x3, waiting for transfers between devices, shards(): lax.ppermute(sq, 'head', [(i, (i + by) % heads) for i in range(heads)])  3.86 us
    pallas_call x1, Pallas kernels, combine(): pl.pallas_call(combine_body, grid=(1,), in_specs=[pl.BlockSpec(x.shape, l...  3.57 us
    pallas_call x1, Pallas kernels, linear_part(): pl.pallas_call(linear_body, grid=(nb // WIDE,), in_specs=[pl.BlockSpec((W...  3.03 us
    pallas_call x1, Pallas kernels, local_states(): pl.pallas_call(functools.partial(state_body, ahead=ahead), grid=(kv,), in...  2.84 us
  transfers between devices with their start and end apart: 12, of which 8 were waited for; matrix products, arithmetic and copies ran while one was open for 0% of the time, Pallas kernels for 28%

profile of v6, /device:TPU:8, one launch (start us, length us, event | category | flops | bytes accessed | tf_op | source)
XLA Modules:
  0.0 52.7 jit_solution(15473510035387781301)
XLA Ops:
  0.0 2.8 %local_states.1 = (f32[2,8,128,128]{3,2,1,0:T(8,128)S(1)}, f32[2,128,128]{2,1,0:T(8,128)S(1)}, f32[2,256,128]{2,1,0:T(8,128)S(1)}, bf16[2,1024,512]{2,1,0:T(8,12...) custom-call(f32[1024,256]{1,0:T(8,128)} %k_ref.1, f32[1024,256]{1,0:T(8,128)} %v_ref.1, ...), custom_call_target="tpu_custom_call" | custom-call | tf_op jit(solution)/shard_map/local_states/pallas_call | solution.py:97
  2.8 0.1 collective-permute-start
  2.9 1.3 %collective-permute-done.other_ref = f32[2,128,128]{2,1,0:T(8,128)S(1)} collective-permute-done((f32[2,128,128]{2,1,0:T(8,128)S(1)}, f32[2,128,128]{2,1,0:T(8,128)S(1)}, u32[]{:S(2)}, u32[]{:S(2)}) %collective-permute-start) | collective-permute-done | bytes 131104 | tf_op jit(solution)/shard_map/ppermute | solution.py:367
  4.3 2.8 %collective-permute-start.3 = (f32[128,128]{1,0:T(8,128)S(1)}, f32[128,128]{1,0:T(8,128)S(1)}, u32[]{:S(2)}, u32[]{:S(2)}) collective-permute-start(f32[128,128]{1,0:T(8,128)S(1)} %chip_sum.1.own_ref), channel_id=1, source_target_pairs={{0,24},{4,28},{8,0},{12,4},{16,8},{20,12},{24,16},{28,20},{32,56},... | collective-permute-start | bytes 196616 | tf_op jit(solution)/shard_map/ppermute | solution.py:367
  7.1 0.8 %collective-permute-start.2 = (f32[128,128]{1,0:T(8,128)S(1)}, f32[128,128]{1,0:T(8,128)S(1)}, u32[]{:S(2)}, u32[]{:S(2)}) collective-permute-start(f32[128,128]{1,0:T(8,128)S(1)} %chip_sum.1.own_ref), channel_id=1, source_target_pairs={{0,16},{4,20},{8,24},{12,28},{16,0},{20,4},{24,8},{28,12},{32,48},... | collective-permute-start | bytes 196616 | tf_op jit(solution)/shard_map/ppermute | solution.py:367
  7.9 0.9 %collective-permute-start.1 = (f32[128,128]{1,0:T(8,128)S(1)}, f32[128,128]{1,0:T(8,128)S(1)}, u32[]{:S(2)}, u32[]{:S(2)}) collective-permute-start(f32[128,128]{1,0:T(8,128)S(1)} %chip_sum.1.own_ref), channel_id=1, source_target_pairs={{0,8},{4,12},{8,16},{12,20},{16,24},{20,28},{24,0},{28,4},{32,40},... | collective-permute-start | bytes 196616 | tf_op jit(solution)/shard_map/ppermute | solution.py:367
  8.8 3.7 %blocks_1.1 = (f32[1024,2048]{1,0:T(8,128)S(1)}, f32[1024,2048]{1,0:T(8,128)S(1)}, bf16[8,2048,256]{2,1,0:T(8,128)(2,1)S(1)}, f32[256,2048]{1,0:T(8,128)S(1)}) custom-call(f32[256,2048]{1,0:T(8,128)S(1)} %get-tuple-element.60.refs_0_, bf16[2,1024,512]{2,1,0:T(8,128)(2,1)S(1)} %get-tuple-element.61.refs_1_, ...), custom_call_target="tpu_custom_call" | custom-call | tf_op jit(solution)/shard_map/blocks_1/pallas_call | solution.py:251
  12.5 0.0 collective-permute-done.3.three_ref
  12.6 0.6 %collective-permute-done.2.two_ref = f32[128,128]{1,0:T(8,128)S(1)} collective-permute-done((f32[128,128]{1,0:T(8,128)S(1)}, f32[128,128]{1,0:T(8,128)S(1)}, u32[]{:S(2)}, u32[]{:S(2)}) %collective-permute-start.2) | collective-permute-done | bytes 65568 | tf_op jit(solution)/shard_map/ppermute | solution.py:367
  13.2 0.7 %collective-permute-done.1.one_ref = f32[128,128]{1,0:T(8,128)S(1)} collective-permute-done((f32[128,128]{1,0:T(8,128)S(1)}, f32[128,128]{1,0:T(8,128)S(1)}, u32[]{:S(2)}, u32[]{:S(2)}) %collective-permute-start.1) | collective-permute-done | bytes 65568 | tf_op jit(solution)/shard_map/ppermute | solution.py:367
  13.9 1.3 %collective-permute-start.4 = (f32[128,128]{1,0:T(8,128)S(1)}, f32[128,128]{1,0:T(8,128)S(1)}, u32[]{:S(2)}, u32[]{:S(2)}) collective-permute-start(f32[128,128]{1,0:T(8,128)S(1)} %get-tuple-element.82), channel_id=1, source_target_pairs={{0,32},{4,36},{8,40},{12,44},{16,48},{20,52},{24,56},{28,60},{1,33... | collective-permute-start | bytes 196616 | tf_op jit(solution)/shard_map/ppermute | solution.py:367
  15.2 3.8 %blocks_2.1 = (f32[1024,2048]{1,0:T(8,128)S(1)}, f32[1024,2048]{1,0:T(8,128)S(1)}, bf16[8,2048,256]{2,1,0:T(8,128)(2,1)S(1)}, f32[256,2048]{1,0:T(8,128)S(1)}) custom-call(f32[256,2048]{1,0:T(8,128)S(1)} %get-tuple-element.63.refs_0_, ...), custom_call_target="tpu_custom_call", output_to_operand_aliasing={{0}: (4, {}), {1}: (5, {}), {2}: (6, {})} | custom-call | tf_op jit(solution)/shard_map/blocks_2/pallas_call | solution.py:251
  19.0 1.1 %collective-permute-done.4 = f32[128,128]{1,0:T(8,128)S(1)} collective-permute-done((f32[128,128]{1,0:T(8,128)S(1)}, f32[128,128]{1,0:T(8,128)S(1)}, u32[]{:S(2)}, u32[]{:S(2)}) %collective-permute-start.4) | collective-permute-done | bytes 65568 | tf_op jit(solution)/shard_map/ppermute | solution.py:367
  20.1 1.8 %collective-permute-start.6 = (f32[128,128]{1,0:T(8,128)S(1)}, f32[128,128]{1,0:T(8,128)S(1)}, u32[]{:S(2)}, u32[]{:S(2)}) collective-permute-start(f32[128,128]{1,0:T(8,128)S(1)} %get-tuple-element.117), channel_id=1, source_target_pairs={{32,64},{36,68},{40,72},{44,76},{48,80},{52,84},{56,88},{60,92},{3... | collective-permute-start | bytes 196616 | tf_op jit(solution)/shard_map/ppermute | solution.py:367
  21.9 2.1 %collective-permute-start.5 = (f32[2,256,128]{2,1,0:T(8,128)S(1)}, f32[2,256,128]{2,1,0:T(8,128)S(1)}, u32[]{:S(2)}, u32[]{:S(2)}) collective-permute-start(f32[2,256,128]{2,1,0:T(8,128)S(1)} %get-tuple-element.92), channel_id=1, source_target_pairs={{0,4},{4,8},{8,12},{12,16},{16,20},{20,24},{24,28},{28,32},{32,36}... | collective-permute-start | bytes 786440 | tf_op jit(solution)/shard_map/ppermute | solution.py:367
  24.0 3.7 %blocks_3.1 = (f32[1024,2048]{1,0:T(8,128)S(1)}, f32[1024,2048]{1,0:T(8,128)S(1)}, bf16[8,2048,256]{2,1,0:T(8,128)(2,1)S(1)}, f32[256,2048]{1,0:T(8,128)S(1)}) custom-call(f32[256,2048]{1,0:T(8,128)S(1)} %get-tuple-element.78.refs_0_, ...), custom_call_target="tpu_custom_call", output_to_operand_aliasing={{0}: (4, {}), {1}: (5, {}), {2}: (6, {})} | custom-call | tf_op jit(solution)/shard_map/blocks_3/pallas_call | solution.py:251
  27.8 0.0 collective-permute-done.6
  27.8 0.7 %collective-permute-start.7 = (f32[128,128]{1,0:T(8,128)S(1)}, f32[128,128]{1,0:T(8,128)S(1)}, u32[]{:S(2)}, u32[]{:S(2)}) collective-permute-start(f32[128,128]{1,0:T(8,128)S(1)} %get-tuple-element.115), channel_id=1, source_target_pairs={{64,96},{68,100},{72,104},{76,108},{80,112},{84,116},{88,120},{92,... | collective-permute-start | bytes 196616 | tf_op jit(solution)/shard_map/ppermute | solution.py:367
  28.5 3.2 %collective-permute-done.5.refs_3_ = f32[2,256,128]{2,1,0:T(8,128)S(1)} collective-permute-done((f32[2,256,128]{2,1,0:T(8,128)S(1)}, f32[2,256,128]{2,1,0:T(8,128)S(1)}, u32[]{:S(2)}, u32[]{:S(2)}) %collective-permute-start.5) | collective-permute-done | bytes 262176 | tf_op jit(solution)/shard_map/ppermute | solution.py:367
  31.7 3.7 %blocks_0.1 = (f32[1024,2048]{1,0:T(8,128)S(1)}, f32[1024,2048]{1,0:T(8,128)S(1)}, bf16[8,2048,256]{2,1,0:T(8,128)(2,1)S(1)}) custom-call(f32[256,2048]{1,0:T(8,128)S(1)} %get-tuple-element.91.refs_0_, bf16[2,1024,512]{2,1,0:T(8,128)(2,1)S(1)} %get-tuple-element.61.refs_1_, ...), custom_call_target="tpu_custom_call", output_to_operand_aliasing={{0}: (4, {}), {1}: (5, {}), {2}: (6, {})} | custom-call | tf_op jit(solution)/shard_map/blocks_0/pallas_call | solution.py:251
  35.4 0.0 collective-permute-done.7
  35.4 0.1 collective-permute-start.8
  35.5 1.2 %collective-permute-done.8.their_ref = f32[128,128]{1,0:T(8,128)S(1)} collective-permute-done((f32[128,128]{1,0:T(8,128)S(1)}, f32[128,128]{1,0:T(8,128)S(1)}, u32[]{:S(2)}, u32[]{:S(2)}) %collective-permute-start.8) | collective-permute-done | bytes 65568 | tf_op jit(solution)/shard_map/ppermute | solution.py:367
  36.8 0.0 copy-start
  36.8 3.0 %linear.1 = (f32[1024,2048]{1,0:T(8,128)S(1)}, f32[8,1,128]{2,1,0:T(1,128)S(1)}) custom-call(bf16[8,2048,256]{2,1,0:T(8,128)(2,1)S(1)} %get-tuple-element.107.fq_ref, f32[1024,2048]{1,0:T(8,128)S(1)} %get-tuple-element.108.part_ref, f32[2,8,128,128]{3,2,1,0:T(8,128)S(1)} %get-tuple-element.109.inner_ref, f32[128,128]{1,0:T(8,128)S(1)} %add.19.mine_ref, ...), custom_call_target="tpu_custom_call" | custom-call | tf_op jit(solution)/shard_map/linear/pallas_call | solution.py:288
  39.8 4.1 %collective-permute-start.11 = (f32[8,1,128]{2,1,0:T(1,128)S(1)}, f32[8,1,128]{2,1,0:T(1,128)S(1)}, u32[]{:S(2)}, u32[]{:S(2)}) collective-permute-start(f32[8,1,128]{2,1,0:T(1,128)S(1)} %get-tuple-element.114.s0), channel_id=1, source_target_pairs={{0,3},{1,0},{2,1},{3,2},{4,7},{5,4},{6,5},{7,6},{8,11},{9,8},{10,9... | collective-permute-start | bytes 12296 | tf_op jit(solution)/shard_map/ppermute | solution.py:395
  43.9 0.0 collective-permute-start.10
  43.9 1.3 %collective-permute-start.9 = (f32[8,1,128]{2,1,0:T(1,128)S(1)}, f32[8,1,128]{2,1,0:T(1,128)S(1)}, u32[]{:S(2)}, u32[]{:S(2)}) collective-permute-start(f32[8,1,128]{2,1,0:T(1,128)S(1)} %get-tuple-element.114.s0), channel_id=1, source_target_pairs={{0,1},{1,2},{2,3},{3,0},{4,5},{5,6},{6,7},{7,4},{8,9},{9,10},{10,1... | collective-permute-start | bytes 12296 | tf_op jit(solution)/shard_map/ppermute | solution.py:395
  45.2 0.1 collective-permute-done.11.s3
  45.2 3.8 %collective-permute-done.10.s2 = f32[8,1,128]{2,1,0:T(1,128)S(1)} collective-permute-done((f32[8,1,128]{2,1,0:T(1,128)S(1)}, f32[8,1,128]{2,1,0:T(1,128)S(1)}, u32[]{:S(2)}, u32[]{:S(2)}) %collective-permute-start.10) | collective-permute-done | bytes 4128 | tf_op jit(solution)/shard_map/ppermute | solution.py:395
  49.0 0.0 collective-permute-done.9.s1
  49.0 0.0 copy-done
  49.0 3.6 %combine.1 = f32[1024,2048]{1,0:T(8,128)} custom-call(f32[1024,2048]{1,0:T(8,128)S(1)} %get-tuple-element.112.lin_ref, f32[1024,2048]{1,0:T(8,128)S(1)} %get-tuple-element.113.win_ref, f32[8,1,128]{2,1,0:T(1,128)S(1)} %get-tuple-element.114.s0, f32[8,1,128]{2,1,0:T(1,128)S(1)} %collective-permute-done.9.s1, f32[8,1,128]{2,1,0:T(1,128)S(1)} %collective-permute-done.10.s2, ...), custom_call_target="tpu_custom_call" | custom-call | tf_op jit(solution)/shard_map/combine/pallas_call | solution.py:331
  (5 shorter events, 0.1 us)
Async XLA Ops:
  2.8 1.4 %collective-permute-start = (f32[2,128,128]{2,1,0:T(8,128)S(1)}, f32[2,128,128]{2,1,0:T(8,128)S(1)}, u32[]{:S(2)}, u32[]{:S(2)}) collective-permute-start(f32[2,128,128]{2,1,0:T(8,128)S(1)} %get-tuple-element.67.own_ref), channel_id=1, source_target_pairs={{0,4},{4,0},{8,12},{12,8},{16,20},{20,16},{24,28},{28,24},{32,36},... | collective-permute-start | bytes 393224 | tf_op jit(solution)/shard_map/ppermute | solution.py:367
  4.3 8.3 %collective-permute-start.3 = (f32[128,128]{1,0:T(8,128)S(1)}, f32[128,128]{1,0:T(8,128)S(1)}, u32[]{:S(2)}, u32[]{:S(2)}) collective-permute-start(f32[128,128]{1,0:T(8,128)S(1)} %chip_sum.1.own_ref), channel_id=1, source_target_pairs={{0,24},{4,28},{8,0},{12,4},{16,8},{20,12},{24,16},{28,20},{32,56},... | collective-permute-start | bytes 196616 | tf_op jit(solution)/shard_map/ppermute | solution.py:367
  7.1 6.1 %collective-permute-start.2 = (f32[128,128]{1,0:T(8,128)S(1)}, f32[128,128]{1,0:T(8,128)S(1)}, u32[]{:S(2)}, u32[]{:S(2)}) collective-permute-start(f32[128,128]{1,0:T(8,128)S(1)} %chip_sum.1.own_ref), channel_id=1, source_target_pairs={{0,16},{4,20},{8,24},{12,28},{16,0},{20,4},{24,8},{28,12},{32,48},... | collective-permute-start | bytes 196616 | tf_op jit(solution)/shard_map/ppermute | solution.py:367
  7.9 6.0 %collective-permute-start.1 = (f32[128,128]{1,0:T(8,128)S(1)}, f32[128,128]{1,0:T(8,128)S(1)}, u32[]{:S(2)}, u32[]{:S(2)}) collective-permute-start(f32[128,128]{1,0:T(8,128)S(1)} %chip_sum.1.own_ref), channel_id=1, source_target_pairs={{0,8},{4,12},{8,16},{12,20},{16,24},{20,28},{24,0},{28,4},{32,40},... | collective-permute-start | bytes 196616 | tf_op jit(solution)/shard_map/ppermute | solution.py:367
  13.9 6.2 %collective-permute-start.4 = (f32[128,128]{1,0:T(8,128)S(1)}, f32[128,128]{1,0:T(8,128)S(1)}, u32[]{:S(2)}, u32[]{:S(2)}) collective-permute-start(f32[128,128]{1,0:T(8,128)S(1)} %get-tuple-element.82), channel_id=1, source_target_pairs={{0,32},{4,36},{8,40},{12,44},{16,48},{20,52},{24,56},{28,60},{1,33... | collective-permute-start | bytes 196616 | tf_op jit(solution)/shard_map/ppermute | solution.py:367
  20.1 7.6 %collective-permute-start.6 = (f32[128,128]{1,0:T(8,128)S(1)}, f32[128,128]{1,0:T(8,128)S(1)}, u32[]{:S(2)}, u32[]{:S(2)}) collective-permute-start(f32[128,128]{1,0:T(8,128)S(1)} %get-tuple-element.117), channel_id=1, source_target_pairs={{32,64},{36,68},{40,72},{44,76},{48,80},{52,84},{56,88},{60,92},{3... | collective-permute-start | bytes 196616 | tf_op jit(solution)/shard_map/ppermute | solution.py:367
  21.9 9.8 %collective-permute-start.5 = (f32[2,256,128]{2,1,0:T(8,128)S(1)}, f32[2,256,128]{2,1,0:T(8,128)S(1)}, u32[]{:S(2)}, u32[]{:S(2)}) collective-permute-start(f32[2,256,128]{2,1,0:T(8,128)S(1)} %get-tuple-element.92), channel_id=1, source_target_pairs={{0,4},{4,8},{8,12},{12,16},{16,20},{20,24},{24,28},{28,32},{32,36}... | collective-permute-start | bytes 786440 | tf_op jit(solution)/shard_map/ppermute | solution.py:367
  27.8 7.6 %collective-permute-start.7 = (f32[128,128]{1,0:T(8,128)S(1)}, f32[128,128]{1,0:T(8,128)S(1)}, u32[]{:S(2)}, u32[]{:S(2)}) collective-permute-start(f32[128,128]{1,0:T(8,128)S(1)} %get-tuple-element.115), channel_id=1, source_target_pairs={{64,96},{68,100},{72,104},{76,108},{80,112},{84,116},{88,120},{92,... | collective-permute-start | bytes 196616 | tf_op jit(solution)/shard_map/ppermute | solution.py:367
  35.4 1.3 %collective-permute-start.8 = (f32[128,128]{1,0:T(8,128)S(1)}, f32[128,128]{1,0:T(8,128)S(1)}, u32[]{:S(2)}, u32[]{:S(2)}) collective-permute-start(f32[128,128]{1,0:T(8,128)S(1)} %add.19.mine_ref), channel_id=1, source_target_pairs={{0,4},{4,0},{8,12},{12,8},{16,20},{20,16},{24,28},{28,24},{32,36},... | collective-permute-start | bytes 196616 | tf_op jit(solution)/shard_map/ppermute | solution.py:367
  36.8 12.3 %copy-start = (f32[2048]{0:T(1024)S(1)}, f32[2048]{0:T(1024)}, u32[]{:S(2)}) copy-start(f32[2048]{0:T(1024)} %param.7) | copy-start | bytes 24580
  39.8 5.4 %collective-permute-start.11 = (f32[8,1,128]{2,1,0:T(1,128)S(1)}, f32[8,1,128]{2,1,0:T(1,128)S(1)}, u32[]{:S(2)}, u32[]{:S(2)}) collective-permute-start(f32[8,1,128]{2,1,0:T(1,128)S(1)} %get-tuple-element.114.s0), channel_id=1, source_target_pairs={{0,3},{1,0},{2,1},{3,2},{4,7},{5,4},{6,5},{7,6},{8,11},{9,8},{10,9... | collective-permute-start | bytes 12296 | tf_op jit(solution)/shard_map/ppermute | solution.py:395
  43.9 5.1 %collective-permute-start.10 = (f32[8,1,128]{2,1,0:T(1,128)S(1)}, f32[8,1,128]{2,1,0:T(1,128)S(1)}, u32[]{:S(2)}, u32[]{:S(2)}) collective-permute-start(f32[8,1,128]{2,1,0:T(1,128)S(1)} %get-tuple-element.114.s0), channel_id=1, source_target_pairs={{0,2},{1,3},{2,0},{3,1},{4,6},{5,7},{6,4},{7,5},{8,10},{9,11},{10,... | collective-permute-start | bytes 12296 | tf_op jit(solution)/shard_map/ppermute | solution.py:395
  43.9 5.1 %collective-permute-start.9 = (f32[8,1,128]{2,1,0:T(1,128)S(1)}, f32[8,1,128]{2,1,0:T(1,128)S(1)}, u32[]{:S(2)}, u32[]{:S(2)}) collective-permute-start(f32[8,1,128]{2,1,0:T(1,128)S(1)} %get-tuple-element.114.s0), channel_id=1, source_target_pairs={{0,1},{1,2},{2,3},{3,0},{4,5},{5,6},{6,7},{7,4},{8,9},{9,10},{10,1... | collective-permute-start | bytes 12296 | tf_op jit(solution)/shard_map/ppermute | solution.py:395

commit v7 on v6

--- a/solution.py
+++ b/solution.py
@@ -7,6 +7,7 @@
 from jax.experimental import pallas as pl
 from jax.experimental.pallas import tpu as pltpu
 from jax.sharding import PartitionSpec as P
+
 
 QUERY_HEADS = 64
 KEY_VALUE_HEADS = 8
@@ -141,13 +142,12 @@
     before_ref[...] = before
 
 
-def small_call(body, outs, name, *args):
+def small_call(body, outs, *args):
     shape = jax.ShapeDtypeStruct((D, D), f32)
     return pl.pallas_call(
         body,
         out_shape=[shape] * outs,
         compiler_params=pltpu.CompilerParams(vmem_limit_bytes=2 << 20),
-        name=name,
     )(*args)
 
 
@@ -257,7 +257,6 @@
         scratch_shapes=scratch,
         input_output_aliases=aliases,
         compiler_params=params(6),
-        name=f"blocks_{piece}",
     )(*args, *made)
 
 
@@ -372,12 +371,12 @@
     order = (1, 2, 3, 0)
     inner, total, tail, kp, vp, q = local_states(queries, keys, values, order[0])
     other = move(total, SWAP)
-    (chip,) = small_call(chip_body, 1, "chip_sum", total, other)
+    (chip,) = small_call(chip_body, 1, total, other)
     along_x = [move(chip, shift_x(by)) for by in (1, 2, 3)]
     halo = move(tail, [(i, i + 1) for i in range(31)])
     *made, q = block_part(order[0], q, kp, vp, (), order[1], queries)
     *made, one, two, three = tie(*made, *along_x)
-    row, mine = small_call(row_body, 2, "row_sum", chip, one, two, three)
+    row, mine = small_call(row_body, 2, chip, one, two, three)
     for y in range(3):
         got = move(row, down_from(y))
         *made, mine = tie(*made, mine)

time: 53 us -> 53 us (level)
  no operation moved by 1% of the time
where the time goes in v7:
time: 53 us; the launch traced here: 52.7 us
  Pallas kernels  24.4 us (46%)
  starting transfers between devices  15.9 us (30%)
  waiting for transfers between devices  12.1 us (23%)
    pallas_call x4, Pallas kernels, block_part(): pl.pallas_call(lambda *refs: block_body(piece, ahead, len(made), *refs),...  14.9 us
    ppermute x9, starting transfers between devices, move(): return lax.ppermute(x, 'seq', pairs)  10.5 us
    ppermute x9, waiting for transfers between devices, move(): return lax.ppermute(x, 'seq', pairs)  8.24 us
    ppermute x3, starting transfers between devices, shards(): lax.ppermute(sq, 'head', [(i, (i + by) % heads) for i in range(heads)])  5.37 us
    ppermute x3, waiting for transfers between devices, shards(): lax.ppermute(sq, 'head', [(i, (i + by) % heads) for i in range(heads)])  3.86 us
    pallas_call x1, Pallas kernels, combine(): pl.pallas_call(combine_body, grid=(1,), in_specs=[pl.BlockSpec(x.shape, l...  3.57 us
    pallas_call x1, Pallas kernels, linear_part(): pl.pallas_call(linear_body, grid=(nb // WIDE,), in_specs=[pl.BlockSpec((W...  3.03 us
    pallas_call x1, Pallas kernels, local_states(): pl.pallas_call(functools.partial(state_body, ahead=ahead), grid=(kv,), in...  2.84 us
  transfers between devices with their start and end apart: 12, of which 8 were waited for; matrix products, arithmetic and copies ran while one was open for 0% of the time, Pallas kernels for 28%

profile of v7, /device:TPU:8, one launch (start us, length us, event | category | flops | bytes accessed | tf_op | source)
XLA Modules:
  0.0 52.7 jit_solution(15473510035387781301)
XLA Ops:
  0.0 2.8 %local_states.1 = (f32[2,8,128,128]{3,2,1,0:T(8,128)S(1)}, f32[2,128,128]{2,1,0:T(8,128)S(1)}, f32[2,256,128]{2,1,0:T(8,128)S(1)}, bf16[2,1024,512]{2,1,0:T(8,12...) custom-call(f32[1024,256]{1,0:T(8,128)} %k_ref.1, f32[1024,256]{1,0:T(8,128)} %v_ref.1, ...), custom_call_target="tpu_custom_call" | custom-call | tf_op jit(solution)/shard_map/local_states/pallas_call | solution.py:98
  2.8 0.1 collective-permute-start
  2.9 1.3 %collective-permute-done.other_ref = f32[2,128,128]{2,1,0:T(8,128)S(1)} collective-permute-done((f32[2,128,128]{2,1,0:T(8,128)S(1)}, f32[2,128,128]{2,1,0:T(8,128)S(1)}, u32[]{:S(2)}, u32[]{:S(2)}) %collective-permute-start) | collective-permute-done | bytes 131104 | tf_op jit(solution)/shard_map/ppermute | solution.py:366
  4.3 2.8 %collective-permute-start.3 = (f32[128,128]{1,0:T(8,128)S(1)}, f32[128,128]{1,0:T(8,128)S(1)}, u32[]{:S(2)}, u32[]{:S(2)}) collective-permute-start(f32[128,128]{1,0:T(8,128)S(1)} %shard_map.47.own_ref), channel_id=1, source_target_pairs={{0,24},{4,28},{8,0},{12,4},{16,8},{20,12},{24,16},{28,20},{32,56},... | collective-permute-start | bytes 196616 | tf_op jit(solution)/shard_map/ppermute | solution.py:366
  7.1 0.8 %collective-permute-start.2 = (f32[128,128]{1,0:T(8,128)S(1)}, f32[128,128]{1,0:T(8,128)S(1)}, u32[]{:S(2)}, u32[]{:S(2)}) collective-permute-start(f32[128,128]{1,0:T(8,128)S(1)} %shard_map.47.own_ref), channel_id=1, source_target_pairs={{0,16},{4,20},{8,24},{12,28},{16,0},{20,4},{24,8},{28,12},{32,48},... | collective-permute-start | bytes 196616 | tf_op jit(solution)/shard_map/ppermute | solution.py:366
  7.9 0.9 %collective-permute-start.1 = (f32[128,128]{1,0:T(8,128)S(1)}, f32[128,128]{1,0:T(8,128)S(1)}, u32[]{:S(2)}, u32[]{:S(2)}) collective-permute-start(f32[128,128]{1,0:T(8,128)S(1)} %shard_map.47.own_ref), channel_id=1, source_target_pairs={{0,8},{4,12},{8,16},{12,20},{16,24},{20,28},{24,0},{28,4},{32,40},... | collective-permute-start | bytes 196616 | tf_op jit(solution)/shard_map/ppermute | solution.py:366
  8.8 3.7 %shard_map.46 = (f32[1024,2048]{1,0:T(8,128)S(1)}, f32[1024,2048]{1,0:T(8,128)S(1)}, bf16[8,2048,256]{2,1,0:T(8,128)(2,1)S(1)}, f32[256,2048]{1,0:T(8,128)S(1)}) custom-call(f32[256,2048]{1,0:T(8,128)S(1)} %get-tuple-element.60.refs_0_, bf16[2,1024,512]{2,1,0:T(8,128)(2,1)S(1)} %get-tuple-element.61.refs_1_, ...), custom_call_target="tpu_custom_call" | custom-call | tf_op jit(solution)/shard_map/pallas_call | solution.py:251
  12.5 0.0 collective-permute-done.3.three_ref
  12.6 0.6 %collective-permute-done.2.two_ref = f32[128,128]{1,0:T(8,128)S(1)} collective-permute-done((f32[128,128]{1,0:T(8,128)S(1)}, f32[128,128]{1,0:T(8,128)S(1)}, u32[]{:S(2)}, u32[]{:S(2)}) %collective-permute-start.2) | collective-permute-done | bytes 65568 | tf_op jit(solution)/shard_map/ppermute | solution.py:366
  13.2 0.7 %collective-permute-done.1.one_ref = f32[128,128]{1,0:T(8,128)S(1)} collective-permute-done((f32[128,128]{1,0:T(8,128)S(1)}, f32[128,128]{1,0:T(8,128)S(1)}, u32[]{:S(2)}, u32[]{:S(2)}) %collective-permute-start.1) | collective-permute-done | bytes 65568 | tf_op jit(solution)/shard_map/ppermute | solution.py:366
  13.9 1.3 %collective-permute-start.4 = (f32[128,128]{1,0:T(8,128)S(1)}, f32[128,128]{1,0:T(8,128)S(1)}, u32[]{:S(2)}, u32[]{:S(2)}) collective-permute-start(f32[128,128]{1,0:T(8,128)S(1)} %get-tuple-element.82), channel_id=1, source_target_pairs={{0,32},{4,36},{8,40},{12,44},{16,48},{20,52},{24,56},{28,60},{1,33... | collective-permute-start | bytes 196616 | tf_op jit(solution)/shard_map/ppermute | solution.py:366
  15.2 3.8 %shard_map.49 = (f32[1024,2048]{1,0:T(8,128)S(1)}, f32[1024,2048]{1,0:T(8,128)S(1)}, bf16[8,2048,256]{2,1,0:T(8,128)(2,1)S(1)}, f32[256,2048]{1,0:T(8,128)S(1)}) custom-call(f32[256,2048]{1,0:T(8,128)S(1)} %get-tuple-element.63.refs_0_, ...), custom_call_target="tpu_custom_call", output_to_operand_aliasing={{0}: (4, {}), {1}: (5, {}), {2}: (6, {})} | custom-call | tf_op jit(solution)/shard_map/pallas_call | solution.py:251
  19.0 1.1 %collective-permute-done.4 = f32[128,128]{1,0:T(8,128)S(1)} collective-permute-done((f32[128,128]{1,0:T(8,128)S(1)}, f32[128,128]{1,0:T(8,128)S(1)}, u32[]{:S(2)}, u32[]{:S(2)}) %collective-permute-start.4) | collective-permute-done | bytes 65568 | tf_op jit(solution)/shard_map/ppermute | solution.py:366
  20.1 1.8 %collective-permute-start.6 = (f32[128,128]{1,0:T(8,128)S(1)}, f32[128,128]{1,0:T(8,128)S(1)}, u32[]{:S(2)}, u32[]{:S(2)}) collective-permute-start(f32[128,128]{1,0:T(8,128)S(1)} %get-tuple-element.117), channel_id=1, source_target_pairs={{32,64},{36,68},{40,72},{44,76},{48,80},{52,84},{56,88},{60,92},{3... | collective-permute-start | bytes 196616 | tf_op jit(solution)/shard_map/ppermute | solution.py:366
  21.9 2.1 %collective-permute-start.5 = (f32[2,256,128]{2,1,0:T(8,128)S(1)}, f32[2,256,128]{2,1,0:T(8,128)S(1)}, u32[]{:S(2)}, u32[]{:S(2)}) collective-permute-start(f32[2,256,128]{2,1,0:T(8,128)S(1)} %get-tuple-element.92), channel_id=1, source_target_pairs={{0,4},{4,8},{8,12},{12,16},{16,20},{20,24},{24,28},{28,32},{32,36}... | collective-permute-start | bytes 786440 | tf_op jit(solution)/shard_map/ppermute | solution.py:366
  24.0 3.7 %shard_map.50 = (f32[1024,2048]{1,0:T(8,128)S(1)}, f32[1024,2048]{1,0:T(8,128)S(1)}, bf16[8,2048,256]{2,1,0:T(8,128)(2,1)S(1)}, f32[256,2048]{1,0:T(8,128)S(1)}) custom-call(f32[256,2048]{1,0:T(8,128)S(1)} %get-tuple-element.78.refs_0_, ...), custom_call_target="tpu_custom_call", output_to_operand_aliasing={{0}: (4, {}), {1}: (5, {}), {2}: (6, {})} | custom-call | tf_op jit(solution)/shard_map/pallas_call | solution.py:251
  27.8 0.0 collective-permute-done.6
  27.8 0.7 %collective-permute-start.7 = (f32[128,128]{1,0:T(8,128)S(1)}, f32[128,128]{1,0:T(8,128)S(1)}, u32[]{:S(2)}, u32[]{:S(2)}) collective-permute-start(f32[128,128]{1,0:T(8,128)S(1)} %get-tuple-element.115), channel_id=1, source_target_pairs={{64,96},{68,100},{72,104},{76,108},{80,112},{84,116},{88,120},{92,... | collective-permute-start | bytes 196616 | tf_op jit(solution)/shard_map/ppermute | solution.py:366
  28.5 3.2 %collective-permute-done.5.refs_3_ = f32[2,256,128]{2,1,0:T(8,128)S(1)} collective-permute-done((f32[2,256,128]{2,1,0:T(8,128)S(1)}, f32[2,256,128]{2,1,0:T(8,128)S(1)}, u32[]{:S(2)}, u32[]{:S(2)}) %collective-permute-start.5) | collective-permute-done | bytes 262176 | tf_op jit(solution)/shard_map/ppermute | solution.py:366
  31.7 3.7 %shard_map.51 = (f32[1024,2048]{1,0:T(8,128)S(1)}, f32[1024,2048]{1,0:T(8,128)S(1)}, bf16[8,2048,256]{2,1,0:T(8,128)(2,1)S(1)}) custom-call(f32[256,2048]{1,0:T(8,128)S(1)} %get-tuple-element.91.refs_0_, bf16[2,1024,512]{2,1,0:T(8,128)(2,1)S(1)} %get-tuple-element.61.refs_1_, ...), custom_call_target="tpu_custom_call", output_to_operand_aliasing={{0}: (4, {}), {1}: (5, {}), {2}: (6, {})} | custom-call | tf_op jit(solution)/shard_map/pallas_call | solution.py:251
  35.4 0.0 collective-permute-done.7
  35.4 0.1 collective-permute-start.8
  35.5 1.2 %collective-permute-done.8.their_ref = f32[128,128]{1,0:T(8,128)S(1)} collective-permute-done((f32[128,128]{1,0:T(8,128)S(1)}, f32[128,128]{1,0:T(8,128)S(1)}, u32[]{:S(2)}, u32[]{:S(2)}) %collective-permute-start.8) | collective-permute-done | bytes 65568 | tf_op jit(solution)/shard_map/ppermute | solution.py:366
  36.8 0.0 copy-start
  36.8 3.0 %linear.1 = (f32[1024,2048]{1,0:T(8,128)S(1)}, f32[8,1,128]{2,1,0:T(1,128)S(1)}) custom-call(bf16[8,2048,256]{2,1,0:T(8,128)(2,1)S(1)} %get-tuple-element.107.fq_ref, f32[1024,2048]{1,0:T(8,128)S(1)} %get-tuple-element.108.part_ref, f32[2,8,128,128]{3,2,1,0:T(8,128)S(1)} %get-tuple-element.109.inner_ref, f32[128,128]{1,0:T(8,128)S(1)} %add.19.mine_ref, ...), custom_call_target="tpu_custom_call" | custom-call | tf_op jit(solution)/shard_map/linear/pallas_call | solution.py:287
  39.8 4.1 %collective-permute-start.11 = (f32[8,1,128]{2,1,0:T(1,128)S(1)}, f32[8,1,128]{2,1,0:T(1,128)S(1)}, u32[]{:S(2)}, u32[]{:S(2)}) collective-permute-start(f32[8,1,128]{2,1,0:T(1,128)S(1)} %get-tuple-element.114.s0), channel_id=1, source_target_pairs={{0,3},{1,0},{2,1},{3,2},{4,7},{5,4},{6,5},{7,6},{8,11},{9,8},{10,9... | collective-permute-start | bytes 12296 | tf_op jit(solution)/shard_map/ppermute | solution.py:394
  43.9 0.0 collective-permute-start.10
  43.9 1.3 %collective-permute-start.9 = (f32[8,1,128]{2,1,0:T(1,128)S(1)}, f32[8,1,128]{2,1,0:T(1,128)S(1)}, u32[]{:S(2)}, u32[]{:S(2)}) collective-permute-start(f32[8,1,128]{2,1,0:T(1,128)S(1)} %get-tuple-element.114.s0), channel_id=1, source_target_pairs={{0,1},{1,2},{2,3},{3,0},{4,5},{5,6},{6,7},{7,4},{8,9},{9,10},{10,1... | collective-permute-start | bytes 12296 | tf_op jit(solution)/shard_map/ppermute | solution.py:394
  45.2 0.1 collective-permute-done.11.s3
  45.2 3.8 %collective-permute-done.10.s2 = f32[8,1,128]{2,1,0:T(1,128)S(1)} collective-permute-done((f32[8,1,128]{2,1,0:T(1,128)S(1)}, f32[8,1,128]{2,1,0:T(1,128)S(1)}, u32[]{:S(2)}, u32[]{:S(2)}) %collective-permute-start.10) | collective-permute-done | bytes 4128 | tf_op jit(solution)/shard_map/ppermute | solution.py:394
  49.0 0.0 collective-permute-done.9.s1
  49.0 0.0 copy-done
  49.0 3.6 %combine.1 = f32[1024,2048]{1,0:T(8,128)} custom-call(f32[1024,2048]{1,0:T(8,128)S(1)} %get-tuple-element.112.lin_ref, f32[1024,2048]{1,0:T(8,128)S(1)} %get-tuple-element.113.win_ref, f32[8,1,128]{2,1,0:T(1,128)S(1)} %get-tuple-element.114.s0, f32[8,1,128]{2,1,0:T(1,128)S(1)} %collective-permute-done.9.s1, f32[8,1,128]{2,1,0:T(1,128)S(1)} %collective-permute-done.10.s2, ...), custom_call_target="tpu_custom_call" | custom-call | tf_op jit(solution)/shard_map/combine/pallas_call | solution.py:330
  (5 shorter events, 0.1 us)
Async XLA Ops:
  2.8 1.4 %collective-permute-start = (f32[2,128,128]{2,1,0:T(8,128)S(1)}, f32[2,128,128]{2,1,0:T(8,128)S(1)}, u32[]{:S(2)}, u32[]{:S(2)}) collective-permute-start(f32[2,128,128]{2,1,0:T(8,128)S(1)} %get-tuple-element.67.own_ref), channel_id=1, source_target_pairs={{0,4},{4,0},{8,12},{12,8},{16,20},{20,16},{24,28},{28,24},{32,36},... | collective-permute-start | bytes 393224 | tf_op jit(solution)/shard_map/ppermute | solution.py:366
  4.3 8.3 %collective-permute-start.3 = (f32[128,128]{1,0:T(8,128)S(1)}, f32[128,128]{1,0:T(8,128)S(1)}, u32[]{:S(2)}, u32[]{:S(2)}) collective-permute-start(f32[128,128]{1,0:T(8,128)S(1)} %shard_map.47.own_ref), channel_id=1, source_target_pairs={{0,24},{4,28},{8,0},{12,4},{16,8},{20,12},{24,16},{28,20},{32,56},... | collective-permute-start | bytes 196616 | tf_op jit(solution)/shard_map/ppermute | solution.py:366
  7.1 6.1 %collective-permute-start.2 = (f32[128,128]{1,0:T(8,128)S(1)}, f32[128,128]{1,0:T(8,128)S(1)}, u32[]{:S(2)}, u32[]{:S(2)}) collective-permute-start(f32[128,128]{1,0:T(8,128)S(1)} %shard_map.47.own_ref), channel_id=1, source_target_pairs={{0,16},{4,20},{8,24},{12,28},{16,0},{20,4},{24,8},{28,12},{32,48},... | collective-permute-start | bytes 196616 | tf_op jit(solution)/shard_map/ppermute | solution.py:366
  7.9 6.0 %collective-permute-start.1 = (f32[128,128]{1,0:T(8,128)S(1)}, f32[128,128]{1,0:T(8,128)S(1)}, u32[]{:S(2)}, u32[]{:S(2)}) collective-permute-start(f32[128,128]{1,0:T(8,128)S(1)} %shard_map.47.own_ref), channel_id=1, source_target_pairs={{0,8},{4,12},{8,16},{12,20},{16,24},{20,28},{24,0},{28,4},{32,40},... | collective-permute-start | bytes 196616 | tf_op jit(solution)/shard_map/ppermute | solution.py:366
  13.9 6.2 %collective-permute-start.4 = (f32[128,128]{1,0:T(8,128)S(1)}, f32[128,128]{1,0:T(8,128)S(1)}, u32[]{:S(2)}, u32[]{:S(2)}) collective-permute-start(f32[128,128]{1,0:T(8,128)S(1)} %get-tuple-element.82), channel_id=1, source_target_pairs={{0,32},{4,36},{8,40},{12,44},{16,48},{20,52},{24,56},{28,60},{1,33... | collective-permute-start | bytes 196616 | tf_op jit(solution)/shard_map/ppermute | solution.py:366
  20.1 7.6 %collective-permute-start.6 = (f32[128,128]{1,0:T(8,128)S(1)}, f32[128,128]{1,0:T(8,128)S(1)}, u32[]{:S(2)}, u32[]{:S(2)}) collective-permute-start(f32[128,128]{1,0:T(8,128)S(1)} %get-tuple-element.117), channel_id=1, source_target_pairs={{32,64},{36,68},{40,72},{44,76},{48,80},{52,84},{56,88},{60,92},{3... | collective-permute-start | bytes 196616 | tf_op jit(solution)/shard_map/ppermute | solution.py:366
  21.9 9.8 %collective-permute-start.5 = (f32[2,256,128]{2,1,0:T(8,128)S(1)}, f32[2,256,128]{2,1,0:T(8,128)S(1)}, u32[]{:S(2)}, u32[]{:S(2)}) collective-permute-start(f32[2,256,128]{2,1,0:T(8,128)S(1)} %get-tuple-element.92), channel_id=1, source_target_pairs={{0,4},{4,8},{8,12},{12,16},{16,20},{20,24},{24,28},{28,32},{32,36}... | collective-permute-start | bytes 786440 | tf_op jit(solution)/shard_map/ppermute | solution.py:366
  27.8 7.6 %collective-permute-start.7 = (f32[128,128]{1,0:T(8,128)S(1)}, f32[128,128]{1,0:T(8,128)S(1)}, u32[]{:S(2)}, u32[]{:S(2)}) collective-permute-start(f32[128,128]{1,0:T(8,128)S(1)} %get-tuple-element.115), channel_id=1, source_target_pairs={{64,96},{68,100},{72,104},{76,108},{80,112},{84,116},{88,120},{92,... | collective-permute-start | bytes 196616 | tf_op jit(solution)/shard_map/ppermute | solution.py:366
  35.4 1.3 %collective-permute-start.8 = (f32[128,128]{1,0:T(8,128)S(1)}, f32[128,128]{1,0:T(8,128)S(1)}, u32[]{:S(2)}, u32[]{:S(2)}) collective-permute-start(f32[128,128]{1,0:T(8,128)S(1)} %add.19.mine_ref), channel_id=1, source_target_pairs={{0,4},{4,0},{8,12},{12,8},{16,20},{20,16},{24,28},{28,24},{32,36},... | collective-permute-start | bytes 196616 | tf_op jit(solution)/shard_map/ppermute | solution.py:366
  36.8 12.3 %copy-start = (f32[2048]{0:T(1024)S(1)}, f32[2048]{0:T(1024)}, u32[]{:S(2)}) copy-start(f32[2048]{0:T(1024)} %param.7) | copy-start | bytes 24580
  39.8 5.4 %collective-permute-start.11 = (f32[8,1,128]{2,1,0:T(1,128)S(1)}, f32[8,1,128]{2,1,0:T(1,128)S(1)}, u32[]{:S(2)}, u32[]{:S(2)}) collective-permute-start(f32[8,1,128]{2,1,0:T(1,128)S(1)} %get-tuple-element.114.s0), channel_id=1, source_target_pairs={{0,3},{1,0},{2,1},{3,2},{4,7},{5,4},{6,5},{7,6},{8,11},{9,8},{10,9... | collective-permute-start | bytes 12296 | tf_op jit(solution)/shard_map/ppermute | solution.py:394
  43.9 5.1 %collective-permute-start.10 = (f32[8,1,128]{2,1,0:T(1,128)S(1)}, f32[8,1,128]{2,1,0:T(1,128)S(1)}, u32[]{:S(2)}, u32[]{:S(2)}) collective-permute-start(f32[8,1,128]{2,1,0:T(1,128)S(1)} %get-tuple-element.114.s0), channel_id=1, source_target_pairs={{0,2},{1,3},{2,0},{3,1},{4,6},{5,7},{6,4},{7,5},{8,10},{9,11},{10,... | collective-permute-start | bytes 12296 | tf_op jit(solution)/shard_map/ppermute | solution.py:394
  43.9 5.1 %collective-permute-start.9 = (f32[8,1,128]{2,1,0:T(1,128)S(1)}, f32[8,1,128]{2,1,0:T(1,128)S(1)}, u32[]{:S(2)}, u32[]{:S(2)}) collective-permute-start(f32[8,1,128]{2,1,0:T(1,128)S(1)} %get-tuple-element.114.s0), channel_id=1, source_target_pairs={{0,1},{1,2},{2,3},{3,0},{4,5},{5,6},{6,7},{7,4},{8,9},{9,10},{10,1... | collective-permute-start | bytes 12296 | tf_op jit(solution)/shard_map/ppermute | solution.py:394

commit v8 on v7

--- a/solution.py
+++ b/solution.py
@@ -151,13 +151,17 @@
     )(*args)
 
 
-def block_body(piece, ahead, carried, *refs):
+def block_body(piece, ahead, carried, inner, window, *refs):
     q_ref, kp_ref, vp_ref, *refs = refs
-    if piece == 0:
+    if piece == 0 and window:
         halo_ref, *refs = refs
     if ahead is not None:
         q_hbm, *refs = refs
-    win_ref, lin_ref, fq_ref, *refs = refs[carried:]
+    refs = refs[carried:]
+    if window:
+        win_ref, *refs = refs
+    if inner:
+        lin_ref, fq_ref, *refs = refs
     kv = kp_ref.shape[0]
     if ahead is not None:
         next_ref, sems = refs
@@ -175,55 +179,67 @@
     col = lax.broadcasted_iota(jnp.int32, (BLOCK, BLOCK), 1)
     own = rows(*[row >= col] * G)
     zero = jnp.zeros((BLOCK * G, BLOCK), bf)
+
+    def in_block(j, g, q, heads, tokens, here):
+        fh, fl = kp_ref[g, here, 2 * D : 3 * D], kp_ref[g, here, 3 * D :]
+        v_own = vp_ref[g, here, :]
+        f2 = lanes(*split(jnp.tanh(q)))
+        fq_ref[j, g * G * BLOCK : (g + 1) * G * BLOCK, :] = f2
+        ff = rows(lanes(fh, fh), lanes(fl, fl))
+        a = jnp.where(own, halves(dot(f2, ff, NT)), 0.0)
+        lin = halves(dot(lanes(*split(a)), rows(v_own, v_own)))
+        for i, at in enumerate(heads):
+            lin_ref[tokens, at] = lin[i * BLOCK : (i + 1) * BLOCK]
+
+    def in_window(block, g, q, heads, tokens, here, there):
+        kh, kl = kp_ref[g, here, :D], kp_ref[g, here, D : 2 * D]
+        if block:
+            ph, pl_ = kp_ref[g, there, :D], kp_ref[g, there, D : 2 * D]
+            v_prior = vp_ref[g, there, :]
+        else:
+            ph, pl_ = split(halo_ref[g, :BLOCK] * SCORE_SCALE)
+            v_prior = lanes(*split(halo_ref[g, BLOCK:]))
+        kk = rows(lanes(kh, kh, kl, kl), lanes(ph, ph, pl_, pl_))
+        v_both = rows(vp_ref[g, here, :], v_prior)
+        qh, ql = split(q)
+        s = dot(lanes(qh, ql, qh, ql), kk, NT)
+        before = s[:, BLOCK:]
+        if block == 0:
+            before = jnp.where(lax.axis_index("seq") > 0, before, -1e30)
+        t = jnp.where(own, s[:, :BLOCK], before)
+        p = jnp.exp2(t - jnp.max(t, axis=1, keepdims=True))
+        total = jnp.sum(p, axis=1, keepdims=True)
+        wh, wl = split(p)
+        p4 = lanes(
+            jnp.where(own, wh, zero),
+            jnp.where(own, zero, wh),
+            jnp.where(own, wl, zero),
+            jnp.where(own, zero, wl),
+        )
+        win = halves(dot(p4, rows(v_both, v_both))) * (1.0 / total)
+        for i, at in enumerate(heads):
+            win_ref[tokens, at] = win[i * BLOCK : (i + 1) * BLOCK]
+
     for j in range(STEP):
         block = piece * STEP + j
         tokens = slice(j * BLOCK, (j + 1) * BLOCK)
         here = slice(block * BLOCK, (block + 1) * BLOCK)
         there = slice((block - 1) * BLOCK, block * BLOCK)
         for g in range(kv):
-            kh, kl = kp_ref[g, here, :D], kp_ref[g, here, D : 2 * D]
-            fh, fl = kp_ref[g, here, 2 * D : 3 * D], kp_ref[g, here, 3 * D :]
-            v_own = vp_ref[g, here, :]
-            if block:
-                ph, pl_ = kp_ref[g, there, :D], kp_ref[g, there, D : 2 * D]
-                v_prior = vp_ref[g, there, :]
-            else:
-                ph, pl_ = split(halo_ref[g, :BLOCK] * SCORE_SCALE)
-                v_prior = lanes(*split(halo_ref[g, BLOCK:]))
-            kk = rows(lanes(kh, kh, kl, kl), lanes(ph, ph, pl_, pl_))
-            ff = rows(lanes(fh, fh), lanes(fl, fl))
-            v_both = rows(v_own, v_prior)
             heads = [slice(i * D, (i + 1) * D) for i in range(g * G, (g + 1) * G)]
             q = rows(*[q_ref[tokens, at] for at in heads])
-            qh, ql = split(q)
-            s = dot(lanes(qh, ql, qh, ql), kk, NT)
-            f2 = lanes(*split(jnp.tanh(q)))
-            fq_ref[j, g * G * BLOCK : (g + 1) * G * BLOCK, :] = f2
-            a = jnp.where(own, halves(dot(f2, ff, NT)), 0.0)
-            lin = halves(dot(lanes(*split(a)), rows(v_own, v_own)))
-            before = s[:, BLOCK:]
-            if block == 0:
-                before = jnp.where(lax.axis_index("seq") > 0, before, -1e30)
-            t = jnp.where(own, s[:, :BLOCK], before)
-            p = jnp.exp2(t - jnp.max(t, axis=1, keepdims=True))
-            total = jnp.sum(p, axis=1, keepdims=True)
-            wh, wl = split(p)
-            p4 = lanes(
-                jnp.where(own, wh, zero),
-                jnp.where(own, zero, wh),
-                jnp.where(own, wl, zero),
-                jnp.where(own, zero, wl),
-            )
-            win = halves(dot(p4, rows(v_both, v_both))) * (1.0 / total)
-            for i, at in enumerate(heads):
-                win_ref[tokens, at] = win[i * BLOCK : (i + 1) * BLOCK]
-                lin_ref[tokens, at] = lin[i * BLOCK : (i + 1) * BLOCK]
+            if inner:
+                in_block(j, g, q, heads, tokens, here)
+            if window:
+                in_window(block, g, q, heads, tokens, here, there)
     if ahead is not None:
         for j in range(STEP):
             fetch(j).wait()
 
 
-def block_part(piece, q, kp, vp, made, ahead=None, queries=None, halo=None):
+def block_part(
+    piece, q, kp, vp, made, ahead=None, queries=None, halo=None, inner=True, window=True
+):
     kv, count, _ = kp.shape
     nb = count // BLOCK
     width = q.shape[1]
@@ -237,26 +253,27 @@
         specs.append(pl.BlockSpec(memory_space=pl.ANY))
     aliases = {len(args) + i: i for i in range(len(made))}
     big = pl.BlockSpec((STEP * BLOCK, width), lambda _: (piece, 0))
-    out_specs = [big, big, pl.BlockSpec((STEP, kv * G * BLOCK, 2 * D), lambda _: (piece, 0, 0))]
-    out_shape = [
-        pltpu.VMEM((count, width), f32),
-        pltpu.VMEM((count, width), f32),
-        pltpu.VMEM((nb, kv * G * BLOCK, 2 * D), bf),
-    ]
-    scratch = []
+    out_specs, out_shape, scratch = [], [], []
+    if window:
+        out_specs.append(big)
+        out_shape.append(pltpu.VMEM((count, width), f32))
+    if inner:
+        features = (kv * G * BLOCK, 2 * D)
+        out_specs += [big, pl.BlockSpec((STEP, *features), lambda _: (piece, 0, 0))]
+        out_shape += [pltpu.VMEM((count, width), f32), pltpu.VMEM((nb, *features), bf)]
     if ahead is not None:
         out_specs.append(pl.BlockSpec(memory_space=pl.ANY))
         out_shape.append(pltpu.VMEM(q.shape, f32))
         scratch.append(pltpu.SemaphoreType.DMA((STEP,)))
     return pl.pallas_call(
-        lambda *refs: block_body(piece, ahead, len(made), *refs),
+        lambda *refs: block_body(piece, ahead, len(made), inner, window, *refs),
         grid=(1,),
         in_specs=specs + [pl.BlockSpec(memory_space=pl.ANY)] * len(made),
         out_specs=out_specs,
         out_shape=out_shape,
         scratch_shapes=scratch,
         input_output_aliases=aliases,
-        compiler_params=params(6),
+        compiler_params=params(10),
     )(*args, *made)
 
 
@@ -300,7 +317,7 @@
             pltpu.VMEM((count, width), f32),
             pltpu.VMEM((nb, 1, BLOCK), f32),
         ],
-        compiler_params=params(6),
+        compiler_params=params(10),
         name="linear",
     )(fq, part, inner, mine, theirs, other)
 
@@ -383,15 +400,19 @@
         if y < 2:
             *made, q = block_part(order[y + 1], q, kp, vp, made, order[y + 2], queries)
         else:
-            made = block_part(0, q, kp, vp, made, halo=halo)
+            win, *made = made
+            part, fq = block_part(0, q, kp, vp, made, window=False)
+            made = [win, part, fq]
         *made, got = tie(*made, got)
         row, mine = row + got, mine + got
     theirs = move(mine, SWAP)
     win, part, fq = made
     lin, sq = linear_part(fq, part, inner, mine, theirs, other)
+    q, sq = tie(q, sq)
     squares = [sq]
     for by in range(1, heads):
         squares.append(lax.ppermute(sq, "head", [(i, (i + by) % heads) for i in range(heads)]))
+    (win,) = block_part(0, q, kp, vp, (win,), halo=halo, inner=False)
     return combine(lin, win, squares, gain[None, :])
 
 

time: 53 us -> 50 us (0.943)
  the two profiles are of different devices: /device:TPU:8 before, /device:TPU:24 now
where the time goes in v8:
time: 50 us; the launch traced here: 49.8 us
  Pallas kernels  26.6 us (53%)
  starting transfers between devices  14.9 us (30%)
  waiting for transfers between devices  8.04 us (16%)
    pallas_call x5, Pallas kernels, block_part(): pl.pallas_call(lambda *refs: block_body(piece, ahead, len(made), inner, w...  17.1 us
    ppermute x9, starting transfers between devices, move(): return lax.ppermute(x, 'seq', pairs)  9.48 us
    ppermute x9, waiting for transfers between devices, move(): return lax.ppermute(x, 'seq', pairs)  7.51 us
    ppermute x3, starting transfers between devices, shards(): lax.ppermute(sq, 'head', [(i, (i + by) % heads) for i in range(heads)])  5.37 us
    pallas_call x1, Pallas kernels, combine(): pl.pallas_call(combine_body, grid=(1,), in_specs=[pl.BlockSpec(x.shape, l...  3.57 us
    pallas_call x1, Pallas kernels, linear_part(): pl.pallas_call(linear_body, grid=(nb // WIDE,), in_specs=[pl.BlockSpec((W...  3.03 us
    pallas_call x1, Pallas kernels, local_states(): pl.pallas_call(functools.partial(state_body, ahead=ahead), grid=(kv,), in...  2.84 us
  transfers between devices with their start and end apart: 12, of which 6 were waited for; matrix products, arithmetic and copies ran while one was open for 0% of the time, Pallas kernels for 40%

profile of v8, /device:TPU:24, one launch (start us, length us, event | category | flops | bytes accessed | tf_op | source)
XLA Modules:
  0.0 49.8 jit_solution(13650773422791226329)
XLA Ops:
  0.0 2.8 %local_states.1 = (f32[2,8,128,128]{3,2,1,0:T(8,128)S(1)}, f32[2,128,128]{2,1,0:T(8,128)S(1)}, f32[2,256,128]{2,1,0:T(8,128)S(1)}, bf16[2,1024,512]{2,1,0:T(8,12...) custom-call(f32[1024,256]{1,0:T(8,128)} %k_ref.1, f32[1024,256]{1,0:T(8,128)} %v_ref.1, ...), custom_call_target="tpu_custom_call" | custom-call | tf_op jit(solution)/shard_map/local_states/pallas_call | solution.py:98
  2.8 0.1 collective-permute-start
  2.9 1.3 %collective-permute-done.other_ref = f32[2,128,128]{2,1,0:T(8,128)S(1)} collective-permute-done((f32[2,128,128]{2,1,0:T(8,128)S(1)}, f32[2,128,128]{2,1,0:T(8,128)S(1)}, u32[]{:S(2)}, u32[]{:S(2)}) %collective-permute-start) | collective-permute-done | bytes 131104 | tf_op jit(solution)/shard_map/ppermute | solution.py:383
  4.3 2.8 %collective-permute-start.3 = (f32[128,128]{1,0:T(8,128)S(1)}, f32[128,128]{1,0:T(8,128)S(1)}, u32[]{:S(2)}, u32[]{:S(2)}) collective-permute-start(f32[128,128]{1,0:T(8,128)S(1)} %shard_map.47.own_ref), channel_id=1, source_target_pairs={{0,24},{4,28},{8,0},{12,4},{16,8},{20,12},{24,16},{28,20},{32,56},... | collective-permute-start | bytes 196616 | tf_op jit(solution)/shard_map/ppermute | solution.py:383
  7.1 0.8 %collective-permute-start.2 = (f32[128,128]{1,0:T(8,128)S(1)}, f32[128,128]{1,0:T(8,128)S(1)}, u32[]{:S(2)}, u32[]{:S(2)}) collective-permute-start(f32[128,128]{1,0:T(8,128)S(1)} %shard_map.47.own_ref), channel_id=1, source_target_pairs={{0,16},{4,20},{8,24},{12,28},{16,0},{20,4},{24,8},{28,12},{32,48},... | collective-permute-start | bytes 196616 | tf_op jit(solution)/shard_map/ppermute | solution.py:383
  7.9 0.9 %collective-permute-start.1 = (f32[128,128]{1,0:T(8,128)S(1)}, f32[128,128]{1,0:T(8,128)S(1)}, u32[]{:S(2)}, u32[]{:S(2)}) collective-permute-start(f32[128,128]{1,0:T(8,128)S(1)} %shard_map.47.own_ref), channel_id=1, source_target_pairs={{0,8},{4,12},{8,16},{12,20},{16,24},{20,28},{24,0},{28,4},{32,40},... | collective-permute-start | bytes 196616 | tf_op jit(solution)/shard_map/ppermute | solution.py:383
  8.8 4.1 %shard_map.46 = (f32[1024,2048]{1,0:T(8,128)S(1)}, f32[1024,2048]{1,0:T(8,128)S(1)}, bf16[8,2048,256]{2,1,0:T(8,128)(2,1)S(1)}, f32[256,2048]{1,0:T(8,128)S(1)}) custom-call(f32[256,2048]{1,0:T(8,128)S(1)} %get-tuple-element.61.refs_0_, bf16[2,1024,512]{2,1,0:T(8,128)(2,1)S(1)} %get-tuple-element.62.refs_1_, ...), custom_call_target="tpu_custom_call" | custom-call | tf_op jit(solution)/shard_map/pallas_call | solution.py:268
  12.9 0.0 collective-permute-done.3.three_ref
  12.9 0.3 collective-permute-done.2.two_ref
  13.2 0.7 %collective-permute-done.1.one_ref = f32[128,128]{1,0:T(8,128)S(1)} collective-permute-done((f32[128,128]{1,0:T(8,128)S(1)}, f32[128,128]{1,0:T(8,128)S(1)}, u32[]{:S(2)}, u32[]{:S(2)}) %collective-permute-start.1) | collective-permute-done | bytes 65568 | tf_op jit(solution)/shard_map/ppermute | solution.py:383
  13.9 0.7 %collective-permute-start.4 = (f32[128,128]{1,0:T(8,128)S(1)}, f32[128,128]{1,0:T(8,128)S(1)}, u32[]{:S(2)}, u32[]{:S(2)}) collective-permute-start(f32[128,128]{1,0:T(8,128)S(1)} %get-tuple-element.83), channel_id=1, source_target_pairs={{0,32},{4,36},{8,40},{12,44},{16,48},{20,52},{24,56},{28,60},{1,33... | collective-permute-start | bytes 196616 | tf_op jit(solution)/shard_map/ppermute | solution.py:383
  14.6 4.1 %shard_map.49 = (f32[1024,2048]{1,0:T(8,128)S(1)}, f32[1024,2048]{1,0:T(8,128)S(1)}, bf16[8,2048,256]{2,1,0:T(8,128)(2,1)S(1)}, f32[256,2048]{1,0:T(8,128)S(1)}) custom-call(f32[256,2048]{1,0:T(8,128)S(1)} %get-tuple-element.64.refs_0_, ...), custom_call_target="tpu_custom_call", output_to_operand_aliasing={{0}: (4, {}), {1}: (5, {}), {2}: (6, {})} | custom-call | tf_op jit(solution)/shard_map/pallas_call | solution.py:268
  18.7 0.0 collective-permute-done.4
  18.7 0.7 %collective-permute-start.5 = (f32[128,128]{1,0:T(8,128)S(1)}, f32[128,128]{1,0:T(8,128)S(1)}, u32[]{:S(2)}, u32[]{:S(2)}) collective-permute-start(f32[128,128]{1,0:T(8,128)S(1)} %get-tuple-element.119), channel_id=1, source_target_pairs={{32,64},{36,68},{40,72},{44,76},{48,80},{52,84},{56,88},{60,92},{3... | collective-permute-start | bytes 196616 | tf_op jit(solution)/shard_map/ppermute | solution.py:383
  19.4 2.1 %collective-permute-start.8 = (f32[2,256,128]{2,1,0:T(8,128)S(1)}, f32[2,256,128]{2,1,0:T(8,128)S(1)}, u32[]{:S(2)}, u32[]{:S(2)}) collective-permute-start(f32[2,256,128]{2,1,0:T(8,128)S(1)} %get-tuple-element.114), channel_id=1, source_target_pairs={{0,4},{4,8},{8,12},{12,16},{16,20},{20,24},{24,28},{28,32},{32,36}... | collective-permute-start | bytes 786440 | tf_op jit(solution)/shard_map/ppermute | solution.py:383
  21.5 4.1 %shard_map.50 = (f32[1024,2048]{1,0:T(8,128)S(1)}, f32[1024,2048]{1,0:T(8,128)S(1)}, bf16[8,2048,256]{2,1,0:T(8,128)(2,1)S(1)}, f32[256,2048]{1,0:T(8,128)S(1)}) custom-call(f32[256,2048]{1,0:T(8,128)S(1)} %get-tuple-element.79.refs_0_, ...), custom_call_target="tpu_custom_call", output_to_operand_aliasing={{0}: (4, {}), {1}: (5, {}), {2}: (6, {})} | custom-call | tf_op jit(solution)/shard_map/pallas_call | solution.py:268
  25.6 0.0 collective-permute-done.5
  25.7 1.3 %collective-permute-start.6 = (f32[128,128]{1,0:T(8,128)S(1)}, f32[128,128]{1,0:T(8,128)S(1)}, u32[]{:S(2)}, u32[]{:S(2)}) collective-permute-start(f32[128,128]{1,0:T(8,128)S(1)} %get-tuple-element.117), channel_id=1, source_target_pairs={{64,96},{68,100},{72,104},{76,108},{80,112},{84,116},{88,120},{92,... | collective-permute-start | bytes 196616 | tf_op jit(solution)/shard_map/ppermute | solution.py:383
  27.0 1.5 %shard_map.51 = (f32[1024,2048]{1,0:T(8,128)S(1)}, bf16[8,2048,256]{2,1,0:T(8,128)(2,1)S(1)}) custom-call(f32[256,2048]{1,0:T(8,128)S(1)} %get-tuple-element.113.refs_0_, bf16[2,1024,512]{2,1,0:T(8,128)(2,1)S(1)} %get-tuple-element.62.refs_1_, bf16[2,1024,256]{2,1,0:T(8,128)(2,1)S(1)} %get-tuple-element.63.refs_2_, ...), custom_call_target="tpu_custom_call", output_to_operand_aliasing={{0}: (3, {}), {1}: (4, {})} | custom-call | tf_op jit(solution)/shard_map/pallas_call | solution.py:268
  28.5 4.0 %collective-permute-done.6 = f32[128,128]{1,0:T(8,128)S(1)} collective-permute-done((f32[128,128]{1,0:T(8,128)S(1)}, f32[128,128]{1,0:T(8,128)S(1)}, u32[]{:S(2)}, u32[]{:S(2)}) %collective-permute-start.6) | collective-permute-done | bytes 65568 | tf_op jit(solution)/shard_map/ppermute | solution.py:383
  32.5 0.2 collective-permute-start.7
  32.7 1.2 %collective-permute-done.7.their_ref = f32[128,128]{1,0:T(8,128)S(1)} collective-permute-done((f32[128,128]{1,0:T(8,128)S(1)}, f32[128,128]{1,0:T(8,128)S(1)}, u32[]{:S(2)}, u32[]{:S(2)}) %collective-permute-start.7) | collective-permute-done | bytes 65568 | tf_op jit(solution)/shard_map/ppermute | solution.py:383
  33.8 3.0 %linear.1 = (f32[1024,2048]{1,0:T(8,128)S(1)}, f32[8,1,128]{2,1,0:T(1,128)S(1)}) custom-call(bf16[8,2048,256]{2,1,0:T(8,128)(2,1)S(1)} %get-tuple-element.106.fq_ref, f32[1024,2048]{1,0:T(8,128)S(1)} %get-tuple-element.107.part_ref, f32[2,8,128,128]{3,2,1,0:T(8,128)S(1)} %get-tuple-element.108.inner_ref, f32[128,128]{1,0:T(8,128)S(1)} %add.19.mine_ref, ...), custom_call_target="tpu_custom_call" | custom-call | tf_op jit(solution)/shard_map/linear/pallas_call | solution.py:304
  36.9 0.0 copy-start
  36.9 4.1 %collective-permute-start.11 = (f32[8,1,128]{2,1,0:T(1,128)S(1)}, f32[8,1,128]{2,1,0:T(1,128)S(1)}, u32[]{:S(2)}, u32[]{:S(2)}) collective-permute-start(f32[8,1,128]{2,1,0:T(1,128)S(1)} %get-tuple-element.116.s0), channel_id=1, source_target_pairs={{0,3},{1,0},{2,1},{3,2},{4,7},{5,4},{6,5},{7,6},{8,11},{9,8},{10,9... | collective-permute-start | bytes 12296 | tf_op jit(solution)/shard_map/ppermute | solution.py:414
  41.0 0.0 collective-permute-start.10
  41.0 1.3 %collective-permute-start.9 = (f32[8,1,128]{2,1,0:T(1,128)S(1)}, f32[8,1,128]{2,1,0:T(1,128)S(1)}, u32[]{:S(2)}, u32[]{:S(2)}) collective-permute-start(f32[8,1,128]{2,1,0:T(1,128)S(1)} %get-tuple-element.116.s0), channel_id=1, source_target_pairs={{0,1},{1,2},{2,3},{3,0},{4,5},{5,6},{6,7},{7,4},{8,9},{9,10},{10,1... | collective-permute-start | bytes 12296 | tf_op jit(solution)/shard_map/ppermute | solution.py:414
  42.3 0.0 collective-permute-done.8.refs_3_
  42.3 3.3 %shard_map.52.win_ref = f32[1024,2048]{1,0:T(8,128)S(1)} custom-call(f32[256,2048]{1,0:T(8,128)S(1)} %get-tuple-element.113.refs_0_, bf16[2,1024,512]{2,1,0:T(8,128)(2,1)S(1)} %get-tuple-element.62.refs_1_, bf16[2,1024,256]{2,1,0:T(8,128)(2,1)S(1)} %get-tuple-element.63.refs_2_, ...), custom_call_target="tpu_custom_call", output_to_operand_aliasing={{}: (4, {})} | custom-call | tf_op jit(solution)/shard_map/pallas_call | solution.py:268
  45.6 0.0 collective-permute-done.11.s3
  45.6 0.5 %collective-permute-done.10.s2 = f32[8,1,128]{2,1,0:T(1,128)S(1)} collective-permute-done((f32[8,1,128]{2,1,0:T(1,128)S(1)}, f32[8,1,128]{2,1,0:T(1,128)S(1)}, u32[]{:S(2)}, u32[]{:S(2)}) %collective-permute-start.10) | collective-permute-done | bytes 4128 | tf_op jit(solution)/shard_map/ppermute | solution.py:414
  46.1 0.0 collective-permute-done.9.s1
  46.1 0.0 copy-done
  46.1 3.6 %combine.1 = f32[1024,2048]{1,0:T(8,128)} custom-call(f32[1024,2048]{1,0:T(8,128)S(1)} %get-tuple-element.111.lin_ref, f32[1024,2048]{1,0:T(8,128)S(1)} %shard_map.52.win_ref, f32[8,1,128]{2,1,0:T(1,128)S(1)} %get-tuple-element.116.s0, f32[8,1,128]{2,1,0:T(1,128)S(1)} %collective-permute-done.9.s1, f32[8,1,128]{2,1,0:T(1,128)S(1)} %collective-permute-done.10.s2, ...), custom_call_target="tpu_custom_call" | custom-call | tf_op jit(solution)/shard_map/combine/pallas_call | solution.py:347
  (5 shorter events, 0.1 us)
Async XLA Ops:
  2.8 1.4 %collective-permute-start = (f32[2,128,128]{2,1,0:T(8,128)S(1)}, f32[2,128,128]{2,1,0:T(8,128)S(1)}, u32[]{:S(2)}, u32[]{:S(2)}) collective-permute-start(f32[2,128,128]{2,1,0:T(8,128)S(1)} %get-tuple-element.68.own_ref), channel_id=1, source_target_pairs={{0,4},{4,0},{8,12},{12,8},{16,20},{20,16},{24,28},{28,24},{32,36},... | collective-permute-start | bytes 393224 | tf_op jit(solution)/shard_map/ppermute | solution.py:383
  4.3 8.6 %collective-permute-start.3 = (f32[128,128]{1,0:T(8,128)S(1)}, f32[128,128]{1,0:T(8,128)S(1)}, u32[]{:S(2)}, u32[]{:S(2)}) collective-permute-start(f32[128,128]{1,0:T(8,128)S(1)} %shard_map.47.own_ref), channel_id=1, source_target_pairs={{0,24},{4,28},{8,0},{12,4},{16,8},{20,12},{24,16},{28,20},{32,56},... | collective-permute-start | bytes 196616 | tf_op jit(solution)/shard_map/ppermute | solution.py:383
  7.1 6.1 %collective-permute-start.2 = (f32[128,128]{1,0:T(8,128)S(1)}, f32[128,128]{1,0:T(8,128)S(1)}, u32[]{:S(2)}, u32[]{:S(2)}) collective-permute-start(f32[128,128]{1,0:T(8,128)S(1)} %shard_map.47.own_ref), channel_id=1, source_target_pairs={{0,16},{4,20},{8,24},{12,28},{16,0},{20,4},{24,8},{28,12},{32,48},... | collective-permute-start | bytes 196616 | tf_op jit(solution)/shard_map/ppermute | solution.py:383
  7.9 6.0 %collective-permute-start.1 = (f32[128,128]{1,0:T(8,128)S(1)}, f32[128,128]{1,0:T(8,128)S(1)}, u32[]{:S(2)}, u32[]{:S(2)}) collective-permute-start(f32[128,128]{1,0:T(8,128)S(1)} %shard_map.47.own_ref), channel_id=1, source_target_pairs={{0,8},{4,12},{8,16},{12,20},{16,24},{20,28},{24,0},{28,4},{32,40},... | collective-permute-start | bytes 196616 | tf_op jit(solution)/shard_map/ppermute | solution.py:383
  13.9 4.8 %collective-permute-start.4 = (f32[128,128]{1,0:T(8,128)S(1)}, f32[128,128]{1,0:T(8,128)S(1)}, u32[]{:S(2)}, u32[]{:S(2)}) collective-permute-start(f32[128,128]{1,0:T(8,128)S(1)} %get-tuple-element.83), channel_id=1, source_target_pairs={{0,32},{4,36},{8,40},{12,44},{16,48},{20,52},{24,56},{28,60},{1,33... | collective-permute-start | bytes 196616 | tf_op jit(solution)/shard_map/ppermute | solution.py:383
  18.7 6.9 %collective-permute-start.5 = (f32[128,128]{1,0:T(8,128)S(1)}, f32[128,128]{1,0:T(8,128)S(1)}, u32[]{:S(2)}, u32[]{:S(2)}) collective-permute-start(f32[128,128]{1,0:T(8,128)S(1)} %get-tuple-element.119), channel_id=1, source_target_pairs={{32,64},{36,68},{40,72},{44,76},{48,80},{52,84},{56,88},{60,92},{3... | collective-permute-start | bytes 196616 | tf_op jit(solution)/shard_map/ppermute | solution.py:383
  19.4 22.8 %collective-permute-start.8 = (f32[2,256,128]{2,1,0:T(8,128)S(1)}, f32[2,256,128]{2,1,0:T(8,128)S(1)}, u32[]{:S(2)}, u32[]{:S(2)}) collective-permute-start(f32[2,256,128]{2,1,0:T(8,128)S(1)} %get-tuple-element.114), channel_id=1, source_target_pairs={{0,4},{4,8},{8,12},{12,16},{16,20},{20,24},{24,28},{28,32},{32,36}... | collective-permute-start | bytes 786440 | tf_op jit(solution)/shard_map/ppermute | solution.py:383
  25.7 6.8 %collective-permute-start.6 = (f32[128,128]{1,0:T(8,128)S(1)}, f32[128,128]{1,0:T(8,128)S(1)}, u32[]{:S(2)}, u32[]{:S(2)}) collective-permute-start(f32[128,128]{1,0:T(8,128)S(1)} %get-tuple-element.117), channel_id=1, source_target_pairs={{64,96},{68,100},{72,104},{76,108},{80,112},{84,116},{88,120},{92,... | collective-permute-start | bytes 196616 | tf_op jit(solution)/shard_map/ppermute | solution.py:383
  32.5 1.3 %collective-permute-start.7 = (f32[128,128]{1,0:T(8,128)S(1)}, f32[128,128]{1,0:T(8,128)S(1)}, u32[]{:S(2)}, u32[]{:S(2)}) collective-permute-start(f32[128,128]{1,0:T(8,128)S(1)} %add.19.mine_ref), channel_id=1, source_target_pairs={{0,4},{4,0},{8,12},{12,8},{16,20},{20,16},{24,28},{28,24},{32,36},... | collective-permute-start | bytes 196616 | tf_op jit(solution)/shard_map/ppermute | solution.py:383
  36.9 9.2 %copy-start = (f32[2048]{0:T(1024)S(1)}, f32[2048]{0:T(1024)}, u32[]{:S(2)}) copy-start(f32[2048]{0:T(1024)} %param.7) | copy-start | bytes 24580
  36.9 8.7 %collective-permute-start.11 = (f32[8,1,128]{2,1,0:T(1,128)S(1)}, f32[8,1,128]{2,1,0:T(1,128)S(1)}, u32[]{:S(2)}, u32[]{:S(2)}) collective-permute-start(f32[8,1,128]{2,1,0:T(1,128)S(1)} %get-tuple-element.116.s0), channel_id=1, source_target_pairs={{0,3},{1,0},{2,1},{3,2},{4,7},{5,4},{6,5},{7,6},{8,11},{9,8},{10,9... | collective-permute-start | bytes 12296 | tf_op jit(solution)/shard_map/ppermute | solution.py:414
  41.0 5.1 %collective-permute-start.10 = (f32[8,1,128]{2,1,0:T(1,128)S(1)}, f32[8,1,128]{2,1,0:T(1,128)S(1)}, u32[]{:S(2)}, u32[]{:S(2)}) collective-permute-start(f32[8,1,128]{2,1,0:T(1,128)S(1)} %get-tuple-element.116.s0), channel_id=1, source_target_pairs={{0,2},{1,3},{2,0},{3,1},{4,6},{5,7},{6,4},{7,5},{8,10},{9,11},{10,... | collective-permute-start | bytes 12296 | tf_op jit(solution)/shard_map/ppermute | solution.py:414
  41.0 5.1 %collective-permute-start.9 = (f32[8,1,128]{2,1,0:T(1,128)S(1)}, f32[8,1,128]{2,1,0:T(1,128)S(1)}, u32[]{:S(2)}, u32[]{:S(2)}) collective-permute-start(f32[8,1,128]{2,1,0:T(1,128)S(1)} %get-tuple-element.116.s0), channel_id=1, source_target_pairs={{0,1},{1,2},{2,3},{3,0},{4,5},{5,6},{6,7},{7,4},{8,9},{9,10},{10,1... | collective-permute-start | bytes 12296 | tf_op jit(solution)/shard_map/ppermute | solution.py:414
